TPU v7x, 256 devices: a whole 4x4x8 slice. The times are simulated.
256 devices in a mesh: seq: 64 (over y, z, core), tp: 4 (over x).
Axes of the slice: x: 4, y: 4, z: 8, core: 2. Of those that a mesh axis runs over, the one named last changes fastest.
Arguments:
- queries_short: bfloat16 [128, 4, 2304], P('seq', None, 'tp'), may hold values from -4 to 4
- cache_short: bfloat16 [2, 128, 1024, 2304], P(None, 'seq', None, 'tp'), may hold values from -260 to 260
- fresh_short: bfloat16 [2, 128, 4, 2304], P(None, 'seq', None, 'tp'), may hold values from -260 to 260
- short_len: int32 [128], P('seq'), may hold values from 1 to 1024, as said below
- queries_long: bfloat16 [4, 4, 2304], P(None, None, 'tp'), may hold values from -4 to 4
- cache_long: bfloat16 [2, 4, 16384, 2304], P(None, None, 'seq', 'tp'), may hold values from -260 to 260
- fresh_long: bfloat16 [2, 4, 4, 2304], P(None, None, None, 'tp'), may hold values from -260 to 260
- long_len: int32 [4], replicated, may hold values from 8192 to 16384, as said below
- block_live: int32 [4, 128], P(None, 'seq'), may hold values 0 or 1
- out_weight: bfloat16 [2304, 2304], P('tp'), may hold values from -0.125 to 0.125
Outputs:
- short_out: bfloat16 [128, 4, 2304], P('seq', None, 'tp')
- long_out: bfloat16 [4, 4, 2304], P(None, None, 'tp')
Inputs may be any that keep to these rules, and one draw needn't show every extreme that they name: `short_len`: some short request fills all 1024 slots. `long_len`: some long request fills all 16384 slots.
All inputs are finite; a program needn't handle non-finite values. No bound on the sum of `block_live` on one device may be relied on, other than what follows from the above.
Results may differ from a plain program's by a relative error of at most 0.011.
Values sent between devices are 32-bit elements; how exact they have to be, the bound alone decides.
A program may use at most 64 MiB of HBM per device.

v0:
```python
import math

import jax
import jax.numpy as jnp
from jax import lax
from jax.sharding import PartitionSpec as P

HEAD_DIM = 64


NEGATIVE = -1e30


def split_heads(tensor):
    return tensor.reshape(tensor.shape[0], tensor.shape[1], tensor.shape[2] // HEAD_DIM, HEAD_DIM)


def partial_softmax(query_heads, key_heads, value_heads, usable):
    scores = jnp.einsum(
        "rjhd,rphd->rhjp", query_heads, key_heads, preferred_element_type=jnp.float32
    ) * (1.0 / math.sqrt(HEAD_DIM))
    scores = jnp.where(usable, scores, NEGATIVE)
    highest = jnp.max(scores, axis=-1)
    expo = jnp.where(usable, jnp.exp(scores - highest[..., None]), 0.0)
    totals = jnp.sum(expo, axis=-1)
    summed = jnp.einsum(
        "rhjp,rphd->rhjd",
        expo.astype(jnp.bfloat16),
        value_heads,
        preferred_element_type=jnp.float32,
    )
    return (highest, totals, summed)


def combine_parts(first, second):
    highest = jnp.maximum(first[0], second[0])
    scale_first = jnp.exp(first[0] - highest)
    scale_second = jnp.exp(second[0] - highest)
    totals = first[1] * scale_first + second[1] * scale_second
    summed = first[2] * scale_first[..., None] + second[2] * scale_second[..., None]
    return (highest, totals, summed)


def finish(parts):
    normed = (parts[2] / parts[1][..., None]).astype(jnp.bfloat16)
    normed = jnp.transpose(normed, (0, 2, 1, 3))
    return normed.reshape(normed.shape[0], normed.shape[1], normed.shape[2] * normed.shape[3])


def fresh_part(queries, fresh):
    count = queries.shape[1]
    causal = (jnp.arange(count)[:, None] >= jnp.arange(count)[None, :])[None, None]
    return partial_softmax(
        split_heads(queries), split_heads(fresh[0]), split_heads(fresh[1]), causal
    )


def per_device(
    queries_short,
    cache_short,
    fresh_short,
    short_len,
    queries_long,
    cache_long,
    fresh_long,
    long_len,
    block_live,
    out_weight,
):
    short_query = split_heads(queries_short)
    request_count = queries_short.shape[0]
    token_count = queries_short.shape[1]
    positions = cache_short.shape[2]
    usable = (jnp.arange(positions, dtype=jnp.int32)[None, :] < short_len[:, None])[
        :, None, None, :
    ]
    short_parts = partial_softmax(
        short_query, split_heads(cache_short[0]), split_heads(cache_short[1]), usable
    )
    short_att = finish(combine_parts(short_parts, fresh_part(queries_short, fresh_short)))
    local_len = cache_long.shape[2]
    spots = lax.axis_index("seq") * local_len + jnp.arange(local_len, dtype=jnp.int32)
    live = jnp.repeat(block_live, local_len // block_live.shape[1], axis=1) == 1
    long_usable = ((spots[None, :] < long_len[:, None]) & live)[:, None, None, :]
    long_parts = partial_softmax(
        split_heads(queries_long),
        split_heads(cache_long[0]),
        split_heads(cache_long[1]),
        long_usable,
    )
    every_high, every_total, every_sum = (
        lax.all_gather(long_parts[0][None], "seq", axis=0, tiled=True),
        lax.all_gather(long_parts[1][None], "seq", axis=0, tiled=True),
        lax.all_gather(long_parts[2][None], "seq", axis=0, tiled=True),
    )
    highest = jnp.max(every_high, axis=0)
    scales = jnp.exp(every_high - highest[None])
    merged = (
        highest,
        jnp.sum(every_total * scales, axis=0),
        jnp.sum(every_sum * scales[..., None], axis=0),
    )
    long_att = finish(combine_parts(merged, fresh_part(queries_long, fresh_long)))
    short_term = jnp.dot(
        short_att.reshape(-1, short_att.shape[2]), out_weight, preferred_element_type=jnp.float32
    )
    long_term = jnp.dot(
        long_att.reshape(-1, long_att.shape[2]), out_weight, preferred_element_type=jnp.float32
    )
    short_cols = lax.psum_scatter(short_term, "tp", scatter_dimension=1, tiled=True)
    long_cols = lax.psum_scatter(long_term, "tp", scatter_dimension=1, tiled=True)
    short_out = short_cols.astype(jnp.bfloat16).reshape(
        request_count, token_count, short_cols.shape[1]
    )
    long_out = long_cols.astype(jnp.bfloat16).reshape(
        long_att.shape[0], long_att.shape[1], long_cols.shape[1]
    )
    return (short_out, long_out)


def solution(mesh):
    in_specs = (
        P("seq", None, "tp"),
        P(None, "seq", None, "tp"),
        P(None, "seq", None, "tp"),
        P("seq"),
        P(None, None, "tp"),
        P(None, None, "seq", "tp"),
        P(None, None, None, "tp"),
        P(),
        P(None, "seq"),
        P("tp", None),
    )
    out_specs = (P("seq", None, "tp"), P(None, None, "tp"))
    return jax.shard_map(
        per_device, mesh=mesh, in_specs=in_specs, out_specs=out_specs, check_vma=False
    )
```

profile of v0, /device:TPU:4, one launch (start us, length us, event | category | flops | bytes accessed | tf_op | source)
XLA Modules:
  0.0 180.6 jit_solution(8602789161538166098)
XLA Ops:
  8.1 0.8 broadcast_compare_fusion
  8.9 3.2 %fusion.53 = (bf16[1,4,256,576]{2,3,1,0:T(8,128)(2,1)}, bf16[1,4,256,576]{2,3,1,0:T(8,128)(2,1)}) fusion(bf16[2,4,256,576]{2,3,1,0:T(8,128)(2,1)} %param.15), kind=kLoop, calls=%fused_computation.77 | loop fusion | bytes 4718592 | tf_op jit(solution)/shard_map/slice | solution.py:87
  12.2 0.1 reshape.139
  12.3 1.6 fusion.57
  14.0 2.4 %fusion.19 = f32[4,9,4,64]{3,2,1,0:T(4,128)} fusion(bf16[4,256,9,64]{1,3,2,0:T(8,128)(2,1)} %bitcast.96, f32[4,9,4,256]{3,2,1,0:T(4,128)S(1)} %get-tuple-element.23, f32[4,9,4]{2,1,0:T(8,128)S(1)} %get-tuple-element.22, pred[4,256]{1,0:T(4,128)(4,1)S(1)} %bitcast_and_fusion), kind=kOutput, calls=%fused_computation.30 | convolution fusion | flops 4829184 | bytes 1365568 | tf_op jit(solution)/shard_map/rhjp,rphd->rhjd/dot_general | solution.py:26
  16.6 0.1 fusion.29
  16.8 0.1 copy.143
  16.9 0.1 fusion.36
  17.0 0.1 copy.144
  17.1 0.1 fusion.45
  17.2 0.1 copy.147
  17.3 0.1 copy.145
  17.6 2.9 %fusion.52 = (bf16[1,2,1024,576]{2,3,1,0:T(8,128)(2,1)S(1)}, bf16[1,2,1024,576]{2,3,1,0:T(8,128)(2,1)S(1)}) fusion(bf16[2,2,1024,576]{2,3,1,0:T(8,128)(2,1)} %param.11), kind=kLoop, calls=%fused_computation.76 | loop fusion | bytes 9437184 | tf_op jit(solution)/shard_map/slice | solution.py:78
  20.5 0.5 fusion.56
  21.0 0.3 fusion.11
  21.3 0.7 fusion.9
  22.1 0.2 fusion.10
  22.3 0.1 reshape_reshape.6
  22.4 2.2 %convolution_bitcast_fusion.1 = f32[2304,8]{1,0:T(8,128)} fusion(bf16[8,576]{1,0:T(8,128)(2,1)S(1)} %reshape_reshape.6, bf16[576,2304]{1,0:T(8,128)(2,1)S(1)} %copy-done), kind=kOutput, calls=%fused_computation.2 | convolution fusion | flops 21233664 | bytes 2737152
  24.7 0.1 copy.150
  24.8 0.2 fusion.17
  25.0 53.6 %all-gather.1 = f32[256,9,4]{1,2,0:T(4,128)S(1)} all-gather(f32[4,9,4]{1,2,0:T(4,128)S(1)} %copy.150), channel_id=3, replica_groups=mesh['seq'=64,'tp'=4] {'seq'}, dimensions={0}, use_global_device_ids=true | all-gather | bytes 37440 | tf_op jit(solution)/shard_map/all_gather | solution.py:92
  78.6 0.8 copy-done.1
  79.4 0.1 reduce_max.58
  79.5 1.2 subtract_exponential_fusion
  80.7 0.1 copy.162
  80.9 54.0 %all-gather.2 = f32[256,9,4]{1,2,0:T(4,128)} all-gather(f32[4,9,4]{1,2,0:T(4,128)S(1)} %copy.162), channel_id=4, replica_groups=mesh['seq'=64,'tp'=4] {'seq'}, dimensions={0}, use_global_device_ids=true | all-gather | bytes 37440 | tf_op jit(solution)/shard_map/all_gather | solution.py:93
  134.8 3.0 %copy.151 = f32[64,4,9,4]{3,2,1,0:T(8,128)} copy(f32[64,4,9,4]{2,3,1,0:T(4,128)S(1)} %subtract_exponential_fusion) | data formatting | bytes 73728 | tf_op jit(solution)/shard_map/exp | solution.py:97
  137.8 1.2 multiply_reduce_fusion.1
  139.1 0.1 reshape_squeeze.30
  139.2 0.2 fusion.25
  139.3 0.2 copy.154
  139.6 0.1 fusion.27
  139.7 0.1 fusion.37
  139.8 0.1 copy.157
  139.9 0.1 copy.161
  140.0 0.1 copy.165
  140.2 0.2 copy.159
  140.4 0.1 reshape_squeeze.31
  140.5 6.3 %multiply_reduce_fusion = f32[4,9,4,64]{3,2,1,0:T(4,128)S(1)} fusion(f32[64,4,9,4,64]{4,3,2,1,0:T(4,128)} %bitcast.91, f32[64,4,9,4]{3,2,1,0:T(8,128)} %copy.151), kind=kLoop, calls=%fused_computation | loop fusion | flops 1170432 | bytes 2433024 | tf_op jit(solution)/shard_map/reduce_sum | solution.py:101
  146.8 0.2 fusion.5
  147.0 0.1 reshape_reshape.7
  147.1 2.2 %convolution_bitcast_fusion = f32[2304,16]{1,0:T(8,128)} fusion(bf16[16,576]{1,0:T(8,128)(2,1)S(1)} %reshape_reshape.7, bf16[576,2304]{1,0:T(8,128)(2,1)S(1)} %copy-done), kind=kOutput, calls=%fused_computation.1 | convolution fusion | flops 42467328 | bytes 2820096
  149.4 1.0 copy.168
  150.4 0.6 reshape.138
  151.0 20.4 %reduce-scatter.9.cloned.1.call-done = f32[576,16]{1,0:T(8,128)} async-done(((f32[2304,16]{1,0:T(8,128)}), f32[576,16]{1,0:T(8,128)}) %reduce-scatter.9.cloned.1.call-update) | async-done | bytes 36880
  171.5 1.1 copy.170
  172.5 0.6 reshape.140
  (36 shorter events, 0.8 us)
Async XLA Ops:
  8.0 14.4 %copy-start = (bf16[576,2304]{1,0:T(8,128)(2,1)S(1)}, bf16[576,2304]{1,0:T(8,128)(2,1)}, u32[]{:S(2)}) copy-start(bf16[576,2304]{1,0:T(8,128)(2,1)} %param.19) | copy-start | bytes 7962628
  8.0 132.5 %all-gather.5.cloned.1.call-start = ((), (), s32[]{:S(2)}) async-start(), calls=%async_computation.2 | async-start | bytes 4792320 | tf_op jit(solution)/shard_map/all_gather | solution.py:94
  8.9 3.2 %copy-start.4 = (bf16[4,4,576]{2,1,0:T(4,128)(2,1)S(1)}, bf16[4,4,576]{2,1,0:T(4,128)(2,1)}, u32[]{:S(2)}) copy-start(bf16[4,4,576]{2,1,0:T(4,128)(2,1)} %param.14) | copy-start | bytes 55300
  8.9 3.4 %copy-start.7 = (s32[4]{0:T(128)S(1)}, s32[4]{0:T(128)}, u32[]{:S(2)}) copy-start(s32[4]{0:T(128)} %param.17) | copy-start | bytes 52
  12.1 4.3 %copy-start.5 = (bf16[2,4,576]{2,1,0:T(4,128)(2,1)S(1)}, bf16[2,4,576]{2,1,0:T(4,128)(2,1)}, u32[]{:S(2)}) copy-start(bf16[2,4,576]{2,1,0:T(4,128)(2,1)} %param.10) | copy-start | bytes 27652
  12.1 4.4 %copy-start.3 = (bf16[2,2,4,576]{3,2,1,0:T(4,128)(2,1)S(1)}, bf16[2,2,4,576]{3,2,1,0:T(4,128)(2,1)}, u32[]{:S(2)}) copy-start(bf16[2,2,4,576]{3,2,1,0:T(4,128)(2,1)} %param.12) | copy-start | bytes 55300
  12.1 5.4 %copy-start.6 = (s32[2]{0:T(128)S(1)}, s32[2]{0:T(128)}, u32[]{:S(2)}) copy-start(s32[2]{0:T(128)} %param.13) | copy-start | bytes 28
  16.4 133.0 %reduce-scatter.7.cloned.1.call-start = ((), (), s32[]{:S(2)}) async-start(), calls=%async_computation.3 | async-start | bytes 1474560
  24.6 146.9 %reduce-scatter.9.cloned.1.call-start = ((), (), s32[]{:S(2)}) async-start(), calls=%async_computation.4 | async-start | bytes 1474560
  78.6 0.8 copy-start.1
  80.7 58.3 %copy-start.2 = (bf16[2,4,4,576]{3,2,1,0:T(4,128)(2,1)S(1)}, bf16[2,4,4,576]{3,2,1,0:T(4,128)(2,1)}, u32[]{:S(2)}) copy-start(bf16[2,4,4,576]{3,2,1,0:T(4,128)(2,1)} %param.16) | copy-start | bytes 110596
Sparse Core Ops, SparseCore 0:
  16.5 82.3 all-gather.4
Sparse Core Ops, SparseCore 1:
  24.7 27.9 reduce-scatter.6
  149.4 22.0 reduce-scatter.8
where the time goes:
time: 183 us; the launch traced here: 181 us
  blocking collectives  108 us (59%)
  waiting for transfers between devices  20.5 us (11%)
  local copies, waits for them, and re-layouts  15.7 us (9%)
  between operations  15.7 us (9%)
  other arithmetic  10.8 us (6%)
  matrix products  10.3 us (6%)
    all_gather x1, blocking collectives, per_device(): lax.all_gather(long_parts[1][None], 'seq', axis=0, tiled=True)  54 us
    all_gather x1, blocking collectives, per_device(): lax.all_gather(long_parts[0][None], 'seq', axis=0, tiled=True)  53.6 us
    unnamed x5, waiting for transfers between devices  20.5 us
    reduce_sum x1, other arithmetic, per_device(): jnp.sum(every_sum * scales[..., None], axis=0)  6.27 us
    unnamed x2, matrix products  4.36 us
  transfers between devices with their start and end apart: 3, of which 1 were waited for; matrix products, arithmetic and copies ran while one was open for 14% of the time, Pallas kernels for 0%

commit v1 on v0

--- a/solution.py
+++ b/solution.py
@@ -1,11 +1,16 @@
+import functools
 import math
 
 import jax
 import jax.numpy as jnp
 from jax import lax
+from jax.experimental import pallas as pl
+from jax.experimental.pallas import tpu as pltpu
 from jax.sharding import PartitionSpec as P
 
 HEAD_DIM = 64
+MESH = pl.DeviceIdType.MESH
+LANES = 128
 
 
 NEGATIVE = -1e30
@@ -53,6 +58,77 @@
     return partial_softmax(
         split_heads(queries), split_heads(fresh[0]), split_heads(fresh[1]), causal
     )
+
+
+def merge_states(low, high):
+    lane = lax.broadcasted_iota(jnp.int32, low.shape, 1)
+    top_low = low[:, HEAD_DIM : HEAD_DIM + 1]
+    top_high = high[:, HEAD_DIM : HEAD_DIM + 1]
+    top = jnp.maximum(top_low, top_high)
+    mixed = low * jnp.exp(top_low - top) + high * jnp.exp(top_high - top)
+    return jnp.where(lane == HEAD_DIM, top, mixed)
+
+
+def butterfly_kernel(rounds, x_ref, o_ref, state, recv, send_sem, recv_sem):
+    me = lax.axis_index("seq")
+    column = lax.axis_index("tp")
+    partners = []
+    for k in range(rounds):
+        step = 1 << k
+        bit = (me // step) % 2
+        partners.append((me + step - 2 * step * bit, bit))
+    barrier = pltpu.get_barrier_semaphore()
+    for partner, _ in partners:
+        pl.semaphore_signal(
+            barrier, inc=1, device_id=(partner, column), device_id_type=MESH
+        )
+    pl.semaphore_wait(barrier, rounds)
+    for k in range(rounds):
+        partner, bit = partners[k]
+        source = x_ref if k == 0 else state.at[k - 1]
+        copy = pltpu.make_async_remote_copy(
+            src_ref=source,
+            dst_ref=recv.at[k],
+            send_sem=send_sem.at[k],
+            recv_sem=recv_sem.at[k],
+            device_id=(partner, column),
+            device_id_type=MESH,
+        )
+        copy.start()
+        copy.wait()
+        mine = source[...]
+        theirs = recv[k]
+        first = bit == 0
+        merged = merge_states(
+            jnp.where(first, mine, theirs), jnp.where(first, theirs, mine)
+        )
+        if k == rounds - 1:
+            o_ref[...] = merged
+        else:
+            state[k] = merged
+
+
+def seq_allreduce(packed, devices):
+    rounds = devices.bit_length() - 1
+    rows = packed.shape[0]
+    return pl.pallas_call(
+        functools.partial(butterfly_kernel, rounds),
+        out_shape=jax.ShapeDtypeStruct(packed.shape, jnp.float32),
+        in_specs=[pl.BlockSpec(memory_space=pltpu.VMEM)],
+        out_specs=pl.BlockSpec(memory_space=pltpu.VMEM),
+        scratch_shapes=[
+            pltpu.VMEM((max(rounds - 1, 1), rows, LANES), jnp.float32),
+            pltpu.VMEM((rounds, rows, LANES), jnp.float32),
+            pltpu.SemaphoreType.DMA((rounds,)),
+            pltpu.SemaphoreType.DMA((rounds,)),
+        ],
+        compiler_params=pltpu.CompilerParams(collective_id=0, has_side_effects=True),
+        cost_estimate=pl.CostEstimate(
+            flops=8 * rows * LANES * rounds,
+            transcendentals=2 * rows * rounds,
+            bytes_accessed=2 * rows * LANES * 4 * rounds,
+        ),
+    )(packed)
 
 
 def per_device(
@@ -88,17 +164,23 @@
         split_heads(cache_long[1]),
         long_usable,
     )
-    every_high, every_total, every_sum = (
-        lax.all_gather(long_parts[0][None], "seq", axis=0, tiled=True),
-        lax.all_gather(long_parts[1][None], "seq", axis=0, tiled=True),
-        lax.all_gather(long_parts[2][None], "seq", axis=0, tiled=True),
-    )
-    highest = jnp.max(every_high, axis=0)
-    scales = jnp.exp(every_high - highest[None])
+    highest_long, totals_long, summed_long = long_parts
+    shape = highest_long.shape
+    rows = highest_long.size
+    packed = jnp.concatenate(
+        [
+            summed_long.reshape(rows, HEAD_DIM),
+            highest_long.reshape(rows, 1),
+            totals_long.reshape(rows, 1),
+            jnp.zeros((rows, LANES - HEAD_DIM - 2), jnp.float32),
+        ],
+        axis=1,
+    )
+    reduced = seq_allreduce(packed, lax.axis_size("seq"))
     merged = (
-        highest,
-        jnp.sum(every_total * scales, axis=0),
-        jnp.sum(every_sum * scales[..., None], axis=0),
+        reduced[:, HEAD_DIM].reshape(shape),
+        reduced[:, HEAD_DIM + 1].reshape(shape),
+        reduced[:, :HEAD_DIM].reshape(shape + (HEAD_DIM,)),
     )
     long_att = finish(combine_parts(merged, fresh_part(queries_long, fresh_long)))
     short_term = jnp.dot(

time: 183 us -> 102 us (0.56)
  blocking collectives: 108 us -> 0 us
  Pallas kernels: 0 us -> 34.2 us
  other arithmetic: 10.8 us -> 1.87 us
  matrix products: 10.3 us -> 12.4 us
    all_gather x2 -> x0, blocking collectives: 108 us -> none  [the longest x1 54 us: per_device(): lax.all_gather(long_parts[1][None], 'seq', axis=0, tiled=True)]
    pallas_call x0 -> x1, Pallas kernels: none -> 34.2 us  [seq_allreduce(): pl.pallas_call(functools.partial(butterfly_kernel, rounds), out_shape=jax...]
    reduce_sum x2 -> x0, other arithmetic: 7.49 us -> none  [the longest x1 6.27 us: per_device(): jnp.sum(every_sum * scales[..., None], axis=0)]
    exp x1 -> x0, local copies, waits for them, and re-layouts: 3.03 us -> none  [per_device(): scales = jnp.exp(every_high - highest[None])]
    slice x1, local copies, waits for them, and re-layouts: 2.88 us -> 5.02 us  [per_device(): cache_short[0]]
    slice x1 -> x2, local copies, waits for them, and re-layouts: 3.22 us -> 4.39 us  [the longest x1 3.21 us: per_device(): cache_long[1]]
    unnamed x5 -> x4, waiting for transfers between devices: 20.5 us -> 20.4 us
  transfers between devices with their start and end apart: 3 -> 2, of which waited for: 1 -> 1; matrix products, arithmetic and copies ran while one was open for 14% -> 16% of each run, Pallas kernels for 0% -> 34%
where the time goes in v1:
time: 102 us; the launch traced here: 100 us
  Pallas kernels  34.2 us (34%)
  waiting for transfers between devices  20.4 us (20%)
  local copies, waits for them, and re-layouts  17.1 us (17%)
  between operations  14.3 us (14%)
  matrix products  12.4 us (12%)
  other arithmetic  1.87 us (2%)
    pallas_call x1, Pallas kernels, seq_allreduce(): pl.pallas_call(functools.partial(butterfly_kernel, rounds), out_shape=jax...  34.2 us
    unnamed x4, waiting for transfers between devices  20.4 us
    slice x1, local copies, waits for them, and re-layouts, per_device(): cache_short[0]  5.02 us
    unnamed x2, matrix products  4.41 us
    dot_general x4, matrix products, partial_softmax(): jnp.einsum('rjhd,rphd->rhjp', query_heads, key_heads, preferred_element_t...  4.23 us
    dot_general x4, matrix products, partial_softmax(): jnp.einsum('rhjp,rphd->rhjd', expo.astype(jnp.bfloat16), value_heads, pre...  3.76 us
    slice x1, local copies, waits for them, and re-layouts, per_device(): cache_long[1]  3.21 us
    unnamed x16, local copies, waits for them, and re-layouts  2.14 us
  transfers between devices with their start and end apart: 2, of which 1 were waited for; matrix products, arithmetic and copies ran while one was open for 16% of the time, Pallas kernels for 34%

profile of v1, /device:TPU:4, one launch (start us, length us, event | category | flops | bytes accessed | tf_op | source)
XLA Modules:
  0.0 100.4 jit_solution(14263011813883814202)
XLA Ops:
  7.2 0.9 reshape.158
  8.2 0.7 fusion.54
  8.9 0.1 reshape_squeeze.32
  9.0 0.1 fusion.29
  9.1 0.1 copy.94
  9.3 0.1 fusion.36
  9.4 0.1 fusion.44
  9.5 0.1 copy.95
  9.6 5.0 %fusion.51 = (bf16[1,2,1024,576]{2,3,1,0:T(8,128)(2,1)}, bf16[1,2,1024,576]{2,3,1,0:T(8,128)(2,1)}) fusion(bf16[2,2,1024,576]{2,3,1,0:T(8,128)(2,1)} %param.11), kind=kLoop, calls=%fused_computation.73 | loop fusion | bytes 9437184 | tf_op jit(solution)/shard_map/slice | solution.py:154
  14.7 0.1 copy.98
  14.8 0.1 copy.96
  14.9 0.1 reshape_squeeze.33
  15.0 2.3 %fusion.55 = (f32[2,9,4]{2,1,0:T(8,128)S(1)}, f32[2,9,4,1024]{3,2,1,0:T(4,128)S(1)}) fusion(bf16[2,1024,9,64]{1,3,2,0:T(8,128)(2,1)} %bitcast.66, bf16[2,4,9,64]{3,2,1,0:T(8,128)(2,1)S(1)} %reshape.158, pred[2,1024]{1,0:T(4,128)(4,1)S(1)} %iota_compare_fusion), kind=kOutput, calls=%fused_computation.77 | convolution fusion | flops 9658296 | bytes 2665760 | tf_op jit(solution)/shard_map/rjhd,rphd->rhjp/dot_general | solution.py:24
  17.4 0.3 fusion.11
  17.7 0.7 fusion.9
  18.4 0.2 fusion.10
  18.6 0.1 reshape_reshape.6
  18.7 2.2 %convolution_bitcast_fusion.1 = f32[2304,8]{1,0:T(8,128)} fusion(bf16[8,576]{1,0:T(8,128)(2,1)S(1)} %reshape_reshape.6, bf16[576,2304]{1,0:T(8,128)(2,1)S(1)} %copy-done), kind=kOutput, calls=%fused_computation.1 | convolution fusion | flops 21233664 | bytes 2737152
  21.0 0.1 reshape_squeeze.37
  21.1 0.1 reshape.160
  21.2 0.2 fusion.25
  21.4 0.2 copy.105
  21.6 0.1 fusion.27
  21.7 0.1 fusion.37
  21.9 0.2 copy.109
  22.1 3.2 %fusion.52 = (bf16[1,4,256,576]{2,3,1,0:T(8,128)(2,1)}, bf16[1,4,256,576]{2,3,1,0:T(8,128)(2,1)}) fusion(bf16[2,4,256,576]{2,3,1,0:T(8,128)(2,1)} %param.15), kind=kLoop, calls=%fused_computation.74 | loop fusion | bytes 4718592 | tf_op jit(solution)/shard_map/slice | solution.py:164
  25.4 1.6 %fusion.56 = (f32[4,9,4]{2,1,0:T(8,128)S(1)}, f32[4,9,4,256]{3,2,1,0:T(4,128)S(1)}) fusion(bf16[4,256,9,64]{1,3,2,0:T(8,128)(2,1)} %bitcast.67, bf16[4,4,9,64]{3,2,1,0:T(8,128)(2,1)S(1)} %reshape.160, pred[4,256]{1,0:T(4,128)(4,1)S(1)} %bitcast_and_fusion), kind=kOutput, calls=%fused_computation.78 | convolution fusion | flops 4829040 | bytes 1347136 | tf_op jit(solution)/shard_map/rjhd,rphd->rhjp/dot_general | solution.py:24
  27.1 0.2 fusion.17
  27.4 1.7 %fusion.19 = f32[4,9,4,64]{3,2,1,0:T(4,128)S(1)} fusion(bf16[4,256,9,64]{1,3,2,0:T(8,128)(2,1)} %bitcast.69, f32[4,9,4,256]{3,2,1,0:T(4,128)S(1)} %get-tuple-element.25, f32[4,9,4]{2,1,0:T(8,128)S(1)} %get-tuple-element.24, pred[4,256]{1,0:T(4,128)(4,1)S(1)} %bitcast_and_fusion), kind=kOutput, calls=%fused_computation.27 | convolution fusion | flops 4829184 | bytes 1365568 | tf_op jit(solution)/shard_map/rhjp,rphd->rhjd/dot_general | solution.py:31
  29.2 0.7 maximum_maximum_fusion.x_ref
  30.0 34.2 %shard_map.113 = f32[144,128]{1,0:T(8,128)} custom-call(f32[144,128]{1,0:T(8,128)} %maximum_maximum_fusion.x_ref), custom_call_target="tpu_custom_call" | custom-call | flops 884736 | bytes 884736 | tf_op jit(solution)/shard_map/pallas_call | solution.py:114
  64.2 0.1 reshape_squeeze.38
  64.3 1.2 %slice_reduce_fusion = (f32[144]{0:T(256)S(1)}, f32[144]{0:T(256)S(1)}) fusion(f32[144,128]{1,0:T(8,128)} %shard_map.113), kind=kLoop, calls=%fused_computation.29 | loop fusion | bytes 2304 | tf_op jit(solution)/shard_map/slice | solution.py:182
  65.5 0.1 reshape_squeeze.39
  65.6 0.1 copy.112
  65.7 0.1 reshape_squeeze.36
  65.8 0.1 copy.107
  65.9 0.1 copy.113
  66.1 0.1 copy.111
  66.2 0.1 copy.108
  66.3 1.1 %fusion.5 = bf16[4,4,9,64]{3,1,2,0:T(4,128)(2,1)S(1)} fusion(bf16[4,9,4,4]{3,2,1,0:T(4,128)(2,1)S(1)} %copy.109, f32[4,9,4,64]{3,2,1,0:T(4,128)} %bitcast.70, bf16[4,4,9,64]{3,2,1,0:T(8,128)(2,1)S(1)} %reshape_squeeze.38, f32[4,9,4]{2,1,0:T(8,128)S(1)} %copy.113, f32[4,9,4]{2,1,0:T(8,128)S(1)} %copy.111, f32[4,9,4]{2,1,0:T(8,128)S(1)} %copy.108), kind=kOutput, calls=%fused_computation.10 | convolution fusion | flops 119808 | bytes 76608 | tf_op jit(solution)/shard_map/rhjp,rphd->rhjd/dot_general | solution.py:31
  67.4 0.1 reshape_reshape.7
  67.5 2.2 %convolution_bitcast_fusion = f32[2304,16]{1,0:T(8,128)} fusion(bf16[16,576]{1,0:T(8,128)(2,1)S(1)} %reshape_reshape.7, bf16[576,2304]{1,0:T(8,128)(2,1)S(1)} %copy-done), kind=kOutput, calls=%fused_computation | convolution fusion | flops 42467328 | bytes 2820096
  69.8 1.0 %copy.116 = bf16[8,576]{1,0:T(8,128)(2,1)S(1)} copy(f32[8,576]{0,1:T(8,128)} %bitcast.71) | data formatting | bytes 27648
  70.8 0.6 reshape.159
  71.5 20.4 %reduce-scatter.9.cloned.1.call-done = f32[576,16]{1,0:T(8,128)} async-done(((f32[2304,16]{1,0:T(8,128)}), f32[576,16]{1,0:T(8,128)}) %reduce-scatter.9.cloned.1.call-update) | async-done | bytes 36880
  91.8 1.1 %copy.118 = bf16[16,576]{1,0:T(8,128)(2,1)S(1)} copy(f32[16,576]{0,1:T(8,128)} %bitcast.72) | data formatting | bytes 55296
  92.9 0.6 reshape.165
  (33 shorter events, 0.7 us)
Async XLA Ops:
  7.2 11.6 %copy-start = (bf16[576,2304]{1,0:T(8,128)(2,1)S(1)}, bf16[576,2304]{1,0:T(8,128)(2,1)}, u32[]{:S(2)}) copy-start(bf16[576,2304]{1,0:T(8,128)(2,1)} %param.19) | copy-start | bytes 7962628
  7.2 62.6 %reduce-scatter.7.cloned.1.call-start = ((), (), s32[]{:S(2)}) async-start(), calls=%async_computation.2 | async-start | bytes 1474560
  9.6 5.0 %copy-start.4 = (s32[2]{0:T(128)S(1)}, s32[2]{0:T(128)}, u32[]{:S(2)}) copy-start(s32[2]{0:T(128)} %param.13) | copy-start | bytes 28
  15.0 2.6 %copy-start.1 = (bf16[1,2,1024,576]{2,3,1,0:T(8,128)(2,1)S(1)}, bf16[1,2,1024,576]{2,3,1,0:T(8,128)(2,1)}, u32[]{:S(2)}) copy-start(bf16[1,2,1024,576]{2,3,1,0:T(8,128)(2,1)} %get-tuple-element.11) | copy-start | bytes 7077892
  18.7 2.3 %copy-start.2 = (bf16[2,4,4,576]{3,2,1,0:T(4,128)(2,1)S(1)}, bf16[2,4,4,576]{3,2,1,0:T(4,128)(2,1)}, u32[]{:S(2)}) copy-start(bf16[2,4,4,576]{3,2,1,0:T(4,128)(2,1)} %param.16) | copy-start | bytes 110596
  18.7 2.4 %copy-start.3 = (bf16[4,4,576]{2,1,0:T(4,128)(2,1)S(1)}, bf16[4,4,576]{2,1,0:T(4,128)(2,1)}, u32[]{:S(2)}) copy-start(bf16[4,4,576]{2,1,0:T(4,128)(2,1)} %param.14) | copy-start | bytes 55300
  20.9 70.9 %reduce-scatter.9.cloned.1.call-start = ((), (), s32[]{:S(2)}) async-start(), calls=%async_computation.3 | async-start | bytes 1474560
  22.1 3.2 %copy-start.6 = (s32[4,2]{0,1:T(2,128)S(1)}, s32[4,2]{0,1:T(2,128)}, u32[]{:S(2)}) copy-start(s32[4,2]{0,1:T(2,128)} %param.18) | copy-start | bytes 100
  22.1 3.2 %copy-start.5 = (s32[4]{0:T(128)S(1)}, s32[4]{0:T(128)}, u32[]{:S(2)}) copy-start(s32[4]{0:T(128)} %param.17) | copy-start | bytes 52
Sparse Core Ops, SparseCore 0:
  21.1 27.9 reduce-scatter.6
  69.9 21.9 reduce-scatter.8

commit v2 on v1

--- a/solution.py
+++ b/solution.py
@@ -131,6 +131,70 @@
     )(packed)
 
 
+def scatter_kernel(parts, x_ref, o_ref, recv, local_sem, send_sem, recv_sem):
+    me = lax.axis_index("tp")
+    row = lax.axis_index("seq")
+    barrier = pltpu.get_barrier_semaphore()
+    for d in range(1, parts):
+        pl.semaphore_signal(
+            barrier, inc=1, device_id=(row, (me + d) % parts), device_id_type=MESH
+        )
+    pl.semaphore_wait(barrier, parts - 1)
+    own = pltpu.make_async_copy(x_ref.at[me], recv.at[me], local_sem)
+    own.start()
+    copies = []
+    for d in range(1, parts):
+        copy = pltpu.make_async_remote_copy(
+            src_ref=x_ref.at[(me + d) % parts],
+            dst_ref=recv.at[me],
+            send_sem=send_sem.at[d - 1],
+            recv_sem=recv_sem.at[d - 1],
+            device_id=(row, (me + d) % parts),
+            device_id_type=MESH,
+        )
+        copy.start()
+        copies.append(copy)
+    own.wait()
+    for d in range(1, parts):
+        copies[d - 1].wait_send()
+        pltpu.make_async_remote_copy(
+            src_ref=x_ref.at[0],
+            dst_ref=recv.at[(me + parts - d) % parts],
+            send_sem=send_sem.at[d - 1],
+            recv_sem=recv_sem.at[d - 1],
+            device_id=(row, (me + parts - d) % parts),
+            device_id_type=MESH,
+        ).wait_recv()
+    total = recv[0]
+    for s in range(1, parts):
+        total = total + recv[s]
+    o_ref[...] = total
+
+
+def tp_reduce_scatter(term, parts):
+    rows, width = term.shape
+    cols = width // parts
+    blocks = jnp.transpose(term.reshape(rows, parts, cols), (1, 0, 2))
+    return pl.pallas_call(
+        functools.partial(scatter_kernel, parts),
+        out_shape=jax.ShapeDtypeStruct((rows, cols), jnp.float32),
+        in_specs=[pl.BlockSpec(memory_space=pltpu.VMEM)],
+        out_specs=pl.BlockSpec(memory_space=pltpu.VMEM),
+        scratch_shapes=[
+            pltpu.VMEM((parts, rows, cols), jnp.float32),
+            pltpu.SemaphoreType.DMA(()),
+            pltpu.SemaphoreType.DMA((parts - 1,)),
+            pltpu.SemaphoreType.DMA((parts - 1,)),
+        ],
+        compiler_params=pltpu.CompilerParams(collective_id=1, has_side_effects=True),
+        cost_estimate=pl.CostEstimate(
+            flops=rows * width,
+            transcendentals=0,
+            bytes_accessed=3 * rows * width * 4,
+        ),
+    )(blocks)
+
+
 def per_device(
     queries_short,
     cache_short,
@@ -190,7 +254,7 @@
         long_att.reshape(-1, long_att.shape[2]), out_weight, preferred_element_type=jnp.float32
     )
     short_cols = lax.psum_scatter(short_term, "tp", scatter_dimension=1, tiled=True)
-    long_cols = lax.psum_scatter(long_term, "tp", scatter_dimension=1, tiled=True)
+    long_cols = tp_reduce_scatter(long_term, lax.axis_size("tp"))
     short_out = short_cols.astype(jnp.bfloat16).reshape(
         request_count, token_count, short_cols.shape[1]
     )

time: 102 us -> 85.1 us (0.83); the launches traced: 100 us -> 84.6 us
  waiting for transfers between devices: 20.4 us -> 0.02 us
  Pallas kernels: 34.2 us -> 41.2 us
  matrix products: 12.4 us -> 7.41 us
  local copies, waits for them, and re-layouts: 17.1 us -> 19 us
    unnamed x4 -> x2, waiting for transfers between devices: 20.4 us -> 0.02 us
    pallas_call x0 -> x1, Pallas kernels: none -> 7.56 us  [tp_reduce_scatter(): pl.pallas_call(functools.partial(scatter_kernel, parts), out_shape=jax.Sh...]
    dot_general x0 -> x1, local copies, waits for them, and re-layouts: none -> 4.04 us  [per_device(): jnp.dot(long_att.reshape(-1, long_att.shape[2]), out_weight, preferred_el...]
    dot_general x4, matrix products: 4.23 us -> 1.13 us  [partial_softmax(): jnp.einsum('rjhd,rphd->rhjp', query_heads, key_heads, preferred_element_t...]
    unnamed x2 -> x1, matrix products: 4.41 us -> 2.18 us
    dot_general x0 -> x1, matrix products: none -> 1.61 us  [per_device(): jnp.dot(long_att.reshape(-1, long_att.shape[2]), out_weight, preferred_el...]
    slice x1, local copies, waits for them, and re-layouts: 3.21 us -> 1.8 us  [per_device(): cache_long[1]]
    dot_general x4, matrix products: 3.76 us -> 2.49 us  [partial_softmax(): jnp.einsum('rhjp,rphd->rhjd', expo.astype(jnp.bfloat16), value_heads, pre...]
  transfers between devices with their start and end apart: 2 -> 1, of which waited for: 1 -> 0; matrix products, arithmetic and copies ran while one was open for 16% -> 18% of each run, Pallas kernels for 34% -> 49%
where the time goes in v2:
time: 85.1 us; the launch traced here: 84.6 us
  Pallas kernels  41.2 us (48%)
  local copies, waits for them, and re-layouts  19 us (22%)
  between operations  14.3 us (17%)
  matrix products  7.41 us (9%)
  other arithmetic  2.66 us (3%)
    pallas_call x1, Pallas kernels, seq_allreduce(): pl.pallas_call(functools.partial(butterfly_kernel, rounds), out_shape=jax...  33.6 us
    pallas_call x1, Pallas kernels, tp_reduce_scatter(): pl.pallas_call(functools.partial(scatter_kernel, parts), out_shape=jax.Sh...  7.56 us
    slice x1, local copies, waits for them, and re-layouts, per_device(): cache_short[0]  4.56 us
    dot_general x1, local copies, waits for them, and re-layouts, per_device(): jnp.dot(long_att.reshape(-1, long_att.shape[2]), out_weight, preferred_el...  4.04 us
    dot_general x4, matrix products, partial_softmax(): jnp.einsum('rhjp,rphd->rhjd', expo.astype(jnp.bfloat16), value_heads, pre...  2.49 us
    unnamed x1, matrix products  2.18 us
    unnamed x15, local copies, waits for them, and re-layouts  1.94 us
    slice x1, local copies, waits for them, and re-layouts, per_device(): cache_long[1]  1.8 us
  transfers between devices with their start and end apart: 1, of which 0 were waited for; matrix products, arithmetic and copies ran while one was open for 18% of the time, Pallas kernels for 49%

profile of v2, /device:TPU:4, one launch (start us, length us, event | category | flops | bytes accessed | tf_op | source)
XLA Modules:
  0.0 84.6 jit_solution(9785890609161183468)
XLA Ops:
  7.2 0.8 reshape.160
  8.0 0.7 fusion.54
  8.8 0.1 fusion.29
  9.0 0.1 copy.99
  9.1 0.1 fusion.36
  9.2 0.1 fusion.44
  9.3 0.1 copy.100
  9.4 4.6 %fusion.51 = (bf16[1,2,1024,576]{2,3,1,0:T(8,128)(2,1)S(1)}, bf16[1,2,1024,576]{2,3,1,0:T(8,128)(2,1)}) fusion(bf16[2,2,1024,576]{2,3,1,0:T(8,128)(2,1)} %param.11), kind=kLoop, calls=%fused_computation.73 | loop fusion | bytes 9437184 | tf_op jit(solution)/shard_map/slice | solution.py:218
  14.1 0.1 copy.103
  14.2 0.1 copy.101
  14.4 0.5 fusion.55
  14.9 0.3 fusion.11
  15.2 0.9 %copy-done.1 = bf16[1,2,1024,576]{2,3,1,0:T(8,128)(2,1)S(1)} copy-done((bf16[1,2,1024,576]{2,3,1,0:T(8,128)(2,1)S(1)}, bf16[1,2,1024,576]{2,3,1,0:T(8,128)(2,1)}, u32[]{:S(2)}) %copy-start.1) | copy-done | bytes 2359320
  16.1 0.7 fusion.9
  16.8 0.2 fusion.10
  17.0 0.1 reshape_reshape.6
  17.2 2.2 %convolution_bitcast_fusion = f32[2304,8]{1,0:T(8,128)} fusion(bf16[8,576]{1,0:T(8,128)(2,1)S(1)} %reshape_reshape.6, bf16[576,2304]{1,0:T(8,128)(2,1)S(1)} %copy-done), kind=kOutput, calls=%fused_computation | convolution fusion | flops 21233664 | bytes 2737152
  19.4 0.1 reshape_squeeze.37
  19.5 0.1 reshape.162
  19.6 0.2 fusion.25
  19.8 0.2 copy.110
  20.0 0.1 fusion.27
  20.1 0.1 fusion.37
  20.2 0.2 copy.114
  20.4 1.8 %fusion.52 = (bf16[1,4,256,576]{2,3,1,0:T(8,128)(2,1)S(1)}, bf16[1,4,256,576]{2,3,1,0:T(8,128)(2,1)S(1)}) fusion(bf16[2,4,256,576]{2,3,1,0:T(8,128)(2,1)} %param.15), kind=kLoop, calls=%fused_computation.74 | loop fusion | bytes 4718592 | tf_op jit(solution)/shard_map/slice | solution.py:228
  22.4 0.3 fusion.56
  22.8 0.2 fusion.17
  23.1 0.5 fusion.19
  23.7 0.8 maximum_maximum_fusion.x_ref
  24.4 33.6 %shard_map.113 = f32[144,128]{1,0:T(8,128)} custom-call(f32[144,128]{1,0:T(8,128)} %maximum_maximum_fusion.x_ref), custom_call_target="tpu_custom_call" | custom-call | flops 884736 | bytes 884736 | tf_op jit(solution)/shard_map/pallas_call | solution.py:114
  58.1 0.1 reshape_squeeze.38
  58.2 1.2 %slice_reduce_fusion = (f32[144]{0:T(256)S(1)}, f32[144]{0:T(256)S(1)}) fusion(f32[144,128]{1,0:T(8,128)} %shard_map.113), kind=kLoop, calls=%fused_computation.29 | loop fusion | bytes 2304 | tf_op jit(solution)/shard_map/slice | solution.py:246
  59.4 0.1 reshape_squeeze.39
  59.5 0.1 copy.117
  59.6 0.1 reshape_squeeze.36
  59.7 0.1 copy.112
  59.8 0.1 copy.118
  59.9 0.1 copy.116
  60.0 0.1 copy.113
  60.2 1.1 %fusion.5 = bf16[4,4,9,64]{3,1,2,0:T(4,128)(2,1)S(1)} fusion(bf16[4,9,4,4]{3,2,1,0:T(4,128)(2,1)S(1)} %copy.114, f32[4,9,4,64]{3,2,1,0:T(4,128)} %bitcast.73, bf16[4,4,9,64]{3,2,1,0:T(8,128)(2,1)S(1)} %reshape_squeeze.38, f32[4,9,4]{2,1,0:T(8,128)S(1)} %copy.118, f32[4,9,4]{2,1,0:T(8,128)S(1)} %copy.116, f32[4,9,4]{2,1,0:T(8,128)S(1)} %copy.113), kind=kOutput, calls=%fused_computation.10 | convolution fusion | flops 119808 | bytes 76608 | tf_op jit(solution)/shard_map/rhjp,rphd->rhjd/dot_general | solution.py:31
  61.3 0.1 reshape.168
  61.4 4.0 %copy.121 = bf16[2304,576]{1,0:T(8,128)(2,1)S(1)} copy(bf16[2304,576]{0,1:T(8,128)(2,1)} %bitcast.68) | data formatting | bytes 5308416 | tf_op jit(solution)/shard_map/dot_general | solution.py:253
  65.4 1.6 %convolution_bitcast_fusion.1.x_ref = f32[4,16,576]{2,1,0:T(8,128)} fusion(bf16[16,576,1]{1,0,2:T(8,128)(2,1)S(1)} %reshape.168, bf16[4,576,576]{2,1,0:T(8,128)(2,1)S(1)} %bitcast.67), kind=kOutput, calls=%fused_computation.3 | convolution fusion | flops 42467328 | bytes 2820096 | tf_op jit(solution)/shard_map/dot_general | solution.py:253
  67.1 7.6 %shard_map.114 = f32[16,576]{1,0:T(8,128)} custom-call(f32[4,16,576]{2,1,0:T(8,128)} %convolution_bitcast_fusion.1.x_ref), custom_call_target="tpu_custom_call" | custom-call | flops 36864 | bytes 442368 | tf_op jit(solution)/shard_map/pallas_call | solution.py:178
  74.6 0.8 convert_element_type.32
  75.4 0.6 reshape.167
  76.0 1.0 %copy.123 = bf16[8,576]{1,0:T(8,128)(2,1)S(1)} copy(f32[8,576]{0,1:T(8,128)} %bitcast.74) | data formatting | bytes 27648
  77.1 0.6 reshape.161
  (32 shorter events, 0.8 us)
Async XLA Ops:
  7.2 68.9 %reduce-scatter.4.cloned.1.call-start = ((), (), s32[]{:S(2)}) async-start(), calls=%async_computation.1 | async-start | bytes 1474560
  9.4 4.6 %copy-start.4 = (s32[2]{0:T(128)S(1)}, s32[2]{0:T(128)}, u32[]{:S(2)}) copy-start(s32[2]{0:T(128)} %param.13) | copy-start | bytes 28
  14.4 1.7 %copy-start.1 = (bf16[1,2,1024,576]{2,3,1,0:T(8,128)(2,1)S(1)}, bf16[1,2,1024,576]{2,3,1,0:T(8,128)(2,1)}, u32[]{:S(2)}) copy-start(bf16[1,2,1024,576]{2,3,1,0:T(8,128)(2,1)} %get-tuple-element.11) | copy-start | bytes 7077892
  14.9 2.2 %copy-start = (bf16[576,2304]{1,0:T(8,128)(2,1)S(1)}, bf16[576,2304]{1,0:T(8,128)(2,1)}, u32[]{:S(2)}) copy-start(bf16[576,2304]{1,0:T(8,128)(2,1)} %param.19) | copy-start | bytes 7962628
  17.1 2.2 %copy-start.2 = (bf16[2,4,4,576]{3,2,1,0:T(4,128)(2,1)S(1)}, bf16[2,4,4,576]{3,2,1,0:T(4,128)(2,1)}, u32[]{:S(2)}) copy-start(bf16[2,4,4,576]{3,2,1,0:T(4,128)(2,1)} %param.16) | copy-start | bytes 110596
  17.1 2.4 %copy-start.3 = (bf16[4,4,576]{2,1,0:T(4,128)(2,1)S(1)}, bf16[4,4,576]{2,1,0:T(4,128)(2,1)}, u32[]{:S(2)}) copy-start(bf16[4,4,576]{2,1,0:T(4,128)(2,1)} %param.14) | copy-start | bytes 55300
  20.4 1.8 %copy-start.6 = (s32[4,2]{0,1:T(2,128)S(1)}, s32[4,2]{0,1:T(2,128)}, u32[]{:S(2)}) copy-start(s32[4,2]{0,1:T(2,128)} %param.18) | copy-start | bytes 100
  20.4 1.9 %copy-start.5 = (s32[4]{0:T(128)S(1)}, s32[4]{0:T(128)}, u32[]{:S(2)}) copy-start(s32[4]{0:T(128)} %param.17) | copy-start | bytes 52
Sparse Core Ops, SparseCore 0:
  19.5 27.9 reduce-scatter.3

commit v3 on v2

--- a/solution.py
+++ b/solution.py
@@ -247,19 +247,13 @@
         reduced[:, :HEAD_DIM].reshape(shape + (HEAD_DIM,)),
     )
     long_att = finish(combine_parts(merged, fresh_part(queries_long, fresh_long)))
-    short_term = jnp.dot(
-        short_att.reshape(-1, short_att.shape[2]), out_weight, preferred_element_type=jnp.float32
-    )
-    long_term = jnp.dot(
-        long_att.reshape(-1, long_att.shape[2]), out_weight, preferred_element_type=jnp.float32
-    )
-    short_cols = lax.psum_scatter(short_term, "tp", scatter_dimension=1, tiled=True)
-    long_cols = tp_reduce_scatter(long_term, lax.axis_size("tp"))
-    short_out = short_cols.astype(jnp.bfloat16).reshape(
-        request_count, token_count, short_cols.shape[1]
-    )
-    long_out = long_cols.astype(jnp.bfloat16).reshape(
-        long_att.shape[0], long_att.shape[1], long_cols.shape[1]
+    short_rows = short_att.reshape(-1, short_att.shape[2])
+    both = jnp.concatenate([short_rows, long_att.reshape(-1, long_att.shape[2])], axis=0)
+    term = jnp.dot(both, out_weight, preferred_element_type=jnp.float32)
+    cols = tp_reduce_scatter(term, lax.axis_size("tp")).astype(jnp.bfloat16)
+    short_out = cols[: short_rows.shape[0]].reshape(request_count, token_count, cols.shape[1])
+    long_out = cols[short_rows.shape[0] :].reshape(
+        long_att.shape[0], long_att.shape[1], cols.shape[1]
     )
     return (short_out, long_out)
 

time: 85.1 us -> 71.3 us (0.84)
  between operations: 14.3 us -> 0.83 us
  local copies, waits for them, and re-layouts: 19 us -> 14.4 us
  matrix products: 7.41 us -> 9.94 us
  Pallas kernels: 41.2 us -> 42.2 us
    dot_general x1 -> x0, local copies, waits for them, and re-layouts: 4.04 us -> none  [per_device(): jnp.dot(long_att.reshape(-1, long_att.shape[2]), out_weight, preferred_el...]
    dot_general x4, matrix products: 1.13 us -> 4.08 us  [partial_softmax(): jnp.einsum('rjhd,rphd->rhjp', query_heads, key_heads, preferred_element_t...]
    dot_general x4, matrix products: 2.49 us -> 5.38 us  [partial_softmax(): jnp.einsum('rhjp,rphd->rhjd', expo.astype(jnp.bfloat16), value_heads, pre...]
    unnamed x1 -> x0, matrix products: 2.18 us -> none
    unnamed x15 -> x14, local copies, waits for them, and re-layouts: 1.94 us -> 0.03 us
    slice x1, local copies, waits for them, and re-layouts: 1.8 us -> 3.2 us  [per_device(): cache_long[1]]
    dot_general x1, matrix products: 1.61 us -> 0.48 us  [per_device(): term = jnp.dot(both, out_weight, preferred_element_type=jnp.float32)]
    reshape x2 -> x4, local copies, waits for them, and re-layouts: 1.26 us -> 2.13 us  [the longest x2 0.9 us: tp_reduce_scatter(): blocks = jnp.transpose(term.reshape(rows, parts, cols), (1, 0, 2))]
  transfers between devices with their start and end apart: 1 -> 0, of which waited for: 0 -> 0; matrix products, arithmetic and copies ran while one was open for 18% -> 0% of each run, Pallas kernels for 49% -> 0%
where the time goes in v3:
time: 71.3 us; the launch traced here: 70.8 us
  Pallas kernels  42.2 us (59%)
  local copies, waits for them, and re-layouts  14.4 us (20%)
  matrix products  9.94 us (14%)
  other arithmetic  3.51 us (5%)
  between operations  0.83 us (1%)
    pallas_call x1, Pallas kernels, seq_allreduce(): pl.pallas_call(functools.partial(butterfly_kernel, rounds), out_shape=jax...  34.1 us
    pallas_call x1, Pallas kernels, tp_reduce_scatter(): pl.pallas_call(functools.partial(scatter_kernel, parts), out_shape=jax.Sh...  8.06 us
    dot_general x4, matrix products, partial_softmax(): jnp.einsum('rhjp,rphd->rhjd', expo.astype(jnp.bfloat16), value_heads, pre...  5.38 us
    slice x1, local copies, waits for them, and re-layouts, per_device(): cache_short[0]  5.02 us
    dot_general x4, matrix products, partial_softmax(): jnp.einsum('rjhd,rphd->rhjp', query_heads, key_heads, preferred_element_t...  4.08 us
    slice x1, local copies, waits for them, and re-layouts, per_device(): cache_long[1]  3.2 us

profile of v3, /device:TPU:4, one launch (start us, length us, event | category | flops | bytes accessed | tf_op | source)
XLA Modules:
  0.0 70.8 jit_solution(1861519467818779781)
XLA Ops:
  0.6 0.9 %iota_compare_fusion = pred[2,1024]{1,0:T(4,128)(4,1)S(1)} fusion(s32[2]{0:T(128)} %param.13), kind=kLoop, calls=%fused_computation.65 | loop fusion | flops 2048 | bytes 2056 | tf_op jit(solution)/shard_map/lt | solution.py:214
  1.5 5.0 %fusion.56 = (bf16[1,2,1024,576]{2,3,1,0:T(8,128)(2,1)}, bf16[1,2,1024,576]{2,3,1,0:T(8,128)(2,1)}) fusion(bf16[2,2,1024,576]{2,3,1,0:T(8,128)(2,1)} %param.11), kind=kLoop, calls=%fused_computation.77 | loop fusion | bytes 9437184 | tf_op jit(solution)/shard_map/slice | solution.py:218
  6.6 0.1 reshape.161
  6.6 2.2 %fusion.61 = (f32[2,9,4]{2,1,0:T(8,128)S(1)}, f32[2,9,4,1024]{3,2,1,0:T(4,128)S(1)}) fusion(bf16[2,1024,9,64]{1,3,2,0:T(8,128)(2,1)} %bitcast.60, bf16[2,4,9,64]{3,2,1,0:T(8,128)(2,1)S(1)} %reshape.161, pred[2,1024]{1,0:T(4,128)(4,1)S(1)} %iota_compare_fusion), kind=kOutput, calls=%fused_computation.82 | convolution fusion | flops 9658296 | bytes 2665760 | tf_op jit(solution)/shard_map/rjhd,rphd->rhjp/dot_general | solution.py:24
  8.8 0.3 fusion.11
  9.1 0.1 reshape_squeeze.32
  9.2 0.1 fusion.33
  9.3 0.1 copy.83
  9.5 0.1 fusion.40
  9.6 0.1 fusion.48
  9.7 0.1 copy.87
  9.8 0.1 copy.84
  9.9 2.4 %fusion.9 = f32[2,4,9,64]{3,1,2,0:T(4,128)S(1)} fusion(bf16[2,1024,9,64]{1,3,2,0:T(8,128)(2,1)} %bitcast.62, f32[2,9,4,1024]{3,2,1,0:T(4,128)S(1)} %get-tuple-element.25, f32[2,9,4]{2,1,0:T(8,128)S(1)} %get-tuple-element.24, pred[2,1024]{1,0:T(4,128)(4,1)S(1)} %iota_compare_fusion, f32[2,4,9]{1,2,0:T(8,128)S(1)} %get-tuple-element.6), kind=kOutput, calls=%fused_computation.14 | convolution fusion | flops 9662976 | bytes 2675264 | tf_op jit(solution)/shard_map/rhjp,rphd->rhjd/dot_general | solution.py:31
  12.3 0.2 copy.85
  12.5 0.1 reshape_squeeze.33
  12.6 0.2 fusion.10
  12.8 0.1 reshape_reshape.6
  13.0 3.2 %fusion.57 = (bf16[1,4,256,576]{2,3,1,0:T(8,128)(2,1)}, bf16[1,4,256,576]{2,3,1,0:T(8,128)(2,1)}) fusion(bf16[2,4,256,576]{2,3,1,0:T(8,128)(2,1)} %param.15), kind=kLoop, calls=%fused_computation.78 | loop fusion | bytes 4718592 | tf_op jit(solution)/shard_map/slice | solution.py:228
  16.2 0.1 reshape.162
  16.3 1.6 %fusion.60 = (f32[4,9,4]{2,1,0:T(8,128)S(1)}, f32[4,9,4,256]{3,2,1,0:T(4,128)S(1)}) fusion(bf16[4,256,9,64]{1,3,2,0:T(8,128)(2,1)} %bitcast.61, bf16[4,4,9,64]{3,2,1,0:T(8,128)(2,1)S(1)} %reshape.162, pred[4,256]{1,0:T(4,128)(4,1)S(1)} %bitcast_and_fusion), kind=kOutput, calls=%fused_computation.81 | convolution fusion | flops 4829040 | bytes 1347136 | tf_op jit(solution)/shard_map/rjhd,rphd->rhjp/dot_general | solution.py:24
  17.9 1.7 %fusion.19 = f32[4,9,4,64]{3,2,1,0:T(4,128)S(1)} fusion(bf16[4,256,9,64]{1,3,2,0:T(8,128)(2,1)} %bitcast.63, f32[4,9,4,256]{3,2,1,0:T(4,128)S(1)} %get-tuple-element.23, f32[4,9,4]{2,1,0:T(8,128)S(1)} %get-tuple-element.22, pred[4,256]{1,0:T(4,128)(4,1)S(1)} %bitcast_and_fusion), kind=kOutput, calls=%fused_computation.26 | convolution fusion | flops 4829184 | bytes 1365568 | tf_op jit(solution)/shard_map/rhjp,rphd->rhjd/dot_general | solution.py:31
  19.6 0.2 fusion.17
  20.1 0.7 %maximum_maximum_fusion.x_ref = f32[144,128]{1,0:T(8,128)} fusion(f32[144,1]{1,0:T(8,128)S(1)} %reshape.171, f32[144,1]{1,0:T(8,128)S(1)} %reshape.170, f32[144,64]{1,0:T(8,128)S(1)} %bitcast.66, f32[128]{0:T(128)S(1)} %pad.5.clone), kind=kLoop, calls=%fused_computation.27 | loop fusion | flops 55296 | bytes 112256 | tf_op jit(solution)/shard_map/concatenate | solution.py:234
  20.9 34.1 %shard_map.113 = f32[144,128]{1,0:T(8,128)} custom-call(f32[144,128]{1,0:T(8,128)} %maximum_maximum_fusion.x_ref), custom_call_target="tpu_custom_call" | custom-call | flops 884736 | bytes 884736 | tf_op jit(solution)/shard_map/pallas_call | solution.py:114
  55.0 1.2 %slice_reduce_fusion = (f32[144]{0:T(256)S(1)}, f32[144]{0:T(256)S(1)}) fusion(f32[144,128]{1,0:T(8,128)} %shard_map.113), kind=kLoop, calls=%fused_computation.28 | loop fusion | bytes 2304 | tf_op jit(solution)/shard_map/slice | solution.py:246
  56.2 0.1 reshape_squeeze.39
  56.3 0.1 copy.101
  56.4 0.1 reshape_squeeze.36
  56.5 0.1 copy.96
  56.6 0.1 reshape_squeeze.37
  56.7 0.2 fusion.25
  56.9 0.2 copy.94
  57.1 0.1 fusion.31
  57.2 0.1 fusion.41
  57.4 0.1 copy.100
  57.5 0.1 copy.102
  57.6 0.1 copy.97
  57.7 0.2 copy.98
  57.9 0.1 reshape_squeeze.38
  58.0 1.1 %fusion.5 = bf16[4,4,9,64]{3,1,2,0:T(4,128)(2,1)S(1)} fusion(bf16[4,9,4,4]{3,2,1,0:T(4,128)(2,1)S(1)} %copy.98, f32[4,9,4,64]{3,2,1,0:T(4,128)} %bitcast.65, bf16[4,4,9,64]{3,2,1,0:T(8,128)(2,1)S(1)} %reshape_squeeze.38, f32[4,9,4]{2,1,0:T(8,128)S(1)} %copy.102, f32[4,9,4]{2,1,0:T(8,128)S(1)} %copy.100, f32[4,9,4]{2,1,0:T(8,128)S(1)} %copy.97), kind=kOutput, calls=%fused_computation.8 | convolution fusion | flops 119808 | bytes 76608 | tf_op jit(solution)/shard_map/rhjp,rphd->rhjd/dot_general | solution.py:31
  59.1 0.1 reshape_reshape.7
  59.3 0.5 fusion.27
  59.7 0.2 reshape.167
  60.0 0.7 copy.126
  60.7 8.1 %shard_map.114 = f32[24,576]{1,0:T(8,128)} custom-call(f32[4,24,576]{2,1,0:T(8,128)} %bitcast.64), custom_call_target="tpu_custom_call" | custom-call | flops 55296 | bytes 663552 | tf_op jit(solution)/shard_map/pallas_call | solution.py:178
  68.7 0.8 %convert_element_type.28 = bf16[24,576]{1,0:T(8,128)(2,1)S(1)} convert(f32[24,576]{1,0:T(8,128)} %shard_map.114) | non-fusion elementwise | flops 13824 | bytes 82944 | tf_op jit(solution)/shard_map/convert_element_type | solution.py:253
  69.6 0.6 reshape.169
  70.2 0.6 reshape.168
  (30 shorter events, 0.4 us)
Async XLA Ops:
  0.6 58.6 %copy-start = (bf16[576,2304]{1,0:T(8,128)(2,1)S(1)}, bf16[576,2304]{1,0:T(8,128)(2,1)}, u32[]{:S(2)}) copy-start(bf16[576,2304]{1,0:T(8,128)(2,1)} %param.19) | copy-start | bytes 7962628
  1.5 5.0 %copy-start.4 = (bf16[2,4,576]{2,1,0:T(4,128)(2,1)S(1)}, bf16[2,4,576]{2,1,0:T(4,128)(2,1)}, u32[]{:S(2)}) copy-start(bf16[2,4,576]{2,1,0:T(4,128)(2,1)} %param.10) | copy-start | bytes 27652
  6.5 2.5 %copy-start.2 = (bf16[2,2,4,576]{3,2,1,0:T(4,128)(2,1)S(1)}, bf16[2,2,4,576]{3,2,1,0:T(4,128)(2,1)}, u32[]{:S(2)}) copy-start(bf16[2,2,4,576]{3,2,1,0:T(4,128)(2,1)} %param.12) | copy-start | bytes 55300
  8.8 4.1 %copy-start.6 = (s32[4,2]{0,1:T(2,128)S(1)}, s32[4,2]{0,1:T(2,128)}, u32[]{:S(2)}) copy-start(s32[4,2]{0,1:T(2,128)} %param.18) | copy-start | bytes 100
  8.8 4.1 %copy-start.5 = (s32[4]{0:T(128)S(1)}, s32[4]{0:T(128)}, u32[]{:S(2)}) copy-start(s32[4]{0:T(128)} %param.17) | copy-start | bytes 52
  13.0 3.2 %copy-start.3 = (bf16[4,4,576]{2,1,0:T(4,128)(2,1)S(1)}, bf16[4,4,576]{2,1,0:T(4,128)(2,1)}, u32[]{:S(2)}) copy-start(bf16[4,4,576]{2,1,0:T(4,128)(2,1)} %param.14) | copy-start | bytes 55300
  16.2 40.4 %copy-start.1 = (bf16[2,4,4,576]{3,2,1,0:T(4,128)(2,1)S(1)}, bf16[2,4,4,576]{3,2,1,0:T(4,128)(2,1)}, u32[]{:S(2)}) copy-start(bf16[2,4,4,576]{3,2,1,0:T(4,128)(2,1)} %param.16) | copy-start | bytes 110596

commit v4 on v3

--- a/solution.py
+++ b/solution.py
@@ -195,6 +195,107 @@
     )(blocks)
 
 
+def attention_kernel(with_fresh, q_ref, k_ref, v_ref, mask_ref, *rest):
+    tokens, width = q_ref.shape[1], q_ref.shape[2]
+    rows = (width // HEAD_DIM) * tokens
+    pick = (
+        lax.broadcasted_iota(jnp.int32, (rows, tokens), 0) % tokens
+        == lax.broadcasted_iota(jnp.int32, (rows, tokens), 1)
+    ).astype(jnp.bfloat16)
+    head_lanes = (
+        lax.broadcasted_iota(jnp.int32, (rows, width), 0) // tokens
+        == lax.broadcasted_iota(jnp.int32, (rows, width), 1) // HEAD_DIM
+    )
+    spread = jnp.dot(pick, q_ref[0], preferred_element_type=jnp.float32)
+    query = jnp.where(head_lanes, spread, 0.0).astype(jnp.bfloat16)
+    contract = (((1,), (1,)), ((), ()))
+    scale = 1.0 / math.sqrt(HEAD_DIM)
+    scores = lax.dot_general(
+        query, k_ref[0, 0], contract, preferred_element_type=jnp.float32
+    ) * scale
+    usable = mask_ref[0] != 0
+    scores = jnp.where(usable, scores, NEGATIVE)
+    highest = jnp.max(scores, axis=1, keepdims=True)
+    if with_fresh:
+        fk_ref, fv_ref, o_ref = rest
+        fresh_scores = lax.dot_general(
+            query, fk_ref[0, 0], contract, preferred_element_type=jnp.float32
+        ) * scale
+        causal = lax.broadcasted_iota(jnp.int32, (rows, tokens), 1) <= (
+            lax.broadcasted_iota(jnp.int32, (rows, tokens), 0) % tokens
+        )
+        fresh_scores = jnp.where(causal, fresh_scores, NEGATIVE)
+        highest = jnp.maximum(highest, jnp.max(fresh_scores, axis=1, keepdims=True))
+    expo = jnp.where(usable, jnp.exp(scores - highest), 0.0)
+    totals = jnp.sum(expo, axis=1, keepdims=True)
+    summed = jnp.dot(
+        expo.astype(jnp.bfloat16), v_ref[0, 0], preferred_element_type=jnp.float32
+    )
+    if with_fresh:
+        fresh_expo = jnp.where(causal, jnp.exp(fresh_scores - highest), 0.0)
+        totals = totals + jnp.sum(fresh_expo, axis=1, keepdims=True)
+        summed = summed + jnp.dot(
+            fresh_expo.astype(jnp.bfloat16), fv_ref[0, 0], preferred_element_type=jnp.float32
+        )
+        normed = jnp.where(head_lanes, (summed / totals).astype(jnp.bfloat16), 0.0)
+        gather = (
+            lax.broadcasted_iota(jnp.int32, (tokens, rows), 1) % tokens
+            == lax.broadcasted_iota(jnp.int32, (tokens, rows), 0)
+        ).astype(jnp.bfloat16)
+        o_ref[0] = jnp.dot(
+            gather, normed.astype(jnp.bfloat16), preferred_element_type=jnp.float32
+        ).astype(o_ref.dtype)
+    else:
+        sum_ref, top_ref, total_ref = rest
+        sum_ref[0] = summed
+        top_ref[0] = highest
+        total_ref[0] = totals
+
+
+def attention(queries, cache, mask, fresh=None):
+    count, tokens, width = queries.shape
+    positions = cache.shape[2]
+    rows = (width // HEAD_DIM) * tokens
+    specs = [
+        pl.BlockSpec((1, tokens, width), lambda r: (r, 0, 0)),
+        pl.BlockSpec((1, 1, positions, width), lambda r: (0, r, 0, 0)),
+        pl.BlockSpec((1, 1, positions, width), lambda r: (1, r, 0, 0)),
+        pl.BlockSpec((1, 1, positions), lambda r: (r, 0, 0)),
+    ]
+    operands = [queries, cache, cache, mask]
+    if fresh is not None:
+        specs += [
+            pl.BlockSpec((1, 1, tokens, width), lambda r: (0, r, 0, 0)),
+            pl.BlockSpec((1, 1, tokens, width), lambda r: (1, r, 0, 0)),
+        ]
+        operands += [fresh, fresh]
+        out_shape = jax.ShapeDtypeStruct((count, tokens, width), jnp.bfloat16)
+        out_specs = pl.BlockSpec((1, tokens, width), lambda r: (r, 0, 0))
+    else:
+        out_shape = (
+            jax.ShapeDtypeStruct((count, rows, width), jnp.float32),
+            jax.ShapeDtypeStruct((count, rows, 1), jnp.float32),
+            jax.ShapeDtypeStruct((count, rows, 1), jnp.float32),
+        )
+        out_specs = (
+            pl.BlockSpec((1, rows, width), lambda r: (r, 0, 0)),
+            pl.BlockSpec((1, rows, 1), lambda r: (r, 0, 0)),
+            pl.BlockSpec((1, rows, 1), lambda r: (r, 0, 0)),
+        )
+    return pl.pallas_call(
+        functools.partial(attention_kernel, fresh is not None),
+        out_shape=out_shape,
+        grid=(count,),
+        in_specs=specs,
+        out_specs=out_specs,
+        cost_estimate=pl.CostEstimate(
+            flops=4 * count * rows * positions * width,
+            transcendentals=count * rows * positions,
+            bytes_accessed=2 * count * positions * width * 2,
+        ),
+    )(*operands)
+
+
 def per_device(
     queries_short,
     cache_short,
@@ -207,26 +308,30 @@
     block_live,
     out_weight,
 ):
-    short_query = split_heads(queries_short)
     request_count = queries_short.shape[0]
     token_count = queries_short.shape[1]
     positions = cache_short.shape[2]
-    usable = (jnp.arange(positions, dtype=jnp.int32)[None, :] < short_len[:, None])[
-        :, None, None, :
-    ]
-    short_parts = partial_softmax(
-        short_query, split_heads(cache_short[0]), split_heads(cache_short[1]), usable
-    )
-    short_att = finish(combine_parts(short_parts, fresh_part(queries_short, fresh_short)))
+    usable = jnp.arange(positions, dtype=jnp.int32)[None, :] < short_len[:, None]
+    short_att = attention(
+        queries_short, cache_short, usable.astype(jnp.int32)[:, None, :], fresh_short
+    )
     local_len = cache_long.shape[2]
     spots = lax.axis_index("seq") * local_len + jnp.arange(local_len, dtype=jnp.int32)
     live = jnp.repeat(block_live, local_len // block_live.shape[1], axis=1) == 1
-    long_usable = ((spots[None, :] < long_len[:, None]) & live)[:, None, None, :]
-    long_parts = partial_softmax(
-        split_heads(queries_long),
-        split_heads(cache_long[0]),
-        split_heads(cache_long[1]),
-        long_usable,
+    long_usable = (spots[None, :] < long_len[:, None]) & live
+    long_sum, long_top, long_total = attention(
+        queries_long, cache_long, long_usable.astype(jnp.int32)[:, None, :]
+    )
+    long_count = queries_long.shape[0]
+    heads = queries_long.shape[2] // HEAD_DIM
+    diagonal = jnp.eye(heads, dtype=jnp.float32)[None, :, None, :, None]
+    long_parts = (
+        long_top.reshape(long_count, heads, token_count),
+        long_total.reshape(long_count, heads, token_count),
+        jnp.sum(
+            long_sum.reshape(long_count, heads, token_count, heads, HEAD_DIM) * diagonal,
+            axis=3,
+        ),
     )
     highest_long, totals_long, summed_long = long_parts
     shape = highest_long.shape

time: 71.3 us -> 86.3 us (1.21)
  Pallas kernels: 42.2 us -> 51.9 us
  matrix products: 9.94 us -> 1.72 us
  local copies, waits for them, and re-layouts: 14.4 us -> 22 us
  other arithmetic: 3.51 us -> 8.92 us
    unnamed x14 -> x4, local copies, waits for them, and re-layouts: 0.03 us -> 12 us
    pallas_call x0 -> x2, Pallas kernels: none -> 9.74 us  [attention(): pl.pallas_call(functools.partial(attention_kernel, fresh is not None), ou...]
    slice x2 -> x0, local copies, waits for them, and re-layouts: 8.22 us -> none  [the longest x1 5.02 us: per_device(): cache_short[0]]
    dot_general x4 -> x1, matrix products: 5.38 us -> 1.09 us  [partial_softmax(): jnp.einsum('rhjp,rphd->rhjd', expo.astype(jnp.bfloat16), value_heads, pre...]
    dot_general x4 -> x1, matrix products: 4.08 us -> 0.15 us  [partial_softmax(): jnp.einsum('rjhd,rphd->rhjp', query_heads, key_heads, preferred_element_t...]
    convert_element_type x1 -> x3, other arithmetic: 0.1 us -> 2.65 us  [the longest x1 1.33 us: per_device(): usable.astype(jnp.int32)[:, None, :]]
    pallas_call x0 -> x2, other arithmetic: none -> 1.97 us  [attention(): pl.pallas_call(functools.partial(attention_kernel, fresh is not None), ou...]
    reshape x2, local copies, waits for them, and re-layouts: 0.16 us -> 2.01 us  [the longest x1 1.29 us: per_device(): long_sum.reshape(long_count, heads, token_count, heads, HEAD_DIM) * diagonal]
where the time goes in v4:
time: 86.3 us; the launch traced here: 85.3 us
  Pallas kernels  51.9 us (60%)
  local copies, waits for them, and re-layouts  22 us (25%)
  other arithmetic  8.92 us (10%)
  matrix products  1.72 us (2%)
    pallas_call x1, Pallas kernels, seq_allreduce(): pl.pallas_call(functools.partial(butterfly_kernel, rounds), out_shape=jax...  34.1 us
    unnamed x4, local copies, waits for them, and re-layouts  12 us
    pallas_call x2, Pallas kernels, attention(): pl.pallas_call(functools.partial(attention_kernel, fresh is not None), ou...  9.74 us
    pallas_call x1, Pallas kernels, tp_reduce_scatter(): pl.pallas_call(functools.partial(scatter_kernel, parts), out_shape=jax.Sh...  8.06 us
    pallas_call x2, other arithmetic, attention(): pl.pallas_call(functools.partial(attention_kernel, fresh is not None), ou...  1.97 us

profile of v4, /device:TPU:4, one launch (start us, length us, event | category | flops | bytes accessed | tf_op | source)
XLA Modules:
  0.0 85.3 jit_solution(9018144558139434891)
XLA Ops:
  0.6 0.0 copy-start
  0.7 0.8 broadcast_compare_fusion
  1.5 0.1 broadcast_bitcast_fusion
  1.6 0.1 pad.5.clone
  1.7 1.3 %fusion.13.mask_ref = s32[4,1,256]{2,1,0:T(1,128)} fusion(pred[4,1,256]{2,0,1:T(4,128)(4,1)S(1)} %broadcast_bitcast_fusion, s32[256]{0:T(256)S(1)} %iota_add_fusion, s32[4]{0:T(128)} %param.17), kind=kLoop, calls=%fused_computation.23 | loop fusion | flops 3072 | bytes 6160 | tf_op jit(solution)/shard_map/convert_element_type | solution.py:323
  3.0 1.3 %compare_convert_fusion.mask_ref = s32[2,1,1024]{2,1,0:T(1,128)} fusion(s32[2]{0:T(128)} %param.13), kind=kLoop, calls=%fused_computation.16 | loop fusion | flops 4096 | bytes 8200 | tf_op jit(solution)/shard_map/convert_element_type | solution.py:316
  4.3 0.8 fusion.22
  5.1 0.1 reshape_squeeze.14
  5.2 0.1 reshape_squeeze.13
  5.3 0.8 reshape.180
  6.1 0.2 fusion.5
  6.3 0.2 copy.78
  6.5 0.1 fusion.12
  6.6 0.1 fusion.14
  6.7 0.2 copy.82
  6.9 4.3 %copy.70.k_ref.v_ref = bf16[2,4,256,576]{3,2,1,0:T(8,128)(2,1)} copy(bf16[2,4,256,576]{2,3,1,0:T(8,128)(2,1)} %param.15) | data formatting | bytes 4718592 | tf_op args[5]
  11.3 4.7 %shard_map.114 = (f32[4,36,576]{2,1,0:T(8,128)}, f32[4,36,1]{2,1,0:T(8,128)}, f32[4,36,1]{2,1,0:T(8,128)}) custom-call(bf16[4,4,576]{2,1,0:T(4,128)(2,1)} %q_ref.3, bf16[2,4,256,576]{3,2,1,0:T(8,128)(2,1)} %copy.70.k_ref.v_ref, bf16[2,4,256,576]{3,2,1,0:T(8,128)(2,1)} %copy.70.k_ref.v_ref, s32[4,1,256]{2,1,0:T(1,128)} %fusion.13.mask_ref), custom_call_target="tpu_custom_call" | custom-call | flops 84934656 | bytes 2359296 | tf_op jit(solution)/shard_map/pallas_call | solution.py:285
  16.0 1.1 %copy.72 = f32[4,36,576]{2,0,1:T(4,128)S(1)} copy(f32[4,36,576]{2,1,0:T(8,128)} %get-tuple-element.5) | data formatting | bytes 663552 | tf_op jit(solution)/shard_map/pallas_call | solution.py:285
  17.1 1.0 %reduce = f32[4,36]{1,0:T(4,128)S(1)} reduce(f32[4,36,1]{2,1,0:T(8,128)} %get-tuple-element.6, f32[]{:T(128)} %constant.24), dimensions={2}, to_apply=%get-tuple-element.6.reduce_sub_computation | reduce | bytes 1156 | tf_op jit(solution)/shard_map/pallas_call | solution.py:285
  18.0 1.0 %reduce.1 = f32[4,36]{1,0:T(4,128)S(1)} reduce(f32[4,36,1]{2,1,0:T(8,128)} %get-tuple-element.7, f32[]{:T(128)} %constant.24), dimensions={2}, to_apply=%get-tuple-element.7.reduce_sub_computation | reduce | bytes 1156 | tf_op jit(solution)/shard_map/pallas_call | solution.py:285
  19.0 0.1 reshape_reshape.13
  19.2 0.1 reshape_reshape.12
  19.3 1.3 %reshape.177 = f32[4,9,4,9,64]{4,3,0,2,1:T(8,128)} reshape(f32[4,36,576]{2,0,1:T(4,128)S(1)} %copy.72) | data formatting | bytes 663552 | tf_op jit(solution)/shard_map/reshape | solution.py:332
  20.6 1.6 %multiply_reduce_fusion = f32[4,9,4,64]{3,0,2,1:T(4,128)S(1)} fusion(f32[4,9,4,9,64]{4,3,0,2,1:T(8,128)} %reshape.177, f32[9,9]{1,0:T(8,128)S(1)} %fusion.18), kind=kLoop, calls=%fused_computation | loop fusion | flops 156672 | bytes 368964 | tf_op jit(solution)/shard_map/reduce_sum | solution.py:331
  22.2 0.7 maximum_maximum_fusion.x_ref
  23.0 34.1 %shard_map.115 = f32[144,128]{1,0:T(8,128)} custom-call(f32[144,128]{1,0:T(8,128)} %maximum_maximum_fusion.x_ref), custom_call_target="tpu_custom_call" | custom-call | flops 884736 | bytes 884736 | tf_op jit(solution)/shard_map/pallas_call | solution.py:114
  57.1 1.2 %slice_reduce_fusion = (f32[144]{0:T(256)S(1)}, f32[144]{0:T(256)S(1)}) fusion(f32[144,128]{1,0:T(8,128)} %shard_map.115), kind=kLoop, calls=%fused_computation.8 | loop fusion | bytes 2304 | tf_op jit(solution)/shard_map/slice | solution.py:351
  58.3 0.1 reshape_squeeze.15
  58.4 0.1 copy.85
  58.5 0.1 reshape_squeeze.12
  58.6 0.1 copy.80
  58.7 0.1 copy.81
  58.9 0.1 copy.84
  59.0 0.1 copy.86
  59.1 1.1 %fusion.3 = bf16[4,4,9,64]{3,1,2,0:T(4,128)(2,1)S(1)} fusion(bf16[4,9,4,4]{3,2,1,0:T(4,128)(2,1)S(1)} %copy.82, f32[4,9,4,64]{3,2,1,0:T(4,128)} %bitcast.22, bf16[4,4,9,64]{3,2,1,0:T(8,128)(2,1)S(1)} %reshape_squeeze.14, f32[4,9,4]{2,1,0:T(8,128)S(1)} %copy.86, f32[4,9,4]{2,1,0:T(8,128)S(1)} %copy.84, f32[4,9,4]{2,1,0:T(8,128)S(1)} %copy.81), kind=kOutput, calls=%fused_computation.5 | convolution fusion | flops 119808 | bytes 76608 | tf_op jit(solution)/shard_map/rhjp,rphd->rhjd/dot_general | solution.py:31
  60.2 0.1 reshape_reshape.11
  60.3 7.7 %copy.66.k_ref.v_ref = bf16[2,2,1024,576]{3,2,1,0:T(8,128)(2,1)} copy(bf16[2,2,1024,576]{2,3,1,0:T(8,128)(2,1)} %param.11) | data formatting | bytes 9437184 | tf_op args[1]
  68.0 5.0 %shard_map.113 = bf16[2,4,576]{2,1,0:T(4,128)(2,1)} custom-call(bf16[2,4,576]{2,1,0:T(4,128)(2,1)} %q_ref.2, bf16[2,2,1024,576]{3,2,1,0:T(8,128)(2,1)} %copy.66.k_ref.v_ref, bf16[2,2,1024,576]{3,2,1,0:T(8,128)(2,1)} %copy.66.k_ref.v_ref, s32[2,1,1024]{2,1,0:T(1,128)} %compare_convert_fusion.mask_ref, bf16[2,2,4,576]{3,2,1,0:T(4,128)(2,1)} %rest_1_.1, ...), custom_call_target="tpu_custom_call" | custom-call | flops 169869312 | bytes 4718592 | tf_op jit(solution)/shard_map/pallas_call | solution.py:285
  73.1 0.7 reshape.176
  73.8 0.0 copy-done
  73.8 0.5 fusion.8
  74.3 0.2 reshape.181
  74.5 0.7 copy.99
  75.2 8.1 %shard_map.116 = f32[24,576]{1,0:T(8,128)} custom-call(f32[4,24,576]{2,1,0:T(8,128)} %bitcast.21), custom_call_target="tpu_custom_call" | custom-call | flops 55296 | bytes 663552 | tf_op jit(solution)/shard_map/pallas_call | solution.py:178
  83.2 0.8 convert_element_type.41
  84.1 0.6 reshape.183
  84.7 0.6 reshape.182
  (9 shorter events, 0.1 us)
Async XLA Ops:
  0.6 73.1 %copy-start = (bf16[576,2304]{1,0:T(8,128)(2,1)S(1)}, bf16[576,2304]{1,0:T(8,128)(2,1)}, u32[]{:S(2)}) copy-start(bf16[576,2304]{1,0:T(8,128)(2,1)} %param.19) | copy-start | bytes 7962628

commit v5 on v4

--- a/solution.py
+++ b/solution.py
@@ -195,9 +195,17 @@
     )(blocks)
 
 
-def attention_kernel(with_fresh, q_ref, k_ref, v_ref, mask_ref, *rest):
+def attention_kernel(with_fresh, len_ref, live_ref, off_ref, q_ref, k_ref, v_ref, *rest):
     tokens, width = q_ref.shape[1], q_ref.shape[2]
+    positions = k_ref.shape[3]
     rows = (width // HEAD_DIM) * tokens
+    request = pl.program_id(0)
+    spot = lax.broadcasted_iota(jnp.int32, (1, positions), 1)
+    blocks = live_ref.shape[1]
+    alive = spot < 0
+    for b in range(blocks):
+        alive = alive | ((spot // (positions // blocks) == b) & (live_ref[request, b] == 1))
+    usable = alive & (spot + off_ref[0] < len_ref[request])
     pick = (
         lax.broadcasted_iota(jnp.int32, (rows, tokens), 0) % tokens
         == lax.broadcasted_iota(jnp.int32, (rows, tokens), 1)
@@ -210,10 +218,7 @@
     query = jnp.where(head_lanes, spread, 0.0).astype(jnp.bfloat16)
     contract = (((1,), (1,)), ((), ()))
     scale = 1.0 / math.sqrt(HEAD_DIM)
-    scores = lax.dot_general(
-        query, k_ref[0, 0], contract, preferred_element_type=jnp.float32
-    ) * scale
-    usable = mask_ref[0] != 0
+    scores = jnp.dot(query, k_ref[0, 0], preferred_element_type=jnp.float32) * scale
     scores = jnp.where(usable, scores, NEGATIVE)
     highest = jnp.max(scores, axis=1, keepdims=True)
     if with_fresh:
@@ -228,8 +233,8 @@
         highest = jnp.maximum(highest, jnp.max(fresh_scores, axis=1, keepdims=True))
     expo = jnp.where(usable, jnp.exp(scores - highest), 0.0)
     totals = jnp.sum(expo, axis=1, keepdims=True)
-    summed = jnp.dot(
-        expo.astype(jnp.bfloat16), v_ref[0, 0], preferred_element_type=jnp.float32
+    summed = lax.dot_general(
+        expo.astype(jnp.bfloat16), v_ref[0, 0], contract, preferred_element_type=jnp.float32
     )
     if with_fresh:
         fresh_expo = jnp.where(causal, jnp.exp(fresh_scores - highest), 0.0)
@@ -252,25 +257,25 @@
         total_ref[0] = totals
 
 
-def attention(queries, cache, mask, fresh=None):
+def attention(queries, cache, lengths, live, offset, fresh=None):
     count, tokens, width = queries.shape
     positions = cache.shape[2]
     rows = (width // HEAD_DIM) * tokens
+    flipped = jnp.swapaxes(cache, 2, 3)
     specs = [
-        pl.BlockSpec((1, tokens, width), lambda r: (r, 0, 0)),
-        pl.BlockSpec((1, 1, positions, width), lambda r: (0, r, 0, 0)),
-        pl.BlockSpec((1, 1, positions, width), lambda r: (1, r, 0, 0)),
-        pl.BlockSpec((1, 1, positions), lambda r: (r, 0, 0)),
+        pl.BlockSpec((1, tokens, width), lambda r, *_: (r, 0, 0)),
+        pl.BlockSpec((1, 1, width, positions), lambda r, *_: (0, r, 0, 0)),
+        pl.BlockSpec((1, 1, width, positions), lambda r, *_: (1, r, 0, 0)),
     ]
-    operands = [queries, cache, cache, mask]
+    operands = [lengths, live, offset, queries, flipped, flipped]
     if fresh is not None:
         specs += [
-            pl.BlockSpec((1, 1, tokens, width), lambda r: (0, r, 0, 0)),
-            pl.BlockSpec((1, 1, tokens, width), lambda r: (1, r, 0, 0)),
+            pl.BlockSpec((1, 1, tokens, width), lambda r, *_: (0, r, 0, 0)),
+            pl.BlockSpec((1, 1, tokens, width), lambda r, *_: (1, r, 0, 0)),
         ]
         operands += [fresh, fresh]
         out_shape = jax.ShapeDtypeStruct((count, tokens, width), jnp.bfloat16)
-        out_specs = pl.BlockSpec((1, tokens, width), lambda r: (r, 0, 0))
+        out_specs = pl.BlockSpec((1, tokens, width), lambda r, *_: (r, 0, 0))
     else:
         out_shape = (
             jax.ShapeDtypeStruct((count, rows, width), jnp.float32),
@@ -278,16 +283,16 @@
             jax.ShapeDtypeStruct((count, rows, 1), jnp.float32),
         )
         out_specs = (
-            pl.BlockSpec((1, rows, width), lambda r: (r, 0, 0)),
-            pl.BlockSpec((1, rows, 1), lambda r: (r, 0, 0)),
-            pl.BlockSpec((1, rows, 1), lambda r: (r, 0, 0)),
+            pl.BlockSpec((1, rows, width), lambda r, *_: (r, 0, 0)),
+            pl.BlockSpec((1, rows, 1), lambda r, *_: (r, 0, 0)),
+            pl.BlockSpec((1, rows, 1), lambda r, *_: (r, 0, 0)),
         )
     return pl.pallas_call(
         functools.partial(attention_kernel, fresh is not None),
         out_shape=out_shape,
-        grid=(count,),
-        in_specs=specs,
-        out_specs=out_specs,
+        grid_spec=pltpu.PrefetchScalarGridSpec(
+            num_scalar_prefetch=3, grid=(count,), in_specs=specs, out_specs=out_specs
+        ),
         cost_estimate=pl.CostEstimate(
             flops=4 * count * rows * positions * width,
             transcendentals=count * rows * positions,
@@ -310,17 +315,21 @@
 ):
     request_count = queries_short.shape[0]
     token_count = queries_short.shape[1]
-    positions = cache_short.shape[2]
-    usable = jnp.arange(positions, dtype=jnp.int32)[None, :] < short_len[:, None]
     short_att = attention(
-        queries_short, cache_short, usable.astype(jnp.int32)[:, None, :], fresh_short
+        queries_short,
+        cache_short,
+        short_len,
+        jnp.ones((request_count, 1), jnp.int32),
+        jnp.zeros((1,), jnp.int32),
+        fresh_short,
     )
     local_len = cache_long.shape[2]
-    spots = lax.axis_index("seq") * local_len + jnp.arange(local_len, dtype=jnp.int32)
-    live = jnp.repeat(block_live, local_len // block_live.shape[1], axis=1) == 1
-    long_usable = (spots[None, :] < long_len[:, None]) & live
     long_sum, long_top, long_total = attention(
-        queries_long, cache_long, long_usable.astype(jnp.int32)[:, None, :]
+        queries_long,
+        cache_long,
+        long_len,
+        block_live,
+        (lax.axis_index("seq") * local_len).astype(jnp.int32).reshape(1),
     )
     long_count = queries_long.shape[0]
     heads = queries_long.shape[2] // HEAD_DIM

time: 86.3 us -> 70.1 us (0.81)
  local copies, waits for them, and re-layouts: 22 us -> 10.5 us
  other arithmetic: 8.92 us -> 3.66 us
  Pallas kernels: 51.9 us -> 52.8 us
    unnamed x4 -> x11, local copies, waits for them, and re-layouts: 12 us -> 1.52 us
    convert_element_type x2 -> x0, other arithmetic: 2.65 us -> none  [the longest x1 1.33 us: per_device(): usable.astype(jnp.int32)[:, None, :]]
    pallas_call x2, other arithmetic: 1.97 us -> 0.19 us  [attention(): pl.pallas_call(functools.partial(attention_kernel, fresh is not None), ou...]
    pallas_call x2, Pallas kernels: 9.74 us -> 10.7 us  [attention(): pl.pallas_call(functools.partial(attention_kernel, fresh is not None), ou...]
where the time goes in v5:
time: 70.1 us; the launch traced here: 69.6 us
  Pallas kernels  52.8 us (75%)
  local copies, waits for them, and re-layouts  10.5 us (15%)
  other arithmetic  3.66 us (5%)
  matrix products  1.73 us (2%)
  between operations  0.83 us (1%)
    pallas_call x1, Pallas kernels, seq_allreduce(): pl.pallas_call(functools.partial(butterfly_kernel, rounds), out_shape=jax...  34.1 us
    pallas_call x2, Pallas kernels, attention(): pl.pallas_call(functools.partial(attention_kernel, fresh is not None), ou...  10.7 us
    pallas_call x1, Pallas kernels, tp_reduce_scatter(): pl.pallas_call(functools.partial(scatter_kernel, parts), out_shape=jax.Sh...  8.06 us
    reduce_sum x1, other arithmetic, per_device(): jnp.sum(long_sum.reshape(long_count, heads, token_count, heads, HEAD_DIM)...  1.64 us
    unnamed x11, local copies, waits for them, and re-layouts  1.52 us

profile of v5, /device:TPU:4, one launch (start us, length us, event | category | flops | bytes accessed | tf_op | source)
XLA Modules:
  0.0 69.6 jit_solution(749077053927823559)
XLA Ops:
  0.6 0.0 copy-start
  0.7 1.5 %copy.49.live_ref = s32[4,2]{1,0:T(4,128)} copy(s32[4,2]{0,1:T(2,128)} %param.18) | data formatting | bytes 64 | tf_op args[8]
  2.1 5.3 %shard_map.114 = (f32[4,36,576]{2,1,0:T(8,128)}, f32[4,36,1]{2,1,0:T(8,128)}, f32[4,36,1]{2,1,0:T(8,128)}) custom-call(s32[4]{0:T(128)} %len_ref.3, s32[4,2]{1,0:T(4,128)} %copy.49.live_ref, s32[1]{0:T(128)} %bitcast.1.off_ref, bf16[4,4,576]{2,1,0:T(4,128)(2,1)} %q_ref.3, bf16[2,4,576,256]{3,2,1,0:T(8,128)(2,1)} %bitcast.24, bf16[2,4,576,256]{3,2,1,0:T(8,128)(2,1)} %bitcast.25), custom_call_target="tpu_custom_call" | custom-call | flops 84934656 | bytes 2359296 | tf_op jit(solution)/shard_map/pallas_call | solution.py:290
  7.5 0.0 copy-start.4
  7.5 0.0 copy-start.3
  7.5 1.1 %copy.50 = f32[4,36,576]{2,0,1:T(4,128)S(1)} copy(f32[4,36,576]{2,1,0:T(8,128)} %get-tuple-element.5) | data formatting | bytes 663552 | tf_op jit(solution)/shard_map/pallas_call | solution.py:290
  8.6 1.3 %reshape.89 = f32[4,9,4,9,64]{4,3,0,2,1:T(8,128)} reshape(f32[4,36,576]{2,0,1:T(4,128)S(1)} %copy.50) | data formatting | bytes 663552 | tf_op jit(solution)/shard_map/reshape | solution.py:341
  9.9 1.6 %multiply_reduce_fusion = f32[4,9,4,64]{3,0,2,1:T(4,128)S(1)} fusion(f32[4,9,4,9,64]{4,3,0,2,1:T(8,128)} %reshape.89, f32[9,9]{1,0:T(8,128)S(1)} %fusion.17), kind=kLoop, calls=%fused_computation | loop fusion | flops 156672 | bytes 368964 | tf_op jit(solution)/shard_map/reduce_sum | solution.py:340
  11.6 0.0 copy-done.2
  11.6 0.1 reduce
  11.7 0.1 reshape_reshape.12
  11.8 0.0 copy-done.1
  11.9 0.1 reduce.1
  12.0 0.1 reshape_reshape.13
  12.1 0.1 pad.5.clone
  12.2 0.7 %maximum_maximum_fusion.x_ref = f32[144,128]{1,0:T(8,128)} fusion(f32[144,1]{1,0:T(8,128)S(1)} %reshape_reshape.13, f32[144,1]{1,0:T(8,128)S(1)} %reshape_reshape.12, f32[144,64]{1,0:T(8,128)S(1)} %bitcast.28, f32[128]{0:T(128)S(1)} %pad.5.clone), kind=kLoop, calls=%fused_computation.7 | loop fusion | flops 55296 | bytes 112256 | tf_op jit(solution)/shard_map/concatenate | solution.py:348
  12.9 34.1 %shard_map.115 = f32[144,128]{1,0:T(8,128)} custom-call(f32[144,128]{1,0:T(8,128)} %maximum_maximum_fusion.x_ref), custom_call_target="tpu_custom_call" | custom-call | flops 884736 | bytes 884736 | tf_op jit(solution)/shard_map/pallas_call | solution.py:114
  47.0 1.2 %slice_reduce_fusion = (f32[144]{0:T(256)S(1)}, f32[144]{0:T(256)S(1)}) fusion(f32[144,128]{1,0:T(8,128)} %shard_map.115), kind=kLoop, calls=%fused_computation.8 | loop fusion | bytes 2304 | tf_op jit(solution)/shard_map/slice | solution.py:360
  48.2 0.1 reshape_squeeze.15
  48.3 0.1 copy.63
  48.4 0.1 reshape_squeeze.12
  48.5 0.1 copy.58
  48.6 0.0 copy-done.4
  48.7 0.1 reshape_squeeze.13
  48.8 0.0 copy-done.3
  48.8 0.1 reshape.92
  48.9 0.2 fusion.5
  49.0 0.2 copy.56
  49.3 0.1 fusion.12
  49.4 0.1 fusion.13
  49.5 0.1 copy.59
  49.6 0.1 copy.62
  49.7 0.1 copy.64
  49.8 0.2 copy.60
  50.1 0.1 reshape_squeeze.14
  50.2 1.1 %fusion.3 = bf16[4,4,9,64]{3,1,2,0:T(4,128)(2,1)S(1)} fusion(bf16[4,9,4,4]{3,2,1,0:T(4,128)(2,1)S(1)} %copy.60, f32[4,9,4,64]{3,2,1,0:T(4,128)} %bitcast.27, bf16[4,4,9,64]{3,2,1,0:T(8,128)(2,1)S(1)} %reshape_squeeze.14, f32[4,9,4]{2,1,0:T(8,128)S(1)} %copy.64, f32[4,9,4]{2,1,0:T(8,128)S(1)} %copy.62, f32[4,9,4]{2,1,0:T(8,128)S(1)} %copy.59), kind=kOutput, calls=%fused_computation.5 | convolution fusion | flops 119808 | bytes 76608 | tf_op jit(solution)/shard_map/rhjp,rphd->rhjd/dot_general | solution.py:31
  51.3 0.1 reshape_reshape.11
  51.4 0.6 broadcast_1_live_ref.2.live_ref
  52.0 5.3 %shard_map.113 = bf16[2,4,576]{2,1,0:T(4,128)(2,1)} custom-call(s32[2]{0:T(128)} %len_ref.2, s32[2,1]{1,0:T(2,128)} %broadcast_1_live_ref.2.live_ref, s32[1]{0:T(128)} %constant.2.clone.1.off_ref, bf16[2,4,576]{2,1,0:T(4,128)(2,1)} %q_ref.2, bf16[2,2,576,1024]{3,2,1,0:T(8,128)(2,1)} %bitcast.22, bf16[2,2,576,1024]{3,2,1,0:T(8,128)(2,1)} %bitcast.23, ...), custom_call_target="tpu_custom_call" | custom-call | flops 169869312 | bytes 4718592 | tf_op jit(solution)/shard_map/pallas_call | solution.py:290
  57.3 0.7 %reshape.87 = bf16[8,576]{1,0:T(8,128)(2,1)S(1)} reshape(bf16[2,4,576]{2,1,0:T(4,128)(2,1)} %shard_map.113) | data formatting | bytes 18432 | tf_op jit(solution)/shard_map/reshape | solution.py:364
  58.0 0.0 copy-done
  58.0 0.5 fusion.8
  58.5 0.2 reshape.93
  58.7 0.7 %copy.74 = f32[24,4,576]{2,0,1:T(8,128)} copy(f32[24,4,576]{2,1,0:T(4,128)S(1)} %reshape.93) | data formatting | bytes 442368 | tf_op jit(solution)/shard_map/reshape | solution.py:177
  59.4 8.1 %shard_map.116 = f32[24,576]{1,0:T(8,128)} custom-call(f32[4,24,576]{2,1,0:T(8,128)} %bitcast.26), custom_call_target="tpu_custom_call" | custom-call | flops 55296 | bytes 663552 | tf_op jit(solution)/shard_map/pallas_call | solution.py:178
  67.5 0.8 %convert_element_type.19 = bf16[24,576]{1,0:T(8,128)(2,1)S(1)} convert(f32[24,576]{1,0:T(8,128)} %shard_map.116) | non-fusion elementwise | flops 13824 | bytes 82944 | tf_op jit(solution)/shard_map/convert_element_type | solution.py:367
  68.3 0.6 reshape.95
  68.9 0.6 reshape.94
  (11 shorter events, 0.1 us)
Async XLA Ops:
  0.6 57.4 %copy-start = (bf16[576,2304]{1,0:T(8,128)(2,1)S(1)}, bf16[576,2304]{1,0:T(8,128)(2,1)}, u32[]{:S(2)}) copy-start(bf16[576,2304]{1,0:T(8,128)(2,1)} %param.19) | copy-start | bytes 7962628
  7.5 4.2 %copy-start.2 = (f32[4,36,1]{2,1,0:T(8,128)S(1)}, f32[4,36,1]{2,1,0:T(8,128)}, u32[]{:S(2)}) copy-start(f32[4,36,1]{2,1,0:T(8,128)} %get-tuple-element.6) | copy-start | bytes 1732
  7.5 4.4 %copy-start.1 = (f32[4,36,1]{2,1,0:T(8,128)S(1)}, f32[4,36,1]{2,1,0:T(8,128)}, u32[]{:S(2)}) copy-start(f32[4,36,1]{2,1,0:T(8,128)} %get-tuple-element.7) | copy-start | bytes 1732
  7.5 41.2 %copy-start.4 = (bf16[2,4,4,576]{3,2,1,0:T(4,128)(2,1)S(1)}, bf16[2,4,4,576]{3,2,1,0:T(4,128)(2,1)}, u32[]{:S(2)}) copy-start(bf16[2,4,4,576]{3,2,1,0:T(4,128)(2,1)} %param.16) | copy-start | bytes 110596
  7.5 41.3 %copy-start.3 = (bf16[4,4,576]{2,1,0:T(4,128)(2,1)S(1)}, bf16[4,4,576]{2,1,0:T(4,128)(2,1)}, u32[]{:S(2)}) copy-start(bf16[4,4,576]{2,1,0:T(4,128)(2,1)} %q_ref.3) | copy-start | bytes 55300

commit v6 on v5

--- a/solution.py
+++ b/solution.py
@@ -61,9 +61,9 @@
 
 
 def merge_states(low, high):
-    lane = lax.broadcasted_iota(jnp.int32, low.shape, 1)
-    top_low = low[:, HEAD_DIM : HEAD_DIM + 1]
-    top_high = high[:, HEAD_DIM : HEAD_DIM + 1]
+    lane = lax.broadcasted_iota(jnp.int32, low.shape, low.ndim - 1)
+    top_low = low[..., HEAD_DIM : HEAD_DIM + 1]
+    top_high = high[..., HEAD_DIM : HEAD_DIM + 1]
     top = jnp.maximum(top_low, top_high)
     mixed = low * jnp.exp(top_low - top) + high * jnp.exp(top_high - top)
     return jnp.where(lane == HEAD_DIM, top, mixed)
@@ -110,15 +110,15 @@
 
 def seq_allreduce(packed, devices):
     rounds = devices.bit_length() - 1
-    rows = packed.shape[0]
+    rows = packed.size // LANES
     return pl.pallas_call(
         functools.partial(butterfly_kernel, rounds),
         out_shape=jax.ShapeDtypeStruct(packed.shape, jnp.float32),
         in_specs=[pl.BlockSpec(memory_space=pltpu.VMEM)],
         out_specs=pl.BlockSpec(memory_space=pltpu.VMEM),
         scratch_shapes=[
-            pltpu.VMEM((max(rounds - 1, 1), rows, LANES), jnp.float32),
-            pltpu.VMEM((rounds, rows, LANES), jnp.float32),
+            pltpu.VMEM((max(rounds - 1, 1),) + packed.shape, jnp.float32),
+            pltpu.VMEM((rounds,) + packed.shape, jnp.float32),
             pltpu.SemaphoreType.DMA((rounds,)),
             pltpu.SemaphoreType.DMA((rounds,)),
         ],
@@ -201,11 +201,15 @@
     rows = (width // HEAD_DIM) * tokens
     request = pl.program_id(0)
     spot = lax.broadcasted_iota(jnp.int32, (1, positions), 1)
-    blocks = live_ref.shape[1]
-    alive = spot < 0
-    for b in range(blocks):
-        alive = alive | ((spot // (positions // blocks) == b) & (live_ref[request, b] == 1))
-    usable = alive & (spot + off_ref[0] < len_ref[request])
+    usable = spot + off_ref[0] < len_ref[request]
+    if not with_fresh:
+        blocks = live_ref.shape[0]
+        alive = spot < 0
+        for b in range(blocks):
+            alive = alive | (
+                (spot // (positions // blocks) == b) & (live_ref[b, request] == 1)
+            )
+        usable = usable & alive
     pick = (
         lax.broadcasted_iota(jnp.int32, (rows, tokens), 0) % tokens
         == lax.broadcasted_iota(jnp.int32, (rows, tokens), 1)
@@ -251,10 +255,20 @@
             gather, normed.astype(jnp.bfloat16), preferred_element_type=jnp.float32
         ).astype(o_ref.dtype)
     else:
-        sum_ref, top_ref, total_ref = rest
-        sum_ref[0] = summed
-        top_ref[0] = highest
-        total_ref[0] = totals
+        (out_ref,) = rest
+        masked = jnp.where(head_lanes, summed, 0.0)
+        folded = masked[:, 0:HEAD_DIM]
+        for g in range(1, width // HEAD_DIM):
+            folded = folded + masked[:, g * HEAD_DIM : (g + 1) * HEAD_DIM]
+        out_ref[0] = jnp.concatenate(
+            [
+                folded,
+                highest,
+                totals,
+                jnp.zeros((rows, LANES - HEAD_DIM - 2), jnp.float32),
+            ],
+            axis=1,
+        )
 
 
 def attention(queries, cache, lengths, live, offset, fresh=None):
@@ -277,16 +291,8 @@
         out_shape = jax.ShapeDtypeStruct((count, tokens, width), jnp.bfloat16)
         out_specs = pl.BlockSpec((1, tokens, width), lambda r, *_: (r, 0, 0))
     else:
-        out_shape = (
-            jax.ShapeDtypeStruct((count, rows, width), jnp.float32),
-            jax.ShapeDtypeStruct((count, rows, 1), jnp.float32),
-            jax.ShapeDtypeStruct((count, rows, 1), jnp.float32),
-        )
-        out_specs = (
-            pl.BlockSpec((1, rows, width), lambda r, *_: (r, 0, 0)),
-            pl.BlockSpec((1, rows, 1), lambda r, *_: (r, 0, 0)),
-            pl.BlockSpec((1, rows, 1), lambda r, *_: (r, 0, 0)),
-        )
+        out_shape = jax.ShapeDtypeStruct((count, rows, LANES), jnp.float32)
+        out_specs = pl.BlockSpec((1, rows, LANES), lambda r, *_: (r, 0, 0))
     return pl.pallas_call(
         functools.partial(attention_kernel, fresh is not None),
         out_shape=out_shape,
@@ -319,46 +325,25 @@
         queries_short,
         cache_short,
         short_len,
-        jnp.ones((request_count, 1), jnp.int32),
+        jnp.zeros((1, 1), jnp.int32),
         jnp.zeros((1,), jnp.int32),
         fresh_short,
     )
     local_len = cache_long.shape[2]
-    long_sum, long_top, long_total = attention(
+    packed = attention(
         queries_long,
         cache_long,
         long_len,
-        block_live,
+        block_live.T,
         (lax.axis_index("seq") * local_len).astype(jnp.int32).reshape(1),
     )
-    long_count = queries_long.shape[0]
     heads = queries_long.shape[2] // HEAD_DIM
-    diagonal = jnp.eye(heads, dtype=jnp.float32)[None, :, None, :, None]
-    long_parts = (
-        long_top.reshape(long_count, heads, token_count),
-        long_total.reshape(long_count, heads, token_count),
-        jnp.sum(
-            long_sum.reshape(long_count, heads, token_count, heads, HEAD_DIM) * diagonal,
-            axis=3,
-        ),
-    )
-    highest_long, totals_long, summed_long = long_parts
-    shape = highest_long.shape
-    rows = highest_long.size
-    packed = jnp.concatenate(
-        [
-            summed_long.reshape(rows, HEAD_DIM),
-            highest_long.reshape(rows, 1),
-            totals_long.reshape(rows, 1),
-            jnp.zeros((rows, LANES - HEAD_DIM - 2), jnp.float32),
-        ],
-        axis=1,
-    )
+    shape = (queries_long.shape[0], heads, token_count)
     reduced = seq_allreduce(packed, lax.axis_size("seq"))
     merged = (
-        reduced[:, HEAD_DIM].reshape(shape),
-        reduced[:, HEAD_DIM + 1].reshape(shape),
-        reduced[:, :HEAD_DIM].reshape(shape + (HEAD_DIM,)),
+        reduced[..., HEAD_DIM].reshape(shape),
+        reduced[..., HEAD_DIM + 1].reshape(shape),
+        reduced[..., :HEAD_DIM].reshape(shape + (HEAD_DIM,)),
     )
     long_att = finish(combine_parts(merged, fresh_part(queries_long, fresh_long)))
     short_rows = short_att.reshape(-1, short_att.shape[2])

time: 70.1 us -> 62.7 us (0.89)
  local copies, waits for them, and re-layouts: 10.5 us -> 6.52 us
  other arithmetic: 3.66 us -> 1.09 us
  matrix products: 1.73 us -> 0.85 us
    reduce_sum x1 -> x0, other arithmetic: 1.64 us -> none  [per_device(): jnp.sum(long_sum.reshape(long_count, heads, token_count, heads, HEAD_DIM)...]
    unnamed x11 -> x6, local copies, waits for them, and re-layouts: 1.52 us -> 0.02 us
    reshape x1 -> x0, local copies, waits for them, and re-layouts: 1.29 us -> none  [per_device(): long_sum.reshape(long_count, heads, token_count, heads, HEAD_DIM) * diagonal]
    pallas_call x1 -> x0, local copies, waits for them, and re-layouts: 1.14 us -> none  [attention(): pl.pallas_call(functools.partial(attention_kernel, fresh is not None), ou...]
    dot_general x1, matrix products: 1.09 us -> 0.21 us  [partial_softmax(): jnp.einsum('rhjp,rphd->rhjd', expo.astype(jnp.bfloat16), value_heads, pre...]
    slice x1 -> x2, local copies, waits for them, and re-layouts: 1.19 us -> 2.06 us  [the longest x1 1.16 us: per_device(): reduced[..., HEAD_DIM + 1].reshape(shape)]
    another operation x7 -> x4, local copies, waits for them, and re-layouts: 1.21 us -> 0.38 us  [the longest x2 0.19 us: per_device(): reduced[..., HEAD_DIM + 1].reshape(shape)]
    concatenate x1 -> x0, other arithmetic: 0.73 us -> none  [per_device(): jnp.concatenate([summed_long.reshape(rows, HEAD_DIM), highest_long.reshap...]
where the time goes in v6:
time: 62.7 us; the launch traced here: 62.3 us
  Pallas kernels  53.1 us (85%)
  local copies, waits for them, and re-layouts  6.52 us (10%)
  other arithmetic  1.09 us (2%)
  matrix products  0.85 us (1%)
  between operations  0.76 us (1%)
    pallas_call x1, Pallas kernels, seq_allreduce(): pl.pallas_call(functools.partial(butterfly_kernel, rounds), out_shape=jax...  34.1 us
    pallas_call x2, Pallas kernels, attention(): pl.pallas_call(functools.partial(attention_kernel, fresh is not None), ou...  10.9 us
    pallas_call x1, Pallas kernels, tp_reduce_scatter(): pl.pallas_call(functools.partial(scatter_kernel, parts), out_shape=jax.Sh...  8.06 us

profile of v6, /device:TPU:4, one launch (start us, length us, event | category | flops | bytes accessed | tf_op | source)
XLA Modules:
  0.0 62.3 jit_solution(1640202487440771330)
XLA Ops:
  0.6 0.0 copy-start
  0.7 0.0 copy-start.2
  0.7 0.0 copy-start.1
  0.7 5.4 %shard_map.113 = bf16[2,4,576]{2,1,0:T(4,128)(2,1)} custom-call(s32[2]{0:T(128)} %len_ref.2, s32[1,1]{1,0:T(1,128)} %constant.2.clone.1.live_ref, s32[1]{0:T(128)} %constant.3.clone.1.off_ref, bf16[2,4,576]{2,1,0:T(4,128)(2,1)} %q_ref.2, bf16[2,2,576,1024]{3,2,1,0:T(8,128)(2,1)} %bitcast.20, bf16[2,2,576,1024]{3,2,1,0:T(8,128)(2,1)} %bitcast.21, ...), custom_call_target="tpu_custom_call" | custom-call | flops 169869312 | bytes 4718592 | tf_op jit(solution)/shard_map/pallas_call | solution.py:296
  6.1 0.7 %reshape.73 = bf16[8,576]{1,0:T(8,128)(2,1)S(1)} reshape(bf16[2,4,576]{2,1,0:T(4,128)(2,1)} %shard_map.113) | data formatting | bytes 18432 | tf_op jit(solution)/shard_map/reshape | solution.py:349
  6.9 0.0 copy-done.2
  6.9 0.1 reshape_squeeze.14
  7.0 0.1 reshape_squeeze.13
  7.1 0.0 copy-done.1
  7.1 0.1 reshape.76
  7.2 0.2 fusion.5
  7.4 0.2 copy.35
  7.6 0.1 fusion.12
  7.7 0.1 fusion.13
  7.8 0.2 copy.40
  8.0 5.4 %shard_map.114.x_ref = f32[4,36,128]{2,1,0:T(8,128)} custom-call(s32[4]{0:T(128)} %len_ref.3, s32[2,4]{1,0:T(2,128)} %bitcast.34, s32[1]{0:T(128)} %bitcast.2.off_ref, bf16[4,4,576]{2,1,0:T(4,128)(2,1)} %q_ref.3, bf16[2,4,576,256]{3,2,1,0:T(8,128)(2,1)} %bitcast.22, bf16[2,4,576,256]{3,2,1,0:T(8,128)(2,1)} %bitcast.23), custom_call_target="tpu_custom_call" | custom-call | flops 84934656 | bytes 2359296 | tf_op jit(solution)/shard_map/pallas_call | solution.py:296
  13.5 34.1 %shard_map.115 = f32[4,36,128]{2,1,0:T(8,128)} custom-call(f32[4,36,128]{2,1,0:T(8,128)} %shard_map.114.x_ref), custom_call_target="tpu_custom_call" | custom-call | flops 884736 | bytes 884736 | tf_op jit(solution)/shard_map/pallas_call | solution.py:114
  47.6 1.2 %slice_reduce_fusion = (f32[4,36]{1,0:T(4,128)S(1)}, f32[4,36]{1,0:T(4,128)S(1)}) fusion(f32[4,36,128]{2,1,0:T(8,128)} %shard_map.115), kind=kLoop, calls=%fused_computation.6 | loop fusion | bytes 2304 | tf_op jit(solution)/shard_map/slice | solution.py:345
  48.8 0.1 reshape_squeeze.15
  48.8 0.1 copy.43
  49.0 0.1 reshape_squeeze.12
  49.0 0.1 copy.37
  49.2 0.1 copy.38
  49.3 0.1 copy.42
  49.4 0.1 copy.44
  49.5 0.9 %copy.32 = f32[4,36,64]{2,0,1:T(4,128)S(1)} copy(f32[4,36,64]{2,1,0:T(8,128)} %bitcast.24) | data formatting | bytes 73728 | tf_op jit(solution)/shard_map/slice | solution.py:346
  50.4 0.2 fusion.3
  50.7 0.1 reshape_reshape.3
  50.8 0.0 copy-done
  50.8 0.5 fusion.8
  51.3 0.2 reshape.77
  51.5 0.7 %copy.57 = f32[24,4,576]{2,0,1:T(8,128)} copy(f32[24,4,576]{2,1,0:T(4,128)S(1)} %reshape.77) | data formatting | bytes 442368 | tf_op jit(solution)/shard_map/reshape | solution.py:177
  52.2 8.1 %shard_map.116 = f32[24,576]{1,0:T(8,128)} custom-call(f32[4,24,576]{2,1,0:T(8,128)} %bitcast.25), custom_call_target="tpu_custom_call" | custom-call | flops 55296 | bytes 663552 | tf_op jit(solution)/shard_map/pallas_call | solution.py:178
  60.2 0.8 %convert_element_type.11 = bf16[24,576]{1,0:T(8,128)(2,1)S(1)} convert(f32[24,576]{1,0:T(8,128)} %shard_map.116) | non-fusion elementwise | flops 13824 | bytes 82944 | tf_op jit(solution)/shard_map/convert_element_type | solution.py:352
  61.1 0.6 reshape.79
  61.7 0.6 reshape.78
  (6 shorter events, 0.1 us)
Async XLA Ops:
  0.6 50.1 %copy-start = (bf16[576,2304]{1,0:T(8,128)(2,1)S(1)}, bf16[576,2304]{1,0:T(8,128)(2,1)}, u32[]{:S(2)}) copy-start(bf16[576,2304]{1,0:T(8,128)(2,1)} %param.19) | copy-start | bytes 7962628
  0.7 6.2 %copy-start.2 = (bf16[2,4,4,576]{3,2,1,0:T(4,128)(2,1)S(1)}, bf16[2,4,4,576]{3,2,1,0:T(4,128)(2,1)}, u32[]{:S(2)}) copy-start(bf16[2,4,4,576]{3,2,1,0:T(4,128)(2,1)} %param.16) | copy-start | bytes 110596
  0.7 6.4 %copy-start.1 = (bf16[4,4,576]{2,1,0:T(4,128)(2,1)S(1)}, bf16[4,4,576]{2,1,0:T(4,128)(2,1)}, u32[]{:S(2)}) copy-start(bf16[4,4,576]{2,1,0:T(4,128)(2,1)} %q_ref.3) | copy-start | bytes 55300

commit v7 on v6

--- a/solution.py
+++ b/solution.py
@@ -69,9 +69,72 @@
     return jnp.where(lane == HEAD_DIM, top, mixed)
 
 
-def butterfly_kernel(rounds, x_ref, o_ref, state, recv, send_sem, recv_sem):
+def short_request(q, k_view, v_view, usable, fk, fv):
+    tokens, width = q.shape
+    rows = (width // HEAD_DIM) * tokens
+    pick = (
+        lax.broadcasted_iota(jnp.int32, (rows, tokens), 0) % tokens
+        == lax.broadcasted_iota(jnp.int32, (rows, tokens), 1)
+    ).astype(jnp.bfloat16)
+    head_lanes = (
+        lax.broadcasted_iota(jnp.int32, (rows, width), 0) // tokens
+        == lax.broadcasted_iota(jnp.int32, (rows, width), 1) // HEAD_DIM
+    )
+    spread = jnp.dot(pick, q, preferred_element_type=jnp.float32)
+    query = jnp.where(head_lanes, spread, 0.0).astype(jnp.bfloat16)
+    contract = (((1,), (1,)), ((), ()))
+    scale = 1.0 / math.sqrt(HEAD_DIM)
+    scores = jnp.dot(query, k_view[...], preferred_element_type=jnp.float32) * scale
+    scores = jnp.where(usable, scores, NEGATIVE)
+    fresh_scores = lax.dot_general(query, fk, contract, preferred_element_type=jnp.float32) * scale
+    causal = lax.broadcasted_iota(jnp.int32, (rows, tokens), 1) <= (
+        lax.broadcasted_iota(jnp.int32, (rows, tokens), 0) % tokens
+    )
+    fresh_scores = jnp.where(causal, fresh_scores, NEGATIVE)
+    highest = jnp.maximum(
+        jnp.max(scores, axis=1, keepdims=True), jnp.max(fresh_scores, axis=1, keepdims=True)
+    )
+    expo = jnp.where(usable, jnp.exp(scores - highest), 0.0)
+    fresh_expo = jnp.where(causal, jnp.exp(fresh_scores - highest), 0.0)
+    totals = jnp.sum(expo, axis=1, keepdims=True) + jnp.sum(fresh_expo, axis=1, keepdims=True)
+    summed = lax.dot_general(
+        expo.astype(jnp.bfloat16), v_view[...], contract, preferred_element_type=jnp.float32
+    ) + jnp.dot(fresh_expo.astype(jnp.bfloat16), fv, preferred_element_type=jnp.float32)
+    normed = jnp.where(head_lanes, (summed / totals).astype(jnp.bfloat16), 0.0)
+    gather = (
+        lax.broadcasted_iota(jnp.int32, (tokens, rows), 1) % tokens
+        == lax.broadcasted_iota(jnp.int32, (tokens, rows), 0)
+    ).astype(jnp.bfloat16)
+    return jnp.dot(gather, normed.astype(jnp.bfloat16), preferred_element_type=jnp.float32)
+
+
+def butterfly_kernel(
+    rounds, len_ref, x_ref, q_ref, f_ref, cache_ref, o_ref, att_ref,
+    state, recv, send_sem, recv_sem, kv_buf, kv_sem,
+):
     me = lax.axis_index("seq")
     column = lax.axis_index("tp")
+    count = q_ref.shape[0]
+    loads = []
+    for r in range(count):
+        pair = []
+        for kv in range(2):
+            load = pltpu.make_async_copy(
+                cache_ref.at[kv, r], kv_buf.at[kv, r], kv_sem.at[kv, r]
+            )
+            load.start()
+            pair.append(load)
+        loads.append(pair)
+
+    def short_step(r):
+        for load in loads[r]:
+            load.wait()
+        spot = lax.broadcasted_iota(jnp.int32, (1, kv_buf.shape[3]), 1)
+        att_ref[r] = short_request(
+            q_ref[r], kv_buf.at[0, r], kv_buf.at[1, r], spot < len_ref[r],
+            f_ref[0, r], f_ref[1, r],
+        ).astype(att_ref.dtype)
+
     partners = []
     for k in range(rounds):
         step = 1 << k
@@ -95,6 +158,8 @@
             device_id_type=MESH,
         )
         copy.start()
+        if k < count:
+            short_step(k)
         copy.wait()
         mine = source[...]
         theirs = recv[k]
@@ -106,29 +171,46 @@
             o_ref[...] = merged
         else:
             state[k] = merged
-
-
-def seq_allreduce(packed, devices):
+    for r in range(rounds, count):
+        short_step(r)
+
+
+def seq_allreduce(packed, devices, lengths, queries, fresh, cache):
     rounds = devices.bit_length() - 1
     rows = packed.size // LANES
+    flipped = jnp.swapaxes(cache, 2, 3)
+    vmem = pl.BlockSpec(memory_space=pltpu.VMEM)
     return pl.pallas_call(
         functools.partial(butterfly_kernel, rounds),
-        out_shape=jax.ShapeDtypeStruct(packed.shape, jnp.float32),
-        in_specs=[pl.BlockSpec(memory_space=pltpu.VMEM)],
-        out_specs=pl.BlockSpec(memory_space=pltpu.VMEM),
+        out_shape=(
+            jax.ShapeDtypeStruct(packed.shape, jnp.float32),
+            jax.ShapeDtypeStruct(queries.shape, jnp.bfloat16),
+        ),
+        in_specs=[
+            pl.BlockSpec(memory_space=pltpu.SMEM),
+            vmem,
+            vmem,
+            vmem,
+            pl.BlockSpec(memory_space=pl.ANY),
+        ],
+        out_specs=(vmem, vmem),
         scratch_shapes=[
             pltpu.VMEM((max(rounds - 1, 1),) + packed.shape, jnp.float32),
             pltpu.VMEM((rounds,) + packed.shape, jnp.float32),
             pltpu.SemaphoreType.DMA((rounds,)),
             pltpu.SemaphoreType.DMA((rounds,)),
+            pltpu.VMEM(flipped.shape, flipped.dtype),
+            pltpu.SemaphoreType.DMA(flipped.shape[:2]),
         ],
-        compiler_params=pltpu.CompilerParams(collective_id=0, has_side_effects=True),
+        compiler_params=pltpu.CompilerParams(
+            collective_id=0, has_side_effects=True, vmem_limit_bytes=48 * 1024 * 1024
+        ),
         cost_estimate=pl.CostEstimate(
-            flops=8 * rows * LANES * rounds,
+            flops=8 * rows * LANES * rounds + 4 * 36 * queries.shape[0] * cache.size // 2,
             transcendentals=2 * rows * rounds,
-            bytes_accessed=2 * rows * LANES * 4 * rounds,
-        ),
-    )(packed)
+            bytes_accessed=2 * rows * LANES * 4 * rounds + cache.size * 2,
+        ),
+    )(lengths, packed, queries, fresh, flipped)
 
 
 def scatter_kernel(parts, x_ref, o_ref, recv, local_sem, send_sem, recv_sem):
@@ -321,14 +403,6 @@
 ):
     request_count = queries_short.shape[0]
     token_count = queries_short.shape[1]
-    short_att = attention(
-        queries_short,
-        cache_short,
-        short_len,
-        jnp.zeros((1, 1), jnp.int32),
-        jnp.zeros((1,), jnp.int32),
-        fresh_short,
-    )
     local_len = cache_long.shape[2]
     packed = attention(
         queries_long,
@@ -339,7 +413,9 @@
     )
     heads = queries_long.shape[2] // HEAD_DIM
     shape = (queries_long.shape[0], heads, token_count)
-    reduced = seq_allreduce(packed, lax.axis_size("seq"))
+    reduced, short_att = seq_allreduce(
+        packed, lax.axis_size("seq"), short_len, queries_short, fresh_short, cache_short
+    )
     merged = (
         reduced[..., HEAD_DIM].reshape(shape),
         reduced[..., HEAD_DIM + 1].reshape(shape),

time: 62.7 us -> 58 us (0.925)
  Pallas kernels: 53.1 us -> 46.1 us
  local copies, waits for them, and re-layouts: 6.52 us -> 8.83 us
    pallas_call x2 -> x1, Pallas kernels: 10.9 us -> 5.43 us  [attention(): pl.pallas_call(functools.partial(attention_kernel, fresh is not None), ou...]
    unnamed x6 -> x12, local copies, waits for them, and re-layouts: 0.02 us -> 3.25 us
    pallas_call x1, Pallas kernels: 34.1 us -> 32.6 us  [seq_allreduce(): pl.pallas_call(functools.partial(butterfly_kernel, rounds), out_shape=(ja...]
    slice x1, local copies, waits for them, and re-layouts: 1.16 us -> 0.2 us  [per_device(): reduced[..., HEAD_DIM + 1].reshape(shape)]
    slice x1, local copies, waits for them, and re-layouts: 0.02 us -> 0.91 us  [fresh_part(): fresh[1]]
    slice x1, local copies, waits for them, and re-layouts: 0.91 us -> 0.02 us  [per_device(): reduced[..., :HEAD_DIM].reshape(shape + (HEAD_DIM,))]
    reshape x1, local copies, waits for them, and re-layouts: 0.1 us -> 0.83 us  [split_heads(): tensor.reshape(tensor.shape[0], tensor.shape[1], tensor.shape[2] // HEAD_...]
    reshape x1, local copies, waits for them, and re-layouts: 0.72 us -> 0.02 us  [per_device(): short_rows = short_att.reshape(-1, short_att.shape[2])]
where the time goes in v7:
time: 58 us; the launch traced here: 57.6 us
  Pallas kernels  46.1 us (79%)
  local copies, waits for them, and re-layouts  8.83 us (15%)
  other arithmetic  1.1 us (2%)
  matrix products  0.84 us (1%)
  between operations  0.77 us (1%)
    pallas_call x1, Pallas kernels, seq_allreduce(): pl.pallas_call(functools.partial(butterfly_kernel, rounds), out_shape=(ja...  32.6 us
    pallas_call x1, Pallas kernels, tp_reduce_scatter(): pl.pallas_call(functools.partial(scatter_kernel, parts), out_shape=jax.Sh...  8.06 us
    pallas_call x1, Pallas kernels, attention(): pl.pallas_call(functools.partial(attention_kernel, fresh is not None), ou...  5.43 us
    unnamed x12, local copies, waits for them, and re-layouts  3.25 us

profile of v7, /device:TPU:4, one launch (start us, length us, event | category | flops | bytes accessed | tf_op | source)
XLA Modules:
  0.0 57.6 jit_solution(14986119269973832122)
XLA Ops:
  0.6 0.0 copy-start
  0.7 0.9 %fusion.20 = (bf16[1,4,4,576]{3,2,1,0:T(4,128)(2,1)S(1)}, bf16[1,4,4,576]{3,2,1,0:T(4,128)(2,1)S(1)}) fusion(bf16[2,4,4,576]{3,2,1,0:T(4,128)(2,1)} %param.16), kind=kLoop, calls=%fused_computation.29 | loop fusion | bytes 73728 | tf_op jit(solution)/shard_map/slice | solution.py:59
  1.6 0.1 reshape_squeeze.14
  1.7 0.1 reshape_squeeze.13
  1.8 0.8 %reshape.76 = bf16[4,4,9,64]{3,2,1,0:T(8,128)(2,1)S(1)} reshape(bf16[4,4,576]{2,1,0:T(4,128)(2,1)} %q_ref.2) | data formatting | bytes 36864 | tf_op jit(solution)/shard_map/reshape | solution.py:20
  2.6 0.0 copy-start.3
  2.6 0.0 copy-start.4
  2.6 0.0 copy-start.5
  2.6 0.2 fusion.5
  2.8 0.2 copy.35
  3.0 0.1 fusion.12
  3.1 0.1 fusion.13
  3.3 0.2 copy.40
  3.5 5.4 %shard_map.113.x_ref = f32[4,36,128]{2,1,0:T(8,128)} custom-call(s32[4]{0:T(128)} %len_ref.2, s32[2,4]{1,0:T(2,128)} %bitcast.33, s32[1]{0:T(128)} %bitcast.1.off_ref, bf16[4,4,576]{2,1,0:T(4,128)(2,1)} %q_ref.2, bf16[2,4,576,256]{3,2,1,0:T(8,128)(2,1)} %bitcast.22, bf16[2,4,576,256]{3,2,1,0:T(8,128)(2,1)} %bitcast.23), custom_call_target="tpu_custom_call" | custom-call | flops 84934656 | bytes 2359296 | tf_op jit(solution)/shard_map/pallas_call | solution.py:378
  8.9 0.0 copy-done.3
  8.9 0.0 copy-done.4
  8.9 0.0 copy-done.5
  8.9 0.0 copy-start.1
  8.9 2.3 %copy-done.1 = bf16[2,2,1024,576]{2,3,1,0:T(8,128)(2,1)S(1)} copy-done((bf16[2,2,1024,576]{2,3,1,0:T(8,128)(2,1)S(1)}, bf16[2,2,1024,576]{2,3,1,0:T(8,128)(2,1)}, u32[]{:S(2)}) %copy-start.1) | copy-done | bytes 4718616
  11.3 0.0 copy-start.2
  11.3 0.9 %copy-done.2 = f32[4,36,128]{2,1,0:T(8,128)S(1)} copy-done((f32[4,36,128]{2,1,0:T(8,128)S(1)}, f32[4,36,128]{2,1,0:T(8,128)}, u32[]{:S(2)}) %copy-start.2) | copy-done | bytes 73752
  12.1 32.6 %shard_map.114 = (f32[4,36,128]{2,1,0:T(8,128)S(1)}, bf16[2,4,576]{2,1,0:T(4,128)(2,1)S(1)}) custom-call(s32[2]{0:T(128)S(1)} %copy-done.5, f32[4,36,128]{2,1,0:T(8,128)S(1)} %copy-done.2, bf16[2,4,576]{2,1,0:T(4,128)(2,1)S(1)} %copy-done.4, bf16[2,2,4,576]{3,2,1,0:T(4,128)(2,1)S(1)} %copy-done.3, bf16[2,2,576,1024]{3,2,1,0:T(8,128)(2,1)S(1)} %bitcast.20), custom_call_target="tpu_custom_call" | custom-call | flops 340623360 | bytes 5603328 | tf_op jit(solution)/shard_map/pallas_call | solution.py:183
  44.7 0.2 slice_reduce_fusion
  44.9 0.1 reshape_squeeze.15
  45.0 0.1 copy.43
  45.1 0.1 reshape_squeeze.12
  45.2 0.1 copy.37
  45.3 0.1 copy.38
  45.5 0.1 copy.42
  45.6 0.1 copy.44
  45.7 0.2 fusion.3
  45.9 0.1 reshape_reshape.3
  46.0 0.0 copy-done
  46.1 0.5 fusion.8
  46.5 0.2 reshape.77
  46.7 0.7 %copy.57 = f32[24,4,576]{2,0,1:T(8,128)} copy(f32[24,4,576]{2,1,0:T(4,128)S(1)} %reshape.77) | data formatting | bytes 442368 | tf_op jit(solution)/shard_map/reshape | solution.py:259
  47.4 8.1 %shard_map.115 = f32[24,576]{1,0:T(8,128)} custom-call(f32[4,24,576]{2,1,0:T(8,128)} %bitcast.24), custom_call_target="tpu_custom_call" | custom-call | flops 55296 | bytes 663552 | tf_op jit(solution)/shard_map/pallas_call | solution.py:260
  55.5 0.8 %convert_element_type.11 = bf16[24,576]{1,0:T(8,128)(2,1)S(1)} convert(f32[24,576]{1,0:T(8,128)} %shard_map.115) | non-fusion elementwise | flops 13824 | bytes 82944 | tf_op jit(solution)/shard_map/convert_element_type | solution.py:428
  56.4 0.6 %reshape.79 = bf16[4,4,576]{2,1,0:T(4,128)(2,1)} reshape(bf16[16,576]{1,0:T(8,128)(2,1)S(1)} %slice.29) | data formatting | bytes 36864 | tf_op jit(solution)/shard_map/reshape | solution.py:430
  57.0 0.6 %reshape.78 = bf16[2,4,576]{2,1,0:T(4,128)(2,1)} reshape(bf16[8,576]{1,0:T(8,128)(2,1)S(1)} %slice.28) | data formatting | bytes 18432 | tf_op jit(solution)/shard_map/reshape | solution.py:429
  (7 shorter events, 0.1 us)
Async XLA Ops:
  0.6 45.4 %copy-start = (bf16[576,2304]{1,0:T(8,128)(2,1)S(1)}, bf16[576,2304]{1,0:T(8,128)(2,1)}, u32[]{:S(2)}) copy-start(bf16[576,2304]{1,0:T(8,128)(2,1)} %param.19) | copy-start | bytes 7962628
  2.6 6.3 %copy-start.3 = (bf16[2,2,4,576]{3,2,1,0:T(4,128)(2,1)S(1)}, bf16[2,2,4,576]{3,2,1,0:T(4,128)(2,1)}, u32[]{:S(2)}) copy-start(bf16[2,2,4,576]{3,2,1,0:T(4,128)(2,1)} %f_ref.1) | copy-start | bytes 55300
  2.6 6.3 %copy-start.4 = (bf16[2,4,576]{2,1,0:T(4,128)(2,1)S(1)}, bf16[2,4,576]{2,1,0:T(4,128)(2,1)}, u32[]{:S(2)}) copy-start(bf16[2,4,576]{2,1,0:T(4,128)(2,1)} %q_ref.3) | copy-start | bytes 27652
  2.6 6.3 %copy-start.5 = (s32[2]{0:T(128)S(1)}, s32[2]{0:T(128)}, u32[]{:S(2)}) copy-start(s32[2]{0:T(128)} %len_ref.3) | copy-start | bytes 28
  8.9 2.3 %copy-start.1 = (bf16[2,2,1024,576]{2,3,1,0:T(8,128)(2,1)S(1)}, bf16[2,2,1024,576]{2,3,1,0:T(8,128)(2,1)}, u32[]{:S(2)}) copy-start(bf16[2,2,1024,576]{2,3,1,0:T(8,128)(2,1)} %param.11) | copy-start | bytes 14155780
  11.3 0.9 %copy-start.2 = (f32[4,36,128]{2,1,0:T(8,128)S(1)}, f32[4,36,128]{2,1,0:T(8,128)}, u32[]{:S(2)}) copy-start(f32[4,36,128]{2,1,0:T(8,128)} %shard_map.113.x_ref) | copy-start | bytes 221188

commit v8 on v7

--- a/solution.py
+++ b/solution.py
@@ -202,9 +202,7 @@
             pltpu.VMEM(flipped.shape, flipped.dtype),
             pltpu.SemaphoreType.DMA(flipped.shape[:2]),
         ],
-        compiler_params=pltpu.CompilerParams(
-            collective_id=0, has_side_effects=True, vmem_limit_bytes=48 * 1024 * 1024
-        ),
+        compiler_params=pltpu.CompilerParams(collective_id=0, has_side_effects=True),
         cost_estimate=pl.CostEstimate(
             flops=8 * rows * LANES * rounds + 4 * 36 * queries.shape[0] * cache.size // 2,
             transcendentals=2 * rows * rounds,

time: 58 us -> 57.4 us (0.990)
  local copies, waits for them, and re-layouts: 8.83 us -> 8.13 us
    unnamed x12 -> x2, local copies, waits for them, and re-layouts: 3.25 us -> 0.01 us
    slice x1, local copies, waits for them, and re-layouts: 0.2 us -> 1.15 us  [per_device(): reduced[..., HEAD_DIM + 1].reshape(shape)]
    slice x1, local copies, waits for them, and re-layouts: 0.02 us -> 0.91 us  [per_device(): reduced[..., :HEAD_DIM].reshape(shape + (HEAD_DIM,))]
    reshape x1, local copies, waits for them, and re-layouts: 0.02 us -> 0.72 us  [per_device(): short_rows = short_att.reshape(-1, short_att.shape[2])]
where the time goes in v8:
time: 57.4 us; the launch traced here: 56.9 us
  Pallas kernels  46.1 us (80%)
  local copies, waits for them, and re-layouts  8.13 us (14%)
  other arithmetic  1.09 us (2%)
  matrix products  0.84 us (1%)
  between operations  0.74 us (1%)
    pallas_call x1, Pallas kernels, seq_allreduce(): pl.pallas_call(functools.partial(butterfly_kernel, rounds), out_shape=(ja...  32.6 us
    pallas_call x1, Pallas kernels, tp_reduce_scatter(): pl.pallas_call(functools.partial(scatter_kernel, parts), out_shape=jax.Sh...  8.06 us
    pallas_call x1, Pallas kernels, attention(): pl.pallas_call(functools.partial(attention_kernel, fresh is not None), ou...  5.43 us
    slice x1, local copies, waits for them, and re-layouts, per_device(): reduced[..., HEAD_DIM + 1].reshape(shape)  1.15 us

profile of v8, /device:TPU:4, one launch (start us, length us, event | category | flops | bytes accessed | tf_op | source)
XLA Modules:
  0.0 56.9 jit_solution(13492277005123302804)
XLA Ops:
  0.6 0.0 copy-start
  0.7 0.9 %fusion.20 = (bf16[1,4,4,576]{3,2,1,0:T(4,128)(2,1)S(1)}, bf16[1,4,4,576]{3,2,1,0:T(4,128)(2,1)S(1)}) fusion(bf16[2,4,4,576]{3,2,1,0:T(4,128)(2,1)} %param.16), kind=kLoop, calls=%fused_computation.29 | loop fusion | bytes 73728 | tf_op jit(solution)/shard_map/slice | solution.py:59
  1.6 0.1 reshape_squeeze.14
  1.7 0.1 reshape_squeeze.13
  1.8 0.8 %reshape.76 = bf16[4,4,9,64]{3,2,1,0:T(8,128)(2,1)S(1)} reshape(bf16[4,4,576]{2,1,0:T(4,128)(2,1)} %q_ref.2) | data formatting | bytes 36864 | tf_op jit(solution)/shard_map/reshape | solution.py:20
  2.6 0.2 fusion.5
  2.8 0.2 copy.35
  3.0 0.1 fusion.12
  3.1 0.1 fusion.13
  3.2 0.2 copy.40
  3.4 5.4 %shard_map.113.x_ref = f32[4,36,128]{2,1,0:T(8,128)} custom-call(s32[4]{0:T(128)} %len_ref.2, s32[2,4]{1,0:T(2,128)} %bitcast.33, s32[1]{0:T(128)} %bitcast.1.off_ref, bf16[4,4,576]{2,1,0:T(4,128)(2,1)} %q_ref.2, bf16[2,4,576,256]{3,2,1,0:T(8,128)(2,1)} %bitcast.20, bf16[2,4,576,256]{3,2,1,0:T(8,128)(2,1)} %bitcast.21), custom_call_target="tpu_custom_call" | custom-call | flops 84934656 | bytes 2359296 | tf_op jit(solution)/shard_map/pallas_call | solution.py:376
  8.9 32.6 %shard_map.114 = (f32[4,36,128]{2,1,0:T(8,128)}, bf16[2,4,576]{2,1,0:T(4,128)(2,1)}) custom-call(s32[2]{0:T(128)} %len_ref.3, f32[4,36,128]{2,1,0:T(8,128)} %shard_map.113.x_ref, bf16[2,4,576]{2,1,0:T(4,128)(2,1)} %q_ref.3, bf16[2,2,4,576]{3,2,1,0:T(4,128)(2,1)} %f_ref.1, bf16[2,2,576,1024]{3,2,1,0:T(8,128)(2,1)} %bitcast.22), custom_call_target="tpu_custom_call" | custom-call | flops 340623360 | bytes 5603328 | tf_op jit(solution)/shard_map/pallas_call | solution.py:183
  41.5 0.7 %reshape.74 = bf16[8,576]{1,0:T(8,128)(2,1)S(1)} reshape(bf16[2,4,576]{2,1,0:T(4,128)(2,1)} %get-tuple-element.4) | data formatting | bytes 18432 | tf_op jit(solution)/shard_map/reshape | solution.py:423
  42.2 1.2 %slice_reduce_fusion = (f32[4,36]{1,0:T(4,128)S(1)}, f32[4,36]{1,0:T(4,128)S(1)}) fusion(f32[4,36,128]{2,1,0:T(8,128)} %get-tuple-element.5), kind=kLoop, calls=%fused_computation.6 | loop fusion | bytes 2304 | tf_op jit(solution)/shard_map/slice | solution.py:419
  43.4 0.1 reshape_squeeze.15
  43.4 0.1 copy.43
  43.6 0.1 reshape_squeeze.12
  43.6 0.1 copy.37
  43.8 0.1 copy.38
  43.9 0.1 copy.42
  44.0 0.1 copy.44
  44.1 0.9 %copy.32 = f32[4,36,64]{2,0,1:T(4,128)S(1)} copy(f32[4,36,64]{2,1,0:T(8,128)} %bitcast.24) | data formatting | bytes 73728 | tf_op jit(solution)/shard_map/slice | solution.py:420
  45.0 0.2 fusion.3
  45.3 0.1 reshape_reshape.3
  45.4 0.0 copy-done
  45.4 0.5 fusion.8
  45.9 0.2 reshape.77
  46.1 0.7 %copy.57 = f32[24,4,576]{2,0,1:T(8,128)} copy(f32[24,4,576]{2,1,0:T(4,128)S(1)} %reshape.77) | data formatting | bytes 442368 | tf_op jit(solution)/shard_map/reshape | solution.py:257
  46.8 8.1 %shard_map.115 = f32[24,576]{1,0:T(8,128)} custom-call(f32[4,24,576]{2,1,0:T(8,128)} %bitcast.23), custom_call_target="tpu_custom_call" | custom-call | flops 55296 | bytes 663552 | tf_op jit(solution)/shard_map/pallas_call | solution.py:258
  54.8 0.8 %convert_element_type.11 = bf16[24,576]{1,0:T(8,128)(2,1)S(1)} convert(f32[24,576]{1,0:T(8,128)} %shard_map.115) | non-fusion elementwise | flops 13824 | bytes 82944 | tf_op jit(solution)/shard_map/convert_element_type | solution.py:426
  55.7 0.6 %reshape.79 = bf16[4,4,576]{2,1,0:T(4,128)(2,1)} reshape(bf16[16,576]{1,0:T(8,128)(2,1)S(1)} %slice.29) | data formatting | bytes 36864 | tf_op jit(solution)/shard_map/reshape | solution.py:428
  56.3 0.6 %reshape.78 = bf16[2,4,576]{2,1,0:T(4,128)(2,1)} reshape(bf16[8,576]{1,0:T(8,128)(2,1)S(1)} %slice.28) | data formatting | bytes 18432 | tf_op jit(solution)/shard_map/reshape | solution.py:427
  (5 shorter events, 0.0 us)
Async XLA Ops:
  0.6 44.7 %copy-start = (bf16[576,2304]{1,0:T(8,128)(2,1)S(1)}, bf16[576,2304]{1,0:T(8,128)(2,1)}, u32[]{:S(2)}) copy-start(bf16[576,2304]{1,0:T(8,128)(2,1)} %param.19) | copy-start | bytes 7962628

commit v9 on v8

--- a/solution.py
+++ b/solution.py
@@ -211,7 +211,8 @@
     )(lengths, packed, queries, fresh, flipped)
 
 
-def scatter_kernel(parts, x_ref, o_ref, recv, local_sem, send_sem, recv_sem):
+def scatter_kernel(parts, x_ref, *rest):
+    *out_refs, recv, local_sem, send_sem, recv_sem = rest
     me = lax.axis_index("tp")
     row = lax.axis_index("seq")
     barrier = pltpu.get_barrier_semaphore()
@@ -248,18 +249,26 @@
     total = recv[0]
     for s in range(1, parts):
         total = total + recv[s]
-    o_ref[...] = total
-
-
-def tp_reduce_scatter(term, parts):
+    total = total.astype(jnp.bfloat16)
+    start = 0
+    for out_ref in out_refs:
+        for r in range(out_ref.shape[0]):
+            out_ref[r] = total[start : start + out_ref.shape[1]]
+            start += out_ref.shape[1]
+
+
+def tp_reduce_scatter(term, parts, shapes):
     rows, width = term.shape
     cols = width // parts
     blocks = jnp.transpose(term.reshape(rows, parts, cols), (1, 0, 2))
+    vmem = pl.BlockSpec(memory_space=pltpu.VMEM)
     return pl.pallas_call(
         functools.partial(scatter_kernel, parts),
-        out_shape=jax.ShapeDtypeStruct((rows, cols), jnp.float32),
-        in_specs=[pl.BlockSpec(memory_space=pltpu.VMEM)],
-        out_specs=pl.BlockSpec(memory_space=pltpu.VMEM),
+        out_shape=tuple(
+            jax.ShapeDtypeStruct(shape + (cols,), jnp.bfloat16) for shape in shapes
+        ),
+        in_specs=[vmem],
+        out_specs=tuple(vmem for _ in shapes),
         scratch_shapes=[
             pltpu.VMEM((parts, rows, cols), jnp.float32),
             pltpu.SemaphoreType.DMA(()),
@@ -423,10 +432,10 @@
     short_rows = short_att.reshape(-1, short_att.shape[2])
     both = jnp.concatenate([short_rows, long_att.reshape(-1, long_att.shape[2])], axis=0)
     term = jnp.dot(both, out_weight, preferred_element_type=jnp.float32)
-    cols = tp_reduce_scatter(term, lax.axis_size("tp")).astype(jnp.bfloat16)
-    short_out = cols[: short_rows.shape[0]].reshape(request_count, token_count, cols.shape[1])
-    long_out = cols[short_rows.shape[0] :].reshape(
-        long_att.shape[0], long_att.shape[1], cols.shape[1]
+    short_out, long_out = tp_reduce_scatter(
+        term,
+        lax.axis_size("tp"),
+        ((request_count, token_count), (long_att.shape[0], long_att.shape[1])),
     )
     return (short_out, long_out)
 

time: 57.4 us -> 58 us (1.010)
  local copies, waits for them, and re-layouts: 8.13 us -> 9.54 us
  other arithmetic: 1.09 us -> 0.26 us
    unnamed x2 -> x4, local copies, waits for them, and re-layouts: 0.01 us -> 2.66 us
    reshape x2 -> x0, local copies, waits for them, and re-layouts: 1.23 us -> none  [the longest x1 0.62 us: per_device(): cols[short_rows.shape[0]:]]
    convert_element_type x1 -> x0, other arithmetic: 0.83 us -> none  [per_device(): cols = tp_reduce_scatter(term, lax.axis_size('tp')).astype(jnp.bfloat16)]
where the time goes in v9:
time: 58 us; the launch traced here: 57.5 us
  Pallas kernels  46.1 us (79%)
  local copies, waits for them, and re-layouts  9.54 us (16%)
  matrix products  0.84 us (1%)
  between operations  0.74 us (1%)
    pallas_call x1, Pallas kernels, seq_allreduce(): pl.pallas_call(functools.partial(butterfly_kernel, rounds), out_shape=(ja...  32.6 us
    pallas_call x1, Pallas kernels, tp_reduce_scatter(): pl.pallas_call(functools.partial(scatter_kernel, parts), out_shape=tuple(...  8.06 us
    pallas_call x1, Pallas kernels, attention(): pl.pallas_call(functools.partial(attention_kernel, fresh is not None), ou...  5.43 us
    unnamed x4, local copies, waits for them, and re-layouts  2.66 us

profile of v9, /device:TPU:4, one launch (start us, length us, event | category | flops | bytes accessed | tf_op | source)
XLA Modules:
  0.0 57.5 jit_solution(6238559652840146022)
XLA Ops:
  0.6 0.0 copy-start
  0.7 0.9 %fusion.20 = (bf16[1,4,4,576]{3,2,1,0:T(4,128)(2,1)S(1)}, bf16[1,4,4,576]{3,2,1,0:T(4,128)(2,1)S(1)}) fusion(bf16[2,4,4,576]{3,2,1,0:T(4,128)(2,1)} %param.16), kind=kLoop, calls=%fused_computation.29 | loop fusion | bytes 73728 | tf_op jit(solution)/shard_map/slice | solution.py:59
  1.6 0.1 reshape_squeeze.14
  1.7 0.1 reshape_squeeze.13
  1.8 0.8 %reshape.70 = bf16[4,4,9,64]{3,2,1,0:T(8,128)(2,1)S(1)} reshape(bf16[4,4,576]{2,1,0:T(4,128)(2,1)} %q_ref.2) | data formatting | bytes 36864 | tf_op jit(solution)/shard_map/reshape | solution.py:20
  2.6 0.2 fusion.5
  2.8 0.2 copy.35
  3.0 0.1 fusion.12
  3.1 0.1 fusion.13
  3.2 0.2 copy.40
  3.4 5.4 %shard_map.113.x_ref = f32[4,36,128]{2,1,0:T(8,128)} custom-call(s32[4]{0:T(128)} %len_ref.2, s32[2,4]{1,0:T(2,128)} %bitcast.33, s32[1]{0:T(128)} %bitcast.1.off_ref, bf16[4,4,576]{2,1,0:T(4,128)(2,1)} %q_ref.2, bf16[2,4,576,256]{3,2,1,0:T(8,128)(2,1)} %bitcast.20, bf16[2,4,576,256]{3,2,1,0:T(8,128)(2,1)} %bitcast.21), custom_call_target="tpu_custom_call" | custom-call | flops 84934656 | bytes 2359296 | tf_op jit(solution)/shard_map/pallas_call | solution.py:385
  8.9 32.6 %shard_map.114 = (f32[4,36,128]{2,1,0:T(8,128)}, bf16[2,4,576]{2,1,0:T(4,128)(2,1)}) custom-call(s32[2]{0:T(128)} %len_ref.3, f32[4,36,128]{2,1,0:T(8,128)} %shard_map.113.x_ref, bf16[2,4,576]{2,1,0:T(4,128)(2,1)} %q_ref.3, bf16[2,2,4,576]{3,2,1,0:T(4,128)(2,1)} %f_ref.1, bf16[2,2,576,1024]{3,2,1,0:T(8,128)(2,1)} %bitcast.22), custom_call_target="tpu_custom_call" | custom-call | flops 340623360 | bytes 5603328 | tf_op jit(solution)/shard_map/pallas_call | solution.py:183
  41.5 0.7 %reshape.68 = bf16[8,576]{1,0:T(8,128)(2,1)S(1)} reshape(bf16[2,4,576]{2,1,0:T(4,128)(2,1)} %get-tuple-element.4) | data formatting | bytes 18432 | tf_op jit(solution)/shard_map/reshape | solution.py:432
  42.2 1.2 %slice_reduce_fusion = (f32[4,36]{1,0:T(4,128)S(1)}, f32[4,36]{1,0:T(4,128)S(1)}) fusion(f32[4,36,128]{2,1,0:T(8,128)} %get-tuple-element.5), kind=kLoop, calls=%fused_computation.6 | loop fusion | bytes 2304 | tf_op jit(solution)/shard_map/slice | solution.py:428
  43.4 0.1 reshape_squeeze.15
  43.4 0.1 copy.43
  43.6 0.1 reshape_squeeze.12
  43.6 0.1 copy.37
  43.8 0.1 copy.38
  43.9 0.1 copy.42
  44.0 0.1 copy.44
  44.1 0.9 %copy.32 = f32[4,36,64]{2,0,1:T(4,128)S(1)} copy(f32[4,36,64]{2,1,0:T(8,128)} %bitcast.24) | data formatting | bytes 73728 | tf_op jit(solution)/shard_map/slice | solution.py:429
  45.0 0.2 fusion.3
  45.3 0.1 reshape_reshape.3
  45.4 0.0 copy-done
  45.4 0.5 fusion.8
  45.9 0.2 reshape.71
  46.1 0.7 %copy.57 = f32[24,4,576]{2,0,1:T(8,128)} copy(f32[24,4,576]{2,1,0:T(4,128)S(1)} %reshape.71) | data formatting | bytes 442368 | tf_op jit(solution)/shard_map/reshape | solution.py:263
  46.8 8.1 %shard_map.115 = (bf16[2,4,576]{2,1,0:T(4,128)(2,1)}, bf16[4,4,576]{2,1,0:T(4,128)(2,1)}) custom-call(f32[4,24,576]{2,1,0:T(8,128)} %bitcast.23), custom_call_target="tpu_custom_call" | custom-call | flops 55296 | bytes 663552 | tf_op jit(solution)/shard_map/pallas_call | solution.py:265
  54.8 1.3 %copy.60 = bf16[2,4,576]{2,1,0:T(4,128)(2,1)} copy(bf16[2,4,576]{2,1,0:T(4,128)(2,1)} %get-tuple-element.20) | data formatting | bytes 18432
  56.1 1.3 %copy.61 = bf16[4,4,576]{2,1,0:T(4,128)(2,1)} copy(bf16[4,4,576]{2,1,0:T(4,128)(2,1)} %get-tuple-element.21) | data formatting | bytes 36864
  (3 shorter events, 0.0 us)
Async XLA Ops:
  0.6 44.7 %copy-start = (bf16[576,2304]{1,0:T(8,128)(2,1)S(1)}, bf16[576,2304]{1,0:T(8,128)(2,1)}, u32[]{:S(2)}) copy-start(bf16[576,2304]{1,0:T(8,128)(2,1)} %param.19) | copy-start | bytes 7962628

commit v10 on v8

--- a/solution.py
+++ b/solution.py
@@ -108,8 +108,54 @@
     return jnp.dot(gather, normed.astype(jnp.bfloat16), preferred_element_type=jnp.float32)
 
 
+def finish_long(state, q, fk, fv):
+    tokens, width = q.shape
+    rows = (width // HEAD_DIM) * tokens
+    pick = (
+        lax.broadcasted_iota(jnp.int32, (rows, tokens), 0) % tokens
+        == lax.broadcasted_iota(jnp.int32, (rows, tokens), 1)
+    ).astype(jnp.bfloat16)
+    head_lanes = (
+        lax.broadcasted_iota(jnp.int32, (rows, width), 0) // tokens
+        == lax.broadcasted_iota(jnp.int32, (rows, width), 1) // HEAD_DIM
+    )
+    spread = jnp.dot(pick, q, preferred_element_type=jnp.float32)
+    query = jnp.where(head_lanes, spread, 0.0).astype(jnp.bfloat16)
+    contract = (((1,), (1,)), ((), ()))
+    fresh_scores = lax.dot_general(
+        query, fk, contract, preferred_element_type=jnp.float32
+    ) * (1.0 / math.sqrt(HEAD_DIM))
+    causal = lax.broadcasted_iota(jnp.int32, (rows, tokens), 1) <= (
+        lax.broadcasted_iota(jnp.int32, (rows, tokens), 0) % tokens
+    )
+    fresh_scores = jnp.where(causal, fresh_scores, NEGATIVE)
+    top = state[:, HEAD_DIM : HEAD_DIM + 1]
+    highest = jnp.maximum(top, jnp.max(fresh_scores, axis=1, keepdims=True))
+    kept = jnp.exp(top - highest)
+    fresh_expo = jnp.where(causal, jnp.exp(fresh_scores - highest), 0.0)
+    totals = state[:, HEAD_DIM + 1 : HEAD_DIM + 2] * kept + jnp.sum(
+        fresh_expo, axis=1, keepdims=True
+    )
+    fresh_sum = jnp.where(
+        head_lanes,
+        jnp.dot(fresh_expo.astype(jnp.bfloat16), fv, preferred_element_type=jnp.float32),
+        0.0,
+    )
+    folded = fresh_sum[:, 0:HEAD_DIM]
+    for g in range(1, width // HEAD_DIM):
+        folded = folded + fresh_sum[:, g * HEAD_DIM : (g + 1) * HEAD_DIM]
+    normed = ((state[:, :HEAD_DIM] * kept + folded) / totals).astype(jnp.float32)
+    spread_back = jnp.concatenate([normed] * (width // HEAD_DIM), axis=1)
+    placed = jnp.where(head_lanes, spread_back.astype(jnp.bfloat16), 0.0).astype(jnp.bfloat16)
+    gather = (
+        lax.broadcasted_iota(jnp.int32, (tokens, rows), 1) % tokens
+        == lax.broadcasted_iota(jnp.int32, (tokens, rows), 0)
+    ).astype(jnp.bfloat16)
+    return jnp.dot(gather, placed, preferred_element_type=jnp.float32)
+
+
 def butterfly_kernel(
-    rounds, len_ref, x_ref, q_ref, f_ref, cache_ref, o_ref, att_ref,
+    rounds, len_ref, x_ref, q_ref, f_ref, cache_ref, ql_ref, fl_ref, o_ref, att_ref,
     state, recv, send_sem, recv_sem, kv_buf, kv_sem,
 ):
     me = lax.axis_index("seq")
@@ -168,14 +214,17 @@
             jnp.where(first, mine, theirs), jnp.where(first, theirs, mine)
         )
         if k == rounds - 1:
-            o_ref[...] = merged
+            for r in range(o_ref.shape[0]):
+                o_ref[r] = finish_long(
+                    merged[r], ql_ref[r], fl_ref[0, r], fl_ref[1, r]
+                ).astype(o_ref.dtype)
         else:
             state[k] = merged
     for r in range(rounds, count):
         short_step(r)
 
 
-def seq_allreduce(packed, devices, lengths, queries, fresh, cache):
+def seq_allreduce(packed, devices, lengths, queries, fresh, cache, queries_long, fresh_long):
     rounds = devices.bit_length() - 1
     rows = packed.size // LANES
     flipped = jnp.swapaxes(cache, 2, 3)
@@ -183,7 +232,7 @@
     return pl.pallas_call(
         functools.partial(butterfly_kernel, rounds),
         out_shape=(
-            jax.ShapeDtypeStruct(packed.shape, jnp.float32),
+            jax.ShapeDtypeStruct(queries_long.shape, jnp.bfloat16),
             jax.ShapeDtypeStruct(queries.shape, jnp.bfloat16),
         ),
         in_specs=[
@@ -192,6 +241,8 @@
             vmem,
             vmem,
             pl.BlockSpec(memory_space=pl.ANY),
+            vmem,
+            vmem,
         ],
         out_specs=(vmem, vmem),
         scratch_shapes=[
@@ -208,7 +259,7 @@
             transcendentals=2 * rows * rounds,
             bytes_accessed=2 * rows * LANES * 4 * rounds + cache.size * 2,
         ),
-    )(lengths, packed, queries, fresh, flipped)
+    )(lengths, packed, queries, fresh, flipped, queries_long, fresh_long)
 
 
 def scatter_kernel(parts, x_ref, o_ref, recv, local_sem, send_sem, recv_sem):
@@ -411,15 +462,16 @@
     )
     heads = queries_long.shape[2] // HEAD_DIM
     shape = (queries_long.shape[0], heads, token_count)
-    reduced, short_att = seq_allreduce(
-        packed, lax.axis_size("seq"), short_len, queries_short, fresh_short, cache_short
-    )
-    merged = (
-        reduced[..., HEAD_DIM].reshape(shape),
-        reduced[..., HEAD_DIM + 1].reshape(shape),
-        reduced[..., :HEAD_DIM].reshape(shape + (HEAD_DIM,)),
-    )
-    long_att = finish(combine_parts(merged, fresh_part(queries_long, fresh_long)))
+    long_att, short_att = seq_allreduce(
+        packed,
+        lax.axis_size("seq"),
+        short_len,
+        queries_short,
+        fresh_short,
+        cache_short,
+        queries_long,
+        fresh_long,
+    )
     short_rows = short_att.reshape(-1, short_att.shape[2])
     both = jnp.concatenate([short_rows, long_att.reshape(-1, long_att.shape[2])], axis=0)
     term = jnp.dot(both, out_weight, preferred_element_type=jnp.float32)

time: 57.4 us -> 55.1 us (0.960)
  local copies, waits for them, and re-layouts: 8.13 us -> 3.62 us
  Pallas kernels: 46.1 us -> 49.2 us
    slice x3 -> x0, local copies, waits for them, and re-layouts: 2.98 us -> none  [the longest x1 1.15 us: per_device(): reduced[..., HEAD_DIM + 1].reshape(shape)]
    pallas_call x1, Pallas kernels: 32.6 us -> 35.5 us  [seq_allreduce(): pl.pallas_call(functools.partial(butterfly_kernel, rounds), out_shape=(ja...]
    another operation x7 -> x0, local copies, waits for them, and re-layouts: 0.69 us -> none  [the longest x2 0.2 us: split_heads(): tensor.reshape(tensor.shape[0], tensor.shape[1], tensor.shape[2] // HEAD_...]
where the time goes in v10:
time: 55.1 us; the launch traced here: 54.8 us
  Pallas kernels  49.2 us (89%)
  local copies, waits for them, and re-layouts  3.62 us (7%)
  other arithmetic  0.83 us (2%)
  between operations  0.68 us (1%)
    pallas_call x1, Pallas kernels, seq_allreduce(): pl.pallas_call(functools.partial(butterfly_kernel, rounds), out_shape=(ja...  35.5 us
    pallas_call x1, Pallas kernels, tp_reduce_scatter(): pl.pallas_call(functools.partial(scatter_kernel, parts), out_shape=jax.Sh...  8.07 us
    pallas_call x1, Pallas kernels, attention(): pl.pallas_call(functools.partial(attention_kernel, fresh is not None), ou...  5.56 us

profile of v10, /device:TPU:4, one launch (start us, length us, event | category | flops | bytes accessed | tf_op | source)
XLA Modules:
  0.0 54.8 jit_solution(660215881601673537)
XLA Ops:
  0.6 0.0 copy-start
  0.7 5.6 %shard_map.113.x_ref = f32[4,36,128]{2,1,0:T(8,128)} custom-call(s32[4]{0:T(128)} %len_ref.2, s32[2,4]{1,0:T(2,128)} %bitcast.12, s32[1]{0:T(128)} %bitcast.1.off_ref, bf16[4,4,576]{2,1,0:T(4,128)(2,1)} %ql_ref.1, bf16[2,4,576,256]{3,2,1,0:T(8,128)(2,1)} %bitcast.8, bf16[2,4,576,256]{3,2,1,0:T(8,128)(2,1)} %bitcast.9), custom_call_target="tpu_custom_call" | custom-call | flops 84934656 | bytes 2359296 | tf_op jit(solution)/shard_map/pallas_call | solution.py:427
  6.2 35.5 %shard_map.114 = (bf16[4,4,576]{2,1,0:T(4,128)(2,1)}, bf16[2,4,576]{2,1,0:T(4,128)(2,1)}) custom-call(s32[2]{0:T(128)} %len_ref.3, f32[4,36,128]{2,1,0:T(8,128)} %shard_map.113.x_ref, bf16[2,4,576]{2,1,0:T(4,128)(2,1)} %q_ref.3, bf16[2,2,4,576]{3,2,1,0:T(4,128)(2,1)} %f_ref.1, bf16[2,2,576,1024]{3,2,1,0:T(8,128)(2,1)} %bitcast.10, ...), custom_call_target="tpu_custom_call" | custom-call | flops 340623360 | bytes 5603328 | tf_op jit(solution)/shard_map/pallas_call | solution.py:232
  41.7 0.7 %reshape.23 = bf16[8,576]{1,0:T(8,128)(2,1)S(1)} reshape(bf16[2,4,576]{2,1,0:T(4,128)(2,1)} %get-tuple-element.4) | data formatting | bytes 18432 | tf_op jit(solution)/shard_map/reshape | solution.py:475
  42.5 0.7 %reshape.24 = bf16[16,576]{1,0:T(8,128)(2,1)S(1)} reshape(bf16[4,4,576]{2,1,0:T(4,128)(2,1)} %get-tuple-element.5) | data formatting | bytes 36864 | tf_op jit(solution)/shard_map/reshape | solution.py:476
  43.2 0.0 copy-done
  43.2 0.5 fusion
  43.7 0.2 reshape.25
  43.9 0.7 %copy.14 = f32[24,4,576]{2,0,1:T(8,128)} copy(f32[24,4,576]{2,1,0:T(4,128)S(1)} %reshape.25) | data formatting | bytes 442368 | tf_op jit(solution)/shard_map/reshape | solution.py:308
  44.6 8.1 %shard_map.115 = f32[24,576]{1,0:T(8,128)} custom-call(f32[4,24,576]{2,1,0:T(8,128)} %bitcast.11), custom_call_target="tpu_custom_call" | custom-call | flops 55296 | bytes 663552 | tf_op jit(solution)/shard_map/pallas_call | solution.py:309
  52.7 0.8 %convert_element_type.3 = bf16[24,576]{1,0:T(8,128)(2,1)S(1)} convert(f32[24,576]{1,0:T(8,128)} %shard_map.115) | non-fusion elementwise | flops 13824 | bytes 82944 | tf_op jit(solution)/shard_map/convert_element_type | solution.py:478
  53.5 0.6 %reshape.27 = bf16[4,4,576]{2,1,0:T(4,128)(2,1)} reshape(bf16[16,576]{1,0:T(8,128)(2,1)S(1)} %slice.9) | data formatting | bytes 36864 | tf_op jit(solution)/shard_map/reshape | solution.py:480
  54.2 0.6 %reshape.26 = bf16[2,4,576]{2,1,0:T(4,128)(2,1)} reshape(bf16[8,576]{1,0:T(8,128)(2,1)S(1)} %slice.8) | data formatting | bytes 18432 | tf_op jit(solution)/shard_map/reshape | solution.py:479
  (2 shorter events, 0.0 us)
Async XLA Ops:
  0.6 42.6 %copy-start = (bf16[576,2304]{1,0:T(8,128)(2,1)S(1)}, bf16[576,2304]{1,0:T(8,128)(2,1)}, u32[]{:S(2)}) copy-start(bf16[576,2304]{1,0:T(8,128)(2,1)} %param.19) | copy-start | bytes 7962628

commit v11 on v10

--- a/solution.py
+++ b/solution.py
@@ -155,12 +155,12 @@
 
 
 def butterfly_kernel(
-    rounds, len_ref, x_ref, q_ref, f_ref, cache_ref, ql_ref, fl_ref, o_ref, att_ref,
+    rounds, len_ref, x_ref, q_ref, f_ref, cache_ref, ql_ref, fl_ref, att_ref,
     state, recv, send_sem, recv_sem, kv_buf, kv_sem,
 ):
     me = lax.axis_index("seq")
     column = lax.axis_index("tp")
-    count = q_ref.shape[0]
+    count, tokens = q_ref.shape[0], q_ref.shape[1]
     loads = []
     for r in range(count):
         pair = []
@@ -176,7 +176,7 @@
         for load in loads[r]:
             load.wait()
         spot = lax.broadcasted_iota(jnp.int32, (1, kv_buf.shape[3]), 1)
-        att_ref[r] = short_request(
+        att_ref[r * tokens : (r + 1) * tokens] = short_request(
             q_ref[r], kv_buf.at[0, r], kv_buf.at[1, r], spot < len_ref[r],
             f_ref[0, r], f_ref[1, r],
         ).astype(att_ref.dtype)
@@ -214,10 +214,11 @@
             jnp.where(first, mine, theirs), jnp.where(first, theirs, mine)
         )
         if k == rounds - 1:
-            for r in range(o_ref.shape[0]):
-                o_ref[r] = finish_long(
+            for r in range(ql_ref.shape[0]):
+                row = (count + r) * tokens
+                att_ref[row : row + tokens] = finish_long(
                     merged[r], ql_ref[r], fl_ref[0, r], fl_ref[1, r]
-                ).astype(o_ref.dtype)
+                ).astype(att_ref.dtype)
         else:
             state[k] = merged
     for r in range(rounds, count):
@@ -231,9 +232,12 @@
     vmem = pl.BlockSpec(memory_space=pltpu.VMEM)
     return pl.pallas_call(
         functools.partial(butterfly_kernel, rounds),
-        out_shape=(
-            jax.ShapeDtypeStruct(queries_long.shape, jnp.bfloat16),
-            jax.ShapeDtypeStruct(queries.shape, jnp.bfloat16),
+        out_shape=jax.ShapeDtypeStruct(
+            (
+                (queries.shape[0] + queries_long.shape[0]) * queries.shape[1],
+                queries.shape[2],
+            ),
+            jnp.bfloat16,
         ),
         in_specs=[
             pl.BlockSpec(memory_space=pltpu.SMEM),
@@ -244,7 +248,7 @@
             vmem,
             vmem,
         ],
-        out_specs=(vmem, vmem),
+        out_specs=vmem,
         scratch_shapes=[
             pltpu.VMEM((max(rounds - 1, 1),) + packed.shape, jnp.float32),
             pltpu.VMEM((rounds,) + packed.shape, jnp.float32),
@@ -462,7 +466,7 @@
     )
     heads = queries_long.shape[2] // HEAD_DIM
     shape = (queries_long.shape[0], heads, token_count)
-    long_att, short_att = seq_allreduce(
+    both = seq_allreduce(
         packed,
         lax.axis_size("seq"),
         short_len,
@@ -472,13 +476,12 @@
         queries_long,
         fresh_long,
     )
-    short_rows = short_att.reshape(-1, short_att.shape[2])
-    both = jnp.concatenate([short_rows, long_att.reshape(-1, long_att.shape[2])], axis=0)
+    short_count = request_count * token_count
     term = jnp.dot(both, out_weight, preferred_element_type=jnp.float32)
     cols = tp_reduce_scatter(term, lax.axis_size("tp")).astype(jnp.bfloat16)
-    short_out = cols[: short_rows.shape[0]].reshape(request_count, token_count, cols.shape[1])
-    long_out = cols[short_rows.shape[0] :].reshape(
-        long_att.shape[0], long_att.shape[1], cols.shape[1]
+    short_out = cols[:short_count].reshape(request_count, token_count, cols.shape[1])
+    long_out = cols[short_count:].reshape(
+        queries_long.shape[0], queries_long.shape[1], cols.shape[1]
     )
     return (short_out, long_out)
 

time: 55.1 us -> 54.4 us (0.987)
  local copies, waits for them, and re-layouts: 3.62 us -> 2.16 us
  matrix products: 0.48 us -> 1.23 us
    reshape x4 -> x2, local copies, waits for them, and re-layouts: 2.69 us -> 1.23 us  [the longest x1 0.62 us: per_device(): cols[short_count:]]
    dot_general x1, matrix products: 0.48 us -> 1.23 us  [per_device(): term = jnp.dot(both, out_weight, preferred_element_type=jnp.float32)]
where the time goes in v11:
time: 54.4 us; the launch traced here: 54 us
  Pallas kernels  49.1 us (90%)
  local copies, waits for them, and re-layouts  2.16 us (4%)
  matrix products  1.23 us (2%)
  other arithmetic  0.83 us (2%)
  between operations  0.68 us (1%)
    pallas_call x1, Pallas kernels, seq_allreduce(): pl.pallas_call(functools.partial(butterfly_kernel, rounds), out_shape=jax...  35.5 us
    pallas_call x1, Pallas kernels, tp_reduce_scatter(): pl.pallas_call(functools.partial(scatter_kernel, parts), out_shape=jax.Sh...  8.06 us
    pallas_call x1, Pallas kernels, attention(): pl.pallas_call(functools.partial(attention_kernel, fresh is not None), ou...  5.56 us
    dot_general x1, matrix products, per_device(): term = jnp.dot(both, out_weight, preferred_element_type=jnp.float32)  1.23 us

profile of v11, /device:TPU:4, one launch (start us, length us, event | category | flops | bytes accessed | tf_op | source)
XLA Modules:
  0.0 54.0 jit_solution(17845846537469868780)
XLA Ops:
  0.6 0.0 copy-start
  0.7 5.6 %shard_map.113.x_ref = f32[4,36,128]{2,1,0:T(8,128)} custom-call(s32[4]{0:T(128)} %len_ref.2, s32[2,4]{1,0:T(2,128)} %bitcast.13, s32[1]{0:T(128)} %bitcast.1.off_ref, bf16[4,4,576]{2,1,0:T(4,128)(2,1)} %ql_ref.1, bf16[2,4,576,256]{3,2,1,0:T(8,128)(2,1)} %bitcast.9, bf16[2,4,576,256]{3,2,1,0:T(8,128)(2,1)} %bitcast.10), custom_call_target="tpu_custom_call" | custom-call | flops 84934656 | bytes 2359296 | tf_op jit(solution)/shard_map/pallas_call | solution.py:431
  6.2 35.5 %shard_map.114 = bf16[24,576]{1,0:T(8,128)(2,1)} custom-call(s32[2]{0:T(128)} %len_ref.3, f32[4,36,128]{2,1,0:T(8,128)} %shard_map.113.x_ref, bf16[2,4,576]{2,1,0:T(4,128)(2,1)} %q_ref.3, bf16[2,2,4,576]{3,2,1,0:T(4,128)(2,1)} %f_ref.1, bf16[2,2,576,1024]{3,2,1,0:T(8,128)(2,1)} %bitcast.11, bf16[4,4,576]{2,1,0:T(4,128)(2,1)} %ql_ref.1, ...), custom_call_target="tpu_custom_call" | custom-call | flops 340623360 | bytes 5603328 | tf_op jit(solution)/shard_map/pallas_call | solution.py:233
  41.7 0.0 copy-done
  41.8 1.2 %fusion = f32[24,2304]{1,0:T(8,128)S(1)} fusion(bf16[24,576]{1,0:T(8,128)(2,1)} %shard_map.114, bf16[576,2304]{1,0:T(8,128)(2,1)S(1)} %copy-done), kind=kOutput, calls=%fused_computation.1 | convolution fusion | flops 63700992 | bytes 2903040 | tf_op jit(solution)/shard_map/dot_general | solution.py:480
  43.0 0.2 reshape.17
  43.2 0.7 %copy.14 = f32[24,4,576]{2,0,1:T(8,128)} copy(f32[24,4,576]{2,1,0:T(4,128)S(1)} %reshape.17) | data formatting | bytes 442368 | tf_op jit(solution)/shard_map/reshape | solution.py:312
  43.9 8.1 %shard_map.115 = f32[24,576]{1,0:T(8,128)} custom-call(f32[4,24,576]{2,1,0:T(8,128)} %bitcast.12), custom_call_target="tpu_custom_call" | custom-call | flops 55296 | bytes 663552 | tf_op jit(solution)/shard_map/pallas_call | solution.py:313
  52.0 0.8 %convert_element_type.3 = bf16[24,576]{1,0:T(8,128)(2,1)S(1)} convert(f32[24,576]{1,0:T(8,128)} %shard_map.115) | non-fusion elementwise | flops 13824 | bytes 82944 | tf_op jit(solution)/shard_map/convert_element_type | solution.py:481
  52.8 0.6 %reshape.19 = bf16[4,4,576]{2,1,0:T(4,128)(2,1)} reshape(bf16[16,576]{1,0:T(8,128)(2,1)S(1)} %slice.9) | data formatting | bytes 36864 | tf_op jit(solution)/shard_map/reshape | solution.py:483
  53.4 0.6 %reshape.18 = bf16[2,4,576]{2,1,0:T(4,128)(2,1)} reshape(bf16[8,576]{1,0:T(8,128)(2,1)S(1)} %slice.8) | data formatting | bytes 18432 | tf_op jit(solution)/shard_map/reshape | solution.py:482
  (2 shorter events, 0.0 us)
Async XLA Ops:
  0.6 41.1 %copy-start = (bf16[576,2304]{1,0:T(8,128)(2,1)S(1)}, bf16[576,2304]{1,0:T(8,128)(2,1)}, u32[]{:S(2)}) copy-start(bf16[576,2304]{1,0:T(8,128)(2,1)} %param.19) | copy-start | bytes 7962628

commit v12 on v11

--- a/solution.py
+++ b/solution.py
@@ -154,13 +154,58 @@
     return jnp.dot(gather, placed, preferred_element_type=jnp.float32)
 
 
+def long_request(q, k_view, v_view, usable):
+    tokens, width = q.shape
+    rows = (width // HEAD_DIM) * tokens
+    pick = (
+        lax.broadcasted_iota(jnp.int32, (rows, tokens), 0) % tokens
+        == lax.broadcasted_iota(jnp.int32, (rows, tokens), 1)
+    ).astype(jnp.bfloat16)
+    head_lanes = (
+        lax.broadcasted_iota(jnp.int32, (rows, width), 0) // tokens
+        == lax.broadcasted_iota(jnp.int32, (rows, width), 1) // HEAD_DIM
+    )
+    spread = jnp.dot(pick, q, preferred_element_type=jnp.float32)
+    query = jnp.where(head_lanes, spread, 0.0).astype(jnp.bfloat16)
+    contract = (((1,), (1,)), ((), ()))
+    scores = jnp.dot(query, k_view[...], preferred_element_type=jnp.float32) * (
+        1.0 / math.sqrt(HEAD_DIM)
+    )
+    scores = jnp.where(usable, scores, NEGATIVE)
+    highest = jnp.max(scores, axis=1, keepdims=True)
+    expo = jnp.where(usable, jnp.exp(scores - highest), 0.0)
+    totals = jnp.sum(expo, axis=1, keepdims=True)
+    summed = lax.dot_general(
+        expo.astype(jnp.bfloat16), v_view[...], contract, preferred_element_type=jnp.float32
+    )
+    masked = jnp.where(head_lanes, summed, 0.0)
+    folded = masked[:, 0:HEAD_DIM]
+    for g in range(1, width // HEAD_DIM):
+        folded = folded + masked[:, g * HEAD_DIM : (g + 1) * HEAD_DIM]
+    return jnp.concatenate(
+        [folded, highest, totals, jnp.zeros((rows, LANES - HEAD_DIM - 2), jnp.float32)],
+        axis=1,
+    )
+
+
 def butterfly_kernel(
-    rounds, len_ref, x_ref, q_ref, f_ref, cache_ref, ql_ref, fl_ref, att_ref,
-    state, recv, send_sem, recv_sem, kv_buf, kv_sem,
+    rounds, len_ref, llen_ref, live_ref, q_ref, f_ref, cache_ref, ql_ref, fl_ref,
+    lcache_ref, att_ref, state, recv, send_sem, recv_sem, kv_buf, kv_sem, lkv_buf, lkv_sem,
 ):
     me = lax.axis_index("seq")
     column = lax.axis_index("tp")
     count, tokens = q_ref.shape[0], q_ref.shape[1]
+    long_count = ql_ref.shape[0]
+    long_loads = []
+    for r in range(long_count):
+        pair = []
+        for kv in range(2):
+            load = pltpu.make_async_copy(
+                lcache_ref.at[kv, r], lkv_buf.at[kv, r], lkv_sem.at[kv, r]
+            )
+            load.start()
+            pair.append(load)
+        long_loads.append(pair)
     loads = []
     for r in range(count):
         pair = []
@@ -191,10 +236,23 @@
         pl.semaphore_signal(
             barrier, inc=1, device_id=(partner, column), device_id_type=MESH
         )
+    positions = lkv_buf.shape[3]
+    spot = lax.broadcasted_iota(jnp.int32, (1, positions), 1)
+    blocks = live_ref.shape[0]
+    for r in range(long_count):
+        alive = spot < 0
+        for b in range(blocks):
+            alive = alive | (
+                (spot // (positions // blocks) == b) & (live_ref[b, r] == 1)
+            )
+        usable = alive & (spot + me * positions < llen_ref[r])
+        for load in long_loads[r]:
+            load.wait()
+        state[0, r] = long_request(ql_ref[r], lkv_buf.at[0, r], lkv_buf.at[1, r], usable)
     pl.semaphore_wait(barrier, rounds)
     for k in range(rounds):
         partner, bit = partners[k]
-        source = x_ref if k == 0 else state.at[k - 1]
+        source = state.at[k]
         copy = pltpu.make_async_remote_copy(
             src_ref=source,
             dst_ref=recv.at[k],
@@ -220,50 +278,47 @@
                     merged[r], ql_ref[r], fl_ref[0, r], fl_ref[1, r]
                 ).astype(att_ref.dtype)
         else:
-            state[k] = merged
+            state[k + 1] = merged
     for r in range(rounds, count):
         short_step(r)
 
 
-def seq_allreduce(packed, devices, lengths, queries, fresh, cache, queries_long, fresh_long):
+def seq_allreduce(
+    devices, lengths, queries, fresh, cache, long_len, live, queries_long, fresh_long, cache_long
+):
     rounds = devices.bit_length() - 1
-    rows = packed.size // LANES
+    tokens, width = queries.shape[1], queries.shape[2]
+    rows = (width // HEAD_DIM) * tokens
+    state_shape = (queries_long.shape[0], rows, LANES)
     flipped = jnp.swapaxes(cache, 2, 3)
+    flipped_long = jnp.swapaxes(cache_long, 2, 3)
     vmem = pl.BlockSpec(memory_space=pltpu.VMEM)
+    smem = pl.BlockSpec(memory_space=pltpu.SMEM)
+    hbm = pl.BlockSpec(memory_space=pl.ANY)
     return pl.pallas_call(
         functools.partial(butterfly_kernel, rounds),
         out_shape=jax.ShapeDtypeStruct(
-            (
-                (queries.shape[0] + queries_long.shape[0]) * queries.shape[1],
-                queries.shape[2],
-            ),
-            jnp.bfloat16,
+            ((queries.shape[0] + queries_long.shape[0]) * tokens, width), jnp.bfloat16
         ),
-        in_specs=[
-            pl.BlockSpec(memory_space=pltpu.SMEM),
-            vmem,
-            vmem,
-            vmem,
-            pl.BlockSpec(memory_space=pl.ANY),
-            vmem,
-            vmem,
-        ],
+        in_specs=[smem, smem, smem, vmem, vmem, hbm, vmem, vmem, hbm],
         out_specs=vmem,
         scratch_shapes=[
-            pltpu.VMEM((max(rounds - 1, 1),) + packed.shape, jnp.float32),
-            pltpu.VMEM((rounds,) + packed.shape, jnp.float32),
+            pltpu.VMEM((rounds,) + state_shape, jnp.float32),
+            pltpu.VMEM((rounds,) + state_shape, jnp.float32),
             pltpu.SemaphoreType.DMA((rounds,)),
             pltpu.SemaphoreType.DMA((rounds,)),
             pltpu.VMEM(flipped.shape, flipped.dtype),
             pltpu.SemaphoreType.DMA(flipped.shape[:2]),
+            pltpu.VMEM(flipped_long.shape, flipped_long.dtype),
+            pltpu.SemaphoreType.DMA(flipped_long.shape[:2]),
         ],
         compiler_params=pltpu.CompilerParams(collective_id=0, has_side_effects=True),
         cost_estimate=pl.CostEstimate(
-            flops=8 * rows * LANES * rounds + 4 * 36 * queries.shape[0] * cache.size // 2,
-            transcendentals=2 * rows * rounds,
-            bytes_accessed=2 * rows * LANES * 4 * rounds + cache.size * 2,
+            flops=4 * rows * (queries.shape[0] * cache.size + queries_long.shape[0] * cache_long.size),
+            transcendentals=rows * (cache.size + cache_long.size) // width,
+            bytes_accessed=2 * (cache.size + cache_long.size),
         ),
-    )(lengths, packed, queries, fresh, flipped, queries_long, fresh_long)
+    )(lengths, long_len, live, queries, fresh, flipped, queries_long, fresh_long, flipped_long)
 
 
 def scatter_kernel(parts, x_ref, o_ref, recv, local_sem, send_sem, recv_sem):
@@ -456,25 +511,17 @@
 ):
     request_count = queries_short.shape[0]
     token_count = queries_short.shape[1]
-    local_len = cache_long.shape[2]
-    packed = attention(
-        queries_long,
-        cache_long,
-        long_len,
-        block_live.T,
-        (lax.axis_index("seq") * local_len).astype(jnp.int32).reshape(1),
-    )
-    heads = queries_long.shape[2] // HEAD_DIM
-    shape = (queries_long.shape[0], heads, token_count)
     both = seq_allreduce(
-        packed,
         lax.axis_size("seq"),
         short_len,
         queries_short,
         fresh_short,
         cache_short,
+        long_len,
+        block_live.T,
         queries_long,
         fresh_long,
+        cache_long,
     )
     short_count = request_count * token_count
     term = jnp.dot(both, out_weight, preferred_element_type=jnp.float32)

time: 54.4 us -> 51.5 us (0.947)
  Pallas kernels: 49.1 us -> 46.3 us
    pallas_call x1 -> x0, Pallas kernels: 5.56 us -> none  [attention(): pl.pallas_call(functools.partial(attention_kernel, fresh is not None), ou...]
    pallas_call x1, Pallas kernels: 35.5 us -> 38.3 us  [seq_allreduce(): pl.pallas_call(functools.partial(butterfly_kernel, rounds), out_shape=jax...]
where the time goes in v12:
time: 51.5 us; the launch traced here: 51.2 us
  Pallas kernels  46.3 us (90%)
  local copies, waits for them, and re-layouts  2.16 us (4%)
  matrix products  1.23 us (2%)
  other arithmetic  0.83 us (2%)
  between operations  0.67 us (1%)
    pallas_call x1, Pallas kernels, seq_allreduce(): pl.pallas_call(functools.partial(butterfly_kernel, rounds), out_shape=jax...  38.3 us
    pallas_call x1, Pallas kernels, tp_reduce_scatter(): pl.pallas_call(functools.partial(scatter_kernel, parts), out_shape=jax.Sh...  8.06 us
    dot_general x1, matrix products, per_device(): term = jnp.dot(both, out_weight, preferred_element_type=jnp.float32)  1.23 us

profile of v12, /device:TPU:4, one launch (start us, length us, event | category | flops | bytes accessed | tf_op | source)
XLA Modules:
  0.0 51.2 jit_solution(9404724041365758820)
XLA Ops:
  0.6 0.0 copy-start
  0.6 38.3 %shard_map.113 = bf16[24,576]{1,0:T(8,128)(2,1)} custom-call(s32[2]{0:T(128)} %len_ref.1, s32[4]{0:T(128)} %llen_ref.1, s32[2,4]{1,0:T(2,128)} %bitcast.11, bf16[2,4,576]{2,1,0:T(4,128)(2,1)} %q_ref.1, bf16[2,2,4,576]{3,2,1,0:T(4,128)(2,1)} %f_ref.1, bf16[2,2,576,1024]{3,2,1,0:T(8,128)(2,1)} %bitcast.8, bf16[4,4,576]{2,1,0:T(4,128)(2,1)} %ql_ref.1, ...), custom_call_target="tpu_custom_call" | custom-call | flops 1358954496 | bytes 7077888 | tf_op jit(solution)/shard_map/pallas_call | solution.py:298
  38.9 0.0 copy-done
  38.9 1.2 %fusion = f32[24,2304]{1,0:T(8,128)S(1)} fusion(bf16[24,576]{1,0:T(8,128)(2,1)} %shard_map.113, bf16[576,2304]{1,0:T(8,128)(2,1)S(1)} %copy-done), kind=kOutput, calls=%fused_computation.1 | convolution fusion | flops 63700992 | bytes 2903040 | tf_op jit(solution)/shard_map/dot_general | solution.py:527
  40.2 0.2 reshape.13
  40.4 0.7 %copy.14 = f32[24,4,576]{2,0,1:T(8,128)} copy(f32[24,4,576]{2,1,0:T(4,128)S(1)} %reshape.13) | data formatting | bytes 442368 | tf_op jit(solution)/shard_map/reshape | solution.py:367
  41.1 8.1 %shard_map.114 = f32[24,576]{1,0:T(8,128)} custom-call(f32[4,24,576]{2,1,0:T(8,128)} %bitcast.10), custom_call_target="tpu_custom_call" | custom-call | flops 55296 | bytes 663552 | tf_op jit(solution)/shard_map/pallas_call | solution.py:368
  49.1 0.8 %convert_element_type.3 = bf16[24,576]{1,0:T(8,128)(2,1)S(1)} convert(f32[24,576]{1,0:T(8,128)} %shard_map.114) | non-fusion elementwise | flops 13824 | bytes 82944 | tf_op jit(solution)/shard_map/convert_element_type | solution.py:528
  50.0 0.6 %reshape.15 = bf16[4,4,576]{2,1,0:T(4,128)(2,1)} reshape(bf16[16,576]{1,0:T(8,128)(2,1)S(1)} %slice.9) | data formatting | bytes 36864 | tf_op jit(solution)/shard_map/reshape | solution.py:530
  50.6 0.6 %reshape.14 = bf16[2,4,576]{2,1,0:T(4,128)(2,1)} reshape(bf16[8,576]{1,0:T(8,128)(2,1)S(1)} %slice.8) | data formatting | bytes 18432 | tf_op jit(solution)/shard_map/reshape | solution.py:529
  (2 shorter events, 0.0 us)
Async XLA Ops:
  0.6 38.3 %copy-start = (bf16[576,2304]{1,0:T(8,128)(2,1)S(1)}, bf16[576,2304]{1,0:T(8,128)(2,1)}, u32[]{:S(2)}) copy-start(bf16[576,2304]{1,0:T(8,128)(2,1)} %param.19) | copy-start | bytes 7962628

commit v13 on v12

--- a/solution.py
+++ b/solution.py
@@ -189,8 +189,8 @@
 
 
 def butterfly_kernel(
-    rounds, len_ref, llen_ref, live_ref, q_ref, f_ref, cache_ref, ql_ref, fl_ref,
-    lcache_ref, att_ref, state, recv, send_sem, recv_sem, kv_buf, kv_sem, lkv_buf, lkv_sem,
+    rounds, parts, len_ref, llen_ref, live_ref, q_ref, f_ref, cache_ref, ql_ref, fl_ref,
+    lcache_ref, w_ref, out_ref, att_ref, state, recv, send_sem, recv_sem, kv_buf, kv_sem, lkv_buf, lkv_sem,
 ):
     me = lax.axis_index("seq")
     column = lax.axis_index("tp")
@@ -281,10 +281,15 @@
             state[k + 1] = merged
     for r in range(rounds, count):
         short_step(r)
+    term = jnp.dot(att_ref[...], w_ref[...], preferred_element_type=jnp.float32)
+    cols = w_ref.shape[1] // parts
+    for q in range(parts):
+        out_ref[q] = term[:, q * cols : (q + 1) * cols]
 
 
 def seq_allreduce(
-    devices, lengths, queries, fresh, cache, long_len, live, queries_long, fresh_long, cache_long
+    devices, lengths, queries, fresh, cache, long_len, live, queries_long, fresh_long, cache_long,
+    weight, parts,
 ):
     rounds = devices.bit_length() - 1
     tokens, width = queries.shape[1], queries.shape[2]
@@ -296,13 +301,15 @@
     smem = pl.BlockSpec(memory_space=pltpu.SMEM)
     hbm = pl.BlockSpec(memory_space=pl.ANY)
     return pl.pallas_call(
-        functools.partial(butterfly_kernel, rounds),
+        functools.partial(butterfly_kernel, rounds, parts),
         out_shape=jax.ShapeDtypeStruct(
-            ((queries.shape[0] + queries_long.shape[0]) * tokens, width), jnp.bfloat16
+            (parts, (queries.shape[0] + queries_long.shape[0]) * tokens, weight.shape[1] // parts),
+            jnp.float32,
         ),
-        in_specs=[smem, smem, smem, vmem, vmem, hbm, vmem, vmem, hbm],
+        in_specs=[smem, smem, smem, vmem, vmem, hbm, vmem, vmem, hbm, vmem],
         out_specs=vmem,
         scratch_shapes=[
+            pltpu.VMEM(((queries.shape[0] + queries_long.shape[0]) * tokens, width), jnp.bfloat16),
             pltpu.VMEM((rounds,) + state_shape, jnp.float32),
             pltpu.VMEM((rounds,) + state_shape, jnp.float32),
             pltpu.SemaphoreType.DMA((rounds,)),
@@ -318,7 +325,7 @@
             transcendentals=rows * (cache.size + cache_long.size) // width,
             bytes_accessed=2 * (cache.size + cache_long.size),
         ),
-    )(lengths, long_len, live, queries, fresh, flipped, queries_long, fresh_long, flipped_long)
+    )(lengths, long_len, live, queries, fresh, flipped, queries_long, fresh_long, flipped_long, weight)
 
 
 def scatter_kernel(parts, x_ref, o_ref, recv, local_sem, send_sem, recv_sem):
@@ -361,10 +368,8 @@
     o_ref[...] = total
 
 
-def tp_reduce_scatter(term, parts):
-    rows, width = term.shape
-    cols = width // parts
-    blocks = jnp.transpose(term.reshape(rows, parts, cols), (1, 0, 2))
+def tp_reduce_scatter(blocks):
+    parts, rows, cols = blocks.shape
     return pl.pallas_call(
         functools.partial(scatter_kernel, parts),
         out_shape=jax.ShapeDtypeStruct((rows, cols), jnp.float32),
@@ -378,9 +383,9 @@
         ],
         compiler_params=pltpu.CompilerParams(collective_id=1, has_side_effects=True),
         cost_estimate=pl.CostEstimate(
-            flops=rows * width,
+            flops=rows * cols * parts,
             transcendentals=0,
-            bytes_accessed=3 * rows * width * 4,
+            bytes_accessed=3 * rows * cols * parts * 4,
         ),
     )(blocks)
 
@@ -511,7 +516,7 @@
 ):
     request_count = queries_short.shape[0]
     token_count = queries_short.shape[1]
-    both = seq_allreduce(
+    blocks = seq_allreduce(
         lax.axis_size("seq"),
         short_len,
         queries_short,
@@ -522,10 +527,11 @@
         queries_long,
         fresh_long,
         cache_long,
+        out_weight,
+        lax.axis_size("tp"),
     )
     short_count = request_count * token_count
-    term = jnp.dot(both, out_weight, preferred_element_type=jnp.float32)
-    cols = tp_reduce_scatter(term, lax.axis_size("tp")).astype(jnp.bfloat16)
+    cols = tp_reduce_scatter(blocks).astype(jnp.bfloat16)
     short_out = cols[:short_count].reshape(request_count, token_count, cols.shape[1])
     long_out = cols[short_count:].reshape(
         queries_long.shape[0], queries_long.shape[1], cols.shape[1]

time: 51.5 us -> 50.8 us (0.986)
  Pallas kernels: 46.3 us -> 47.9 us
  matrix products: 1.23 us -> 0 us
  local copies, waits for them, and re-layouts: 2.16 us -> 1.24 us
    pallas_call x1, Pallas kernels: 38.3 us -> 39.7 us  [seq_allreduce(): pl.pallas_call(functools.partial(butterfly_kernel, rounds, parts), out_sh...]
    dot_general x1 -> x0, matrix products: 1.23 us -> none  [per_device(): term = jnp.dot(both, out_weight, preferred_element_type=jnp.float32)]
    reshape x2 -> x0, local copies, waits for them, and re-layouts: 0.91 us -> none  [tp_reduce_scatter(): blocks = jnp.transpose(term.reshape(rows, parts, cols), (1, 0, 2))]
where the time goes in v13:
time: 50.8 us; the launch traced here: 50.6 us
  Pallas kernels  47.9 us (94%)
  local copies, waits for them, and re-layouts  1.24 us (2%)
  other arithmetic  0.83 us (2%)
  between operations  0.65 us (1%)
    pallas_call x1, Pallas kernels, seq_allreduce(): pl.pallas_call(functools.partial(butterfly_kernel, rounds, parts), out_sh...  39.7 us
    pallas_call x1, Pallas kernels, tp_reduce_scatter(): pl.pallas_call(functools.partial(scatter_kernel, parts), out_shape=jax.Sh...  8.2 us

profile of v13, /device:TPU:4, one launch (start us, length us, event | category | flops | bytes accessed | tf_op | source)
XLA Modules:
  0.0 50.6 jit_solution(7316133335840616655)
XLA Ops:
  0.6 39.7 %shard_map.113.x_ref = f32[4,24,576]{2,1,0:T(8,128)} custom-call(s32[2]{0:T(128)} %len_ref.1, s32[4]{0:T(128)} %llen_ref.1, s32[2,4]{1,0:T(2,128)} %bitcast.5, bf16[2,4,576]{2,1,0:T(4,128)(2,1)} %q_ref.1, bf16[2,2,4,576]{3,2,1,0:T(4,128)(2,1)} %f_ref.1, bf16[2,2,576,1024]{3,2,1,0:T(8,128)(2,1)} %bitcast.3, bf16[4,4,576]{2,1,0:T(4,128)(2,1)} %ql_ref.1, ...), custom_call_target="tpu_custom_call" | custom-call | flops 1358954496 | bytes 7077888 | tf_op jit(solution)/shard_map/pallas_call | solution.py:303
  40.4 8.2 %shard_map.114 = f32[24,576]{1,0:T(8,128)} custom-call(f32[4,24,576]{2,1,0:T(8,128)} %shard_map.113.x_ref), custom_call_target="tpu_custom_call" | custom-call | flops 55296 | bytes 663552 | tf_op jit(solution)/shard_map/pallas_call | solution.py:373
  48.6 0.8 %convert_element_type.3 = bf16[24,576]{1,0:T(8,128)(2,1)S(1)} convert(f32[24,576]{1,0:T(8,128)} %shard_map.114) | non-fusion elementwise | flops 13824 | bytes 82944 | tf_op jit(solution)/shard_map/convert_element_type | solution.py:534
  49.4 0.6 %reshape.11 = bf16[4,4,576]{2,1,0:T(4,128)(2,1)} reshape(bf16[16,576]{1,0:T(8,128)(2,1)S(1)} %slice.9) | data formatting | bytes 36864 | tf_op jit(solution)/shard_map/reshape | solution.py:536
  50.0 0.6 %reshape.10 = bf16[2,4,576]{2,1,0:T(4,128)(2,1)} reshape(bf16[8,576]{1,0:T(8,128)(2,1)S(1)} %slice.8) | data formatting | bytes 18432 | tf_op jit(solution)/shard_map/reshape | solution.py:535
  (2 shorter events, 0.0 us)

commit v14 on v13

--- a/solution.py
+++ b/solution.py
@@ -191,6 +191,7 @@
 def butterfly_kernel(
     rounds, parts, len_ref, llen_ref, live_ref, q_ref, f_ref, cache_ref, ql_ref, fl_ref,
     lcache_ref, w_ref, out_ref, att_ref, state, recv, send_sem, recv_sem, kv_buf, kv_sem, lkv_buf, lkv_sem,
+    blk, tp_recv, tp_local, tp_send, tp_sem,
 ):
     me = lax.axis_index("seq")
     column = lax.axis_index("tp")
@@ -236,6 +237,10 @@
         pl.semaphore_signal(
             barrier, inc=1, device_id=(partner, column), device_id_type=MESH
         )
+    for d in range(1, parts):
+        pl.semaphore_signal(
+            barrier, inc=1, device_id=(me, (column + d) % parts), device_id_type=MESH
+        )
     positions = lkv_buf.shape[3]
     spot = lax.broadcasted_iota(jnp.int32, (1, positions), 1)
     blocks = live_ref.shape[0]
@@ -249,7 +254,7 @@
         for load in long_loads[r]:
             load.wait()
         state[0, r] = long_request(ql_ref[r], lkv_buf.at[0, r], lkv_buf.at[1, r], usable)
-    pl.semaphore_wait(barrier, rounds)
+    pl.semaphore_wait(barrier, rounds + parts - 1)
     for k in range(rounds):
         partner, bit = partners[k]
         source = state.at[k]
@@ -284,7 +289,36 @@
     term = jnp.dot(att_ref[...], w_ref[...], preferred_element_type=jnp.float32)
     cols = w_ref.shape[1] // parts
     for q in range(parts):
-        out_ref[q] = term[:, q * cols : (q + 1) * cols]
+        blk[q] = term[:, q * cols : (q + 1) * cols]
+    own = pltpu.make_async_copy(blk.at[column], tp_recv.at[column], tp_local)
+    own.start()
+    sends = []
+    for d in range(1, parts):
+        send = pltpu.make_async_remote_copy(
+            src_ref=blk.at[(column + d) % parts],
+            dst_ref=tp_recv.at[column],
+            send_sem=tp_send.at[d - 1],
+            recv_sem=tp_sem.at[d - 1],
+            device_id=(me, (column + d) % parts),
+            device_id_type=MESH,
+        )
+        send.start()
+        sends.append(send)
+    own.wait()
+    for d in range(1, parts):
+        sends[d - 1].wait_send()
+        pltpu.make_async_remote_copy(
+            src_ref=blk.at[0],
+            dst_ref=tp_recv.at[(column + parts - d) % parts],
+            send_sem=tp_send.at[d - 1],
+            recv_sem=tp_sem.at[d - 1],
+            device_id=(me, (column + parts - d) % parts),
+            device_id_type=MESH,
+        ).wait_recv()
+    total = tp_recv[0]
+    for s in range(1, parts):
+        total = total + tp_recv[s]
+    out_ref[...] = total
 
 
 def seq_allreduce(
@@ -295,6 +329,11 @@
     tokens, width = queries.shape[1], queries.shape[2]
     rows = (width // HEAD_DIM) * tokens
     state_shape = (queries_long.shape[0], rows, LANES)
+    block_shape = (
+        parts,
+        (queries.shape[0] + queries_long.shape[0]) * tokens,
+        weight.shape[1] // parts,
+    )
     flipped = jnp.swapaxes(cache, 2, 3)
     flipped_long = jnp.swapaxes(cache_long, 2, 3)
     vmem = pl.BlockSpec(memory_space=pltpu.VMEM)
@@ -303,7 +342,7 @@
     return pl.pallas_call(
         functools.partial(butterfly_kernel, rounds, parts),
         out_shape=jax.ShapeDtypeStruct(
-            (parts, (queries.shape[0] + queries_long.shape[0]) * tokens, weight.shape[1] // parts),
+            ((queries.shape[0] + queries_long.shape[0]) * tokens, weight.shape[1] // parts),
             jnp.float32,
         ),
         in_specs=[smem, smem, smem, vmem, vmem, hbm, vmem, vmem, hbm, vmem],
@@ -318,6 +357,11 @@
             pltpu.SemaphoreType.DMA(flipped.shape[:2]),
             pltpu.VMEM(flipped_long.shape, flipped_long.dtype),
             pltpu.SemaphoreType.DMA(flipped_long.shape[:2]),
+            pltpu.VMEM(block_shape, jnp.float32),
+            pltpu.VMEM(block_shape, jnp.float32),
+            pltpu.SemaphoreType.DMA(()),
+            pltpu.SemaphoreType.DMA((parts - 1,)),
+            pltpu.SemaphoreType.DMA((parts - 1,)),
         ],
         compiler_params=pltpu.CompilerParams(collective_id=0, has_side_effects=True),
         cost_estimate=pl.CostEstimate(
@@ -531,7 +575,7 @@
         lax.axis_size("tp"),
     )
     short_count = request_count * token_count
-    cols = tp_reduce_scatter(blocks).astype(jnp.bfloat16)
+    cols = blocks.astype(jnp.bfloat16)
     short_out = cols[:short_count].reshape(request_count, token_count, cols.shape[1])
     long_out = cols[short_count:].reshape(
         queries_long.shape[0], queries_long.shape[1], cols.shape[1]

time: 50.8 us -> 47.3 us (0.931); the launches traced: 50.6 us -> 46.6 us
  Pallas kernels: 47.9 us -> 43.8 us
    pallas_call x1 -> x0, Pallas kernels: 8.2 us -> none  [tp_reduce_scatter(): pl.pallas_call(functools.partial(scatter_kernel, parts), out_shape=jax.Sh...]
    pallas_call x1, Pallas kernels: 39.7 us -> 43.8 us  [seq_allreduce(): pl.pallas_call(functools.partial(butterfly_kernel, rounds, parts), out_sh...]
where the time goes in v14:
time: 47.3 us; the launch traced here: 46.6 us
  Pallas kernels  43.8 us (93%)
  local copies, waits for them, and re-layouts  1.24 us (3%)
  other arithmetic  0.83 us (2%)
  between operations  0.64 us (1%)
    pallas_call x1, Pallas kernels, seq_allreduce(): pl.pallas_call(functools.partial(butterfly_kernel, rounds, parts), out_sh...  43.8 us

profile of v14, /device:TPU:4, one launch (start us, length us, event | category | flops | bytes accessed | tf_op | source)
XLA Modules:
  0.0 46.6 jit_solution(5511129559395240376)
XLA Ops:
  0.6 43.8 %shard_map.113 = f32[24,576]{1,0:T(8,128)} custom-call(s32[2]{0:T(128)} %len_ref.1, s32[4]{0:T(128)} %llen_ref.1, s32[2,4]{1,0:T(2,128)} %bitcast.5, bf16[2,4,576]{2,1,0:T(4,128)(2,1)} %q_ref.1, bf16[2,2,4,576]{3,2,1,0:T(4,128)(2,1)} %f_ref.1, bf16[2,2,576,1024]{3,2,1,0:T(8,128)(2,1)} %bitcast.3, bf16[4,4,576]{2,1,0:T(4,128)(2,1)} %ql_ref.1, ...), custom_call_target="tpu_custom_call" | custom-call | flops 1358954496 | bytes 7077888 | tf_op jit(solution)/shard_map/pallas_call | solution.py:342
  44.5 0.8 %convert_element_type.3 = bf16[24,576]{1,0:T(8,128)(2,1)S(1)} convert(f32[24,576]{1,0:T(8,128)} %shard_map.113) | non-fusion elementwise | flops 13824 | bytes 82944 | tf_op jit(solution)/shard_map/convert_element_type | solution.py:578
  45.3 0.6 %reshape.11 = bf16[4,4,576]{2,1,0:T(4,128)(2,1)} reshape(bf16[16,576]{1,0:T(8,128)(2,1)S(1)} %slice.9) | data formatting | bytes 36864 | tf_op jit(solution)/shard_map/reshape | solution.py:580
  46.0 0.6 %reshape.10 = bf16[2,4,576]{2,1,0:T(4,128)(2,1)} reshape(bf16[8,576]{1,0:T(8,128)(2,1)S(1)} %slice.8) | data formatting | bytes 18432 | tf_op jit(solution)/shard_map/reshape | solution.py:579
  (2 shorter events, 0.0 us)

commit v15 on v14

--- a/solution.py
+++ b/solution.py
@@ -318,7 +318,7 @@
     total = tp_recv[0]
     for s in range(1, parts):
         total = total + tp_recv[s]
-    out_ref[...] = total
+    out_ref[...] = total.astype(out_ref.dtype)
 
 
 def seq_allreduce(
@@ -343,7 +343,7 @@
         functools.partial(butterfly_kernel, rounds, parts),
         out_shape=jax.ShapeDtypeStruct(
             ((queries.shape[0] + queries_long.shape[0]) * tokens, weight.shape[1] // parts),
-            jnp.float32,
+            jnp.bfloat16,
         ),
         in_specs=[smem, smem, smem, vmem, vmem, hbm, vmem, vmem, hbm, vmem],
         out_specs=vmem,
@@ -575,7 +575,7 @@
         lax.axis_size("tp"),
     )
     short_count = request_count * token_count
-    cols = blocks.astype(jnp.bfloat16)
+    cols = blocks
     short_out = cols[:short_count].reshape(request_count, token_count, cols.shape[1])
     long_out = cols[short_count:].reshape(
         queries_long.shape[0], queries_long.shape[1], cols.shape[1]

time: 47.3 us -> 48 us (1.015)
  local copies, waits for them, and re-layouts: 1.24 us -> 2.66 us
  other arithmetic: 0.83 us -> 0 us
    convert_element_type x1 -> x0, other arithmetic: 0.83 us -> none  [per_device(): cols = blocks.astype(jnp.bfloat16)]
    slice x1, local copies, waits for them, and re-layouts: 0.01 us -> 0.73 us  [per_device(): cols[short_count:]]
    slice x1, local copies, waits for them, and re-layouts: 0.01 us -> 0.7 us  [per_device(): cols[:short_count].reshape(request_count, token_count, cols.shape[1])]
where the time goes in v15:
time: 48 us; the launch traced here: 47.1 us
  Pallas kernels  43.8 us (91%)
  local copies, waits for them, and re-layouts  2.66 us (6%)
  between operations  0.64 us (1%)
    pallas_call x1, Pallas kernels, seq_allreduce(): pl.pallas_call(functools.partial(butterfly_kernel, rounds, parts), out_sh...  43.8 us

profile of v15, /device:TPU:4, one launch (start us, length us, event | category | flops | bytes accessed | tf_op | source)
XLA Modules:
  0.0 47.1 jit_solution(10969936517678908789)
XLA Ops:
  0.6 43.8 %shard_map.113 = bf16[24,576]{1,0:T(8,128)(2,1)} custom-call(s32[2]{0:T(128)} %len_ref.1, s32[4]{0:T(128)} %llen_ref.1, s32[2,4]{1,0:T(2,128)} %bitcast.5, bf16[2,4,576]{2,1,0:T(4,128)(2,1)} %q_ref.1, bf16[2,2,4,576]{3,2,1,0:T(4,128)(2,1)} %f_ref.1, bf16[2,2,576,1024]{3,2,1,0:T(8,128)(2,1)} %bitcast.3, bf16[4,4,576]{2,1,0:T(4,128)(2,1)} %ql_ref.1, ...), custom_call_target="tpu_custom_call" | custom-call | flops 1358954496 | bytes 7077888 | tf_op jit(solution)/shard_map/pallas_call | solution.py:342
  44.5 0.7 %slice.6 = bf16[8,576]{1,0:T(8,128)(2,1)S(1)} slice(bf16[24,576]{1,0:T(8,128)(2,1)} %shard_map.113), slice={[0:8], [0:576]} | slice | bytes 18432 | tf_op jit(solution)/shard_map/slice | solution.py:579
  45.2 0.7 %slice.7 = bf16[16,576]{1,0:T(8,128)(2,1)S(1)} slice(bf16[24,576]{1,0:T(8,128)(2,1)} %shard_map.113), slice={[8:24], [0:576]} | slice | bytes 36864 | tf_op jit(solution)/shard_map/slice | solution.py:580
  45.9 0.6 %reshape.11 = bf16[4,4,576]{2,1,0:T(4,128)(2,1)} reshape(bf16[16,576]{1,0:T(8,128)(2,1)S(1)} %slice.7) | data formatting | bytes 36864 | tf_op jit(solution)/shard_map/reshape | solution.py:580
  46.5 0.6 %reshape.10 = bf16[2,4,576]{2,1,0:T(4,128)(2,1)} reshape(bf16[8,576]{1,0:T(8,128)(2,1)S(1)} %slice.6) | data formatting | bytes 18432 | tf_op jit(solution)/shard_map/reshape | solution.py:579

commit v16 on v14

--- a/solution.py
+++ b/solution.py
@@ -227,6 +227,12 @@
             f_ref[0, r], f_ref[1, r],
         ).astype(att_ref.dtype)
 
+    def project(lo, hi):
+        term = jnp.dot(att_ref[lo:hi], w_ref[...], preferred_element_type=jnp.float32)
+        cols = w_ref.shape[1] // parts
+        for q in range(parts):
+            blk[q, lo:hi] = term[:, q * cols : (q + 1) * cols]
+
     partners = []
     for k in range(rounds):
         step = 1 << k
@@ -269,6 +275,8 @@
         copy.start()
         if k < count:
             short_step(k)
+        if k == count:
+            project(0, count * tokens)
         copy.wait()
         mine = source[...]
         theirs = recv[k]
@@ -286,10 +294,9 @@
             state[k + 1] = merged
     for r in range(rounds, count):
         short_step(r)
-    term = jnp.dot(att_ref[...], w_ref[...], preferred_element_type=jnp.float32)
-    cols = w_ref.shape[1] // parts
-    for q in range(parts):
-        blk[q] = term[:, q * cols : (q + 1) * cols]
+    if count >= rounds:
+        project(0, count * tokens)
+    project(count * tokens, att_ref.shape[0])
     own = pltpu.make_async_copy(blk.at[column], tp_recv.at[column], tp_local)
     own.start()
     sends = []

time: 47.3 us -> 47.3 us (level)
  no operation moved by 1% of the time
where the time goes in v16:
time: 47.3 us; the launch traced here: 46.5 us
  Pallas kernels  43.8 us (93%)
  local copies, waits for them, and re-layouts  1.24 us (3%)
  other arithmetic  0.83 us (2%)
  between operations  0.64 us (1%)
    pallas_call x1, Pallas kernels, seq_allreduce(): pl.pallas_call(functools.partial(butterfly_kernel, rounds, parts), out_sh...  43.8 us

profile of v16, /device:TPU:4, one launch (start us, length us, event | category | flops | bytes accessed | tf_op | source)
XLA Modules:
  0.0 46.5 jit_solution(6276423511796586315)
XLA Ops:
  0.6 43.8 %shard_map.113 = f32[24,576]{1,0:T(8,128)} custom-call(s32[2]{0:T(128)} %len_ref.1, s32[4]{0:T(128)} %llen_ref.1, s32[2,4]{1,0:T(2,128)} %bitcast.5, bf16[2,4,576]{2,1,0:T(4,128)(2,1)} %q_ref.1, bf16[2,2,4,576]{3,2,1,0:T(4,128)(2,1)} %f_ref.1, bf16[2,2,576,1024]{3,2,1,0:T(8,128)(2,1)} %bitcast.3, bf16[4,4,576]{2,1,0:T(4,128)(2,1)} %ql_ref.1, ...), custom_call_target="tpu_custom_call" | custom-call | flops 1358954496 | bytes 7077888 | tf_op jit(solution)/shard_map/pallas_call | solution.py:349
  44.4 0.8 %convert_element_type.3 = bf16[24,576]{1,0:T(8,128)(2,1)S(1)} convert(f32[24,576]{1,0:T(8,128)} %shard_map.113) | non-fusion elementwise | flops 13824 | bytes 82944 | tf_op jit(solution)/shard_map/convert_element_type | solution.py:585
  45.3 0.6 %reshape.11 = bf16[4,4,576]{2,1,0:T(4,128)(2,1)} reshape(bf16[16,576]{1,0:T(8,128)(2,1)S(1)} %slice.9) | data formatting | bytes 36864 | tf_op jit(solution)/shard_map/reshape | solution.py:587
  45.9 0.6 %reshape.10 = bf16[2,4,576]{2,1,0:T(4,128)(2,1)} reshape(bf16[8,576]{1,0:T(8,128)(2,1)S(1)} %slice.8) | data formatting | bytes 18432 | tf_op jit(solution)/shard_map/reshape | solution.py:586
  (2 shorter events, 0.0 us)
